TPU v7x, 512 devices: a whole 4x4x16 slice. The times are simulated.
512 devices in a mesh: section: 2 (over z_hi), ctx: 32 (over z_lo, y), chan: 8 (over x, core).
Axes of the slice: x: 4, y: 4, z: 16 (z_hi: 2, z_lo: 8; z = z_hi * 8 + z_lo), core: 2. Of those that a mesh axis runs over, the one named last changes fastest.
Arguments:
- queries: bfloat16 [2, 8192, 8192], P('section', 'ctx', 'chan'), may hold values from -6 to 6
- keys: bfloat16 [2, 8192, 8192], P('section', 'ctx', 'chan'), may hold values from -6 to 6
- values: bfloat16 [8192, 8192], P('ctx', 'chan'), may hold values from -6 to 6
- cotangent: bfloat16 [8192, 8192], P('ctx', 'chan'), may hold values from -6 to 6
- short_filter: float32 [2, 3, 3, 8192], P('section', None, None, 'chan'), may hold values from -4 to 4
- mix_filter: bfloat16 [2, 128, 8192], P('section', None, 'chan'), may hold values from -0.5 to 0.5
- skip: float32 [2, 8192], P('section', 'chan'), may hold values from -5 to 5
Outputs:
- outputs: bfloat16 [2, 8192, 8192], P('section', 'ctx', 'chan')
- grad_q: bfloat16 [2, 8192, 8192], P('section', 'ctx', 'chan')
- grad_k: bfloat16 [2, 8192, 8192], P('section', 'ctx', 'chan')
- grad_input: bfloat16 [2, 8192, 8192], P('section', 'ctx', 'chan')
- grad_filter: float32 [2, 128, 8192], P('section', 'ctx', 'chan')
All inputs are finite; a program needn't handle non-finite values.
Results may differ from a plain program's by a relative error of at most 0.015.
Values may be sent and summed in bfloat16 or wider, within the bound.
A program may use at most 64 MiB of HBM per device.

v0:
```python
import jax
import jax.numpy as jnp
from jax import lax
from jax.sharding import PartitionSpec as P


def shifted(value, axis, by):
    peers = lax.axis_size(axis)
    pairs = [(i, i + by) for i in range(peers) if 0 <= i + by < peers]
    return lax.ppermute(value, axis, pairs)


def depthwise(source, kernel):
    result = lax.conv_general_dilated(
        source[None],
        kernel[:, None, :],
        (1,),
        "VALID",
        dimension_numbers=("NWC", "WIO", "NWC"),
        feature_group_count=source.shape[1],
        preferred_element_type=jnp.float32,
    )
    return result[0]


def short_conv(padded, weights, rows_here):
    widened = padded.astype(jnp.float32)
    return (
        weights[0] * widened[2 : 2 + rows_here]
        + weights[1] * widened[1 : 1 + rows_here]
        + weights[2] * widened[0:rows_here]
    )


def short_back(padded, weights, rows_here):
    widened = padded.astype(jnp.float32)
    return (
        weights[0] * widened[0:rows_here]
        + weights[1] * widened[1 : 1 + rows_here]
        + weights[2] * widened[2 : 2 + rows_here]
    )


def forward(query_rows, key_rows, value_rows, short_taps, mix_taps, skip_row):
    extent = mix_taps.shape[0]
    rows_here = query_rows.shape[0]
    rim_q, rim_k, rim_v = shifted(
        (query_rows[-2:], key_rows[-(extent + 1) :], value_rows[-(extent + 1) :]), "ctx", 1
    )
    q_ext = jnp.concatenate([rim_q, query_rows], axis=0)
    k_big = jnp.concatenate([rim_k, key_rows], axis=0)
    v_big = jnp.concatenate([rim_v, value_rows], axis=0)
    k_big_short = short_conv(k_big, short_taps[1], rows_here + extent - 1)
    v_big_short = short_conv(v_big, short_taps[2], rows_here + extent - 1)
    product_ext = lax.optimization_barrier((k_big_short * v_big_short).astype(jnp.bfloat16))
    k_short = k_big_short[extent - 1 :]
    v_short = v_big_short[extent - 1 :]
    k_ext = k_big[extent - 1 :]
    v_ext = v_big[extent - 1 :]
    q_short = short_conv(q_ext, short_taps[0], rows_here)
    product_here = product_ext[extent - 1 :]
    mixed = depthwise(product_ext, mix_taps[::-1]) + skip_row * product_here.astype(jnp.float32)
    output = (q_short * mixed).astype(jnp.bfloat16)
    return (output, (q_short, mixed, product_ext, k_short, v_short, k_ext, v_ext))


def backward(grad_out, saved, short_taps, mix_taps, skip_row):
    q_short, mixed, product_ext, k_short, v_short, k_ext, v_ext = saved
    extent = mix_taps.shape[0]
    rows_here = q_short.shape[0]
    grad_wide = grad_out.astype(jnp.float32)
    grad_mix = lax.optimization_barrier((grad_wide * q_short).astype(jnp.bfloat16))
    grad_gate = (grad_wide * mixed).astype(jnp.bfloat16)
    rim_mix, rim_gate, rim_k, rim_v = shifted(
        (grad_mix[: extent + 1], grad_gate[:2], k_ext[2:4], v_ext[2:4]), "ctx", -1
    )
    mix_big = jnp.concatenate([grad_mix, rim_mix], axis=0)
    grad_product = depthwise(mix_big, mix_taps) + skip_row * mix_big[: rows_here + 2].astype(
        jnp.float32
    )
    k_next = short_conv(jnp.concatenate([k_ext[-2:], rim_k], axis=0), short_taps[1], 2)
    v_next = short_conv(jnp.concatenate([v_ext[-2:], rim_v], axis=0), short_taps[2], 2)
    kgrad_ext = (grad_product * jnp.concatenate([v_short, v_next], axis=0)).astype(jnp.bfloat16)
    vgrad_ext = (grad_product * jnp.concatenate([k_short, k_next], axis=0)).astype(jnp.bfloat16)
    gate_ext = jnp.concatenate([grad_gate, rim_gate], axis=0)
    grad_query = short_back(gate_ext, short_taps[0], rows_here).astype(jnp.bfloat16)
    grad_key = short_back(kgrad_ext, short_taps[1], rows_here).astype(jnp.bfloat16)
    grad_value = short_back(vgrad_ext, short_taps[2], rows_here).astype(jnp.bfloat16)
    taps_part = depthwise(product_ext, grad_mix)[::-1]
    return (grad_query, grad_key, grad_value, taps_part)


def body(queries, keys, values, cotangent, short_filter, mix_filter, skip):
    section_index = lax.axis_index("section")
    leading = section_index == 0
    short_taps = short_filter[0]
    mix_taps = mix_filter[0]
    skip_row = skip[0]
    first_out, first_saved = forward(queries[0], keys[0], values, short_taps, mix_taps, skip_row)
    handed = shifted(first_out, "section", 1)
    second_out, second_saved = forward(queries[0], keys[0], handed, short_taps, mix_taps, skip_row)
    later = backward(cotangent, second_saved, short_taps, mix_taps, skip_row)
    returned = shifted(later[2], "section", -1)
    earlier = backward(returned, first_saved, short_taps, mix_taps, skip_row)

    def select(upper, lower):
        return jnp.where(leading, upper, lower)

    tap_sum = lax.psum_scatter(select(earlier[3], later[3]), "ctx", scatter_dimension=0, tiled=True)
    outputs = select(first_out, second_out)[None]
    grad_q = select(earlier[0], later[0])[None]
    grad_k = select(earlier[1], later[1])[None]
    grad_input = select(earlier[2], later[2])[None]
    return (outputs, grad_q, grad_k, grad_input, tap_sum[None])


def solution(mesh):
    return jax.shard_map(
        body,
        mesh=mesh,
        in_specs=(
            P("section", "ctx", "chan"),
            P("section", "ctx", "chan"),
            P("ctx", "chan"),
            P("ctx", "chan"),
            P("section", None, None, "chan"),
            P("section", None, "chan"),
            P("section", "chan"),
        ),
        out_specs=(
            P("section", "ctx", "chan"),
            P("section", "ctx", "chan"),
            P("section", "ctx", "chan"),
            P("section", "ctx", "chan"),
            P("section", "ctx", "chan"),
        ),
        check_vma=False,
    )
```

profile of v0, /device:TPU:6, one launch (start us, length us, event | category | flops | bytes accessed | tf_op | source)
XLA Modules:
  0.0 703.0 jit_solution(5323615608486610752)
XLA Ops:
  7.2 1.1 slice_bitcast_fusion
  8.4 3.5 collective-permute-start.1
  11.9 1.7 slice.342
  13.6 3.5 collective-permute-start.2
  17.1 0.7 slice_bitcast_fusion.3
  17.8 3.2 collective-permute-start
  21.0 1.3 collective-permute-start.11
  22.4 1.3 collective-permute-start.6
  23.7 0.8 fusion.78
  24.6 4.4 rev.10
  29.0 1.3 dynamic-slice
  31.6 1.3 collective-permute-start.5
  33.2 1.0 multiply_convert_fusion.1
  34.3 14.2 %fusion.16 = f32[1,256,1024]{2,0,1:T(1,128)S(1)} fusion(bf16[1,383,1024]{2,1,0:T(8,128)(2,1)S(1)} %bitcast.88, bf16[128,1,1024]{2,0,1:T(8,128)(2,1)S(1)} %bitcast.97), kind=kOutput, calls=%fused_computation.31 | convolution fusion | flops 67108864 | bytes 2095104 | tf_op jit(solution)/shard_map/conv_general_dilated | solution.py:14
  48.9 0.5 copy-done.11
  49.4 15.7 %collective-permute-start.3 = (bf16[256,1024]{1,0:T(8,128)(2,1)S(1)}, bf16[256,1024]{1,0:T(8,128)(2,1)S(1)}, u32[]{:S(2)}, u32[]{:S(2)}) collective-permute-start(bf16[256,1024]{1,0:T(8,128)(2,1)S(1)} %multiply_convert_fusion.5), channel_id=1, source_target_pairs={{0,256},{1,257},{2,258},{3,259},{4,260},{5,261},{6,262},{7,263},{8... | collective-permute-start | bytes 1572872 | tf_op jit(solution)/shard_map/ppermute | solution.py:10
  65.4 1.2 slice.434
  66.7 8.8 %collective-permute-done.3 = bf16[256,1024]{1,0:T(8,128)(2,1)S(1)} collective-permute-done((bf16[256,1024]{1,0:T(8,128)(2,1)S(1)}, bf16[256,1024]{1,0:T(8,128)(2,1)S(1)}, u32[]{:S(2)}, u32[]{:S(2)}) %collective-permute-start.3) | collective-permute-done | bytes 524320 | tf_op jit(solution)/shard_map/ppermute | solution.py:10
  75.5 1.3 collective-permute-start.12
  76.8 14.5 %fusion.2 = f32[1,258,1024]{2,0,1:T(1,128)S(1)} fusion(bf16[1,385,1024]{2,1,0:T(8,128)(2,1)S(1)} %fusion.47, bf16[128,1,1024]{2,0,1:T(8,128)(2,1)S(1)} %bitcast.95), kind=kOutput, calls=%fused_computation.2 | convolution fusion | flops 67633152 | bytes 2107392 | tf_op jit(solution)/shard_map/conv_general_dilated | solution.py:14
  91.4 6.2 collective-permute-start.4
  97.6 4.0 collective-permute-done.4
  101.8 0.6 multiply_convert_fusion
  102.5 0.6 fusion.52
  103.0 1.1 fusion.40
  104.2 1.5 collective-permute-start.7
  105.6 13.9 %fusion.10 = f32[1,128,1024]{2,0,1:T(1,128)S(1)} fusion(bf16[1,383,1024]{2,1,0:T(8,128)(2,1)S(1)} %bitcast.86, bf16[256,1,1024]{2,0,1:T(8,128)(2,1)S(1)} %bitcast.84), kind=kOutput, calls=%fused_computation.25 | convolution fusion | flops 67108864 | bytes 1832960 | tf_op jit(solution)/shard_map/conv_general_dilated | solution.py:14
  119.5 14.8 %fusion.12 = f32[1,256,1024]{2,0,1:T(1,128)} fusion(bf16[1,383,1024]{2,1,0:T(8,128)(2,1)S(1)} %bitcast.87, bf16[128,1,1024]{2,0,1:T(8,128)(2,1)S(1)} %bitcast.98), kind=kOutput, calls=%fused_computation.27 | convolution fusion | flops 67108864 | bytes 2095104 | tf_op jit(solution)/shard_map/conv_general_dilated | solution.py:14
  134.3 0.9 copy.100
  135.2 4.7 rev.12
  140.0 3.0 fusion.55
  143.0 3.1 fusion.23
  146.1 13.9 %fusion.14 = f32[1,128,1024]{2,0,1:T(1,128)S(1)} fusion(bf16[1,383,1024]{2,1,0:T(8,128)(2,1)S(1)} %bitcast.89, bf16[256,1,1024]{2,0,1:T(8,128)(2,1)S(1)} %bitcast.85), kind=kOutput, calls=%fused_computation.29 | convolution fusion | flops 67108864 | bytes 1832960 | tf_op jit(solution)/shard_map/conv_general_dilated | solution.py:14
  160.1 2.6 rev.11
  162.8 0.7 slice.423
  163.5 1.4 collective-permute-start.8
  164.9 1.9 broadcast_select_fusion
  166.9 1.3 collective-permute-start.10
  168.2 1.3 collective-permute-start.9
  169.6 1.1 maximum_convert_fusion.4
  170.8 5.7 collective-permute-done.9
  176.6 1.5 fusion.61
  178.1 0.9 copy-done.20
  179.0 14.5 %fusion = f32[1,258,1024]{2,0,1:T(1,128)S(1)} fusion(bf16[1,385,1024]{2,1,0:T(8,128)(2,1)S(1)} %fusion.46, bf16[128,1,1024]{2,0,1:T(8,128)(2,1)S(1)} %bitcast.96), kind=kOutput, calls=%fused_computation | convolution fusion | flops 67633152 | bytes 2107392 | tf_op jit(solution)/shard_map/conv_general_dilated | solution.py:14
  193.6 0.6 fusion.51
  194.2 2.3 fusion.59
  196.5 498.3 %all-reduce.3.cloned.1.call-done = f32[128,1024]{1,0:T(8,128)} async-done(((f32[128,1024]{1,0:T(8,128)}), f32[128,1024]{1,0:T(8,128)}) %all-reduce.3.cloned.1.call-update) | async-done | bytes 524304
  694.8 1.4 dynamic-slice_bitcast_fusion
  (104 shorter events, 2.7 us)
Async XLA Ops:
  7.2 15.2 %copy-start.17 = (bf16[1,256,1024]{2,1,0:T(8,128)(2,1)S(1)}, bf16[1,256,1024]{2,1,0:T(8,128)(2,1)}, u32[]{:S(2)}) copy-start(bf16[1,256,1024]{2,1,0:T(8,128)(2,1)} %param.8) | copy-start | bytes 1572868
  7.2 13.8 %copy-start.16 = (bf16[256,1024]{1,0:T(8,128)(2,1)S(1)}, bf16[256,1024]{1,0:T(8,128)(2,1)}, u32[]{:S(2)}) copy-start(bf16[256,1024]{1,0:T(8,128)(2,1)} %param.9) | copy-start | bytes 1572868
  7.2 23.7 %copy-start.18 = (bf16[1,256,1024]{2,1,0:T(8,128)(2,1)S(1)}, bf16[1,256,1024]{2,1,0:T(8,128)(2,1)}, u32[]{:S(2)}) copy-start(bf16[1,256,1024]{2,1,0:T(8,128)(2,1)} %param.7) | copy-start | bytes 1572868
  7.2 687.6 %all-reduce.3.cloned.1.call-start = ((), (), s32[]{:S(2)}) async-start(), calls=%async_computation | async-start | bytes 1048576
  8.4 24.7 %collective-permute-start.1 = (bf16[129,1024]{1,0:T(8,128)(2,1)S(1)}, bf16[129,1024]{1,0:T(8,128)(2,1)S(1)}, u32[]{:S(2)}, u32[]{:S(2)}) collective-permute-start(bf16[129,1024]{1,0:T(8,128)(2,1)S(1)} %slice_bitcast_fusion), channel_id=1, source_target_pairs={{0,8},{8,16},{16,24},{24,32},{32,40},{40,48},{48,56},{56,64},{64,7... | collective-permute-start | bytes 792584 | tf_op jit(solution)/shard_map/ppermute | solution.py:10
  13.6 19.2 %collective-permute-start.2 = (bf16[129,1024]{1,0:T(8,128)(2,1)}, bf16[129,1024]{1,0:T(8,128)(2,1)S(1)}, u32[]{:S(2)}, u32[]{:S(2)}) collective-permute-start(bf16[129,1024]{1,0:T(8,128)(2,1)} %slice.342), channel_id=1, source_target_pairs={{0,8},{8,16},{16,24},{24,32},{32,40},{40,48},{48,56},{56,64},{64,7... | collective-permute-start | bytes 792584 | tf_op jit(solution)/shard_map/ppermute | solution.py:10
  17.8 13.1 %collective-permute-start = (bf16[2,1024]{1,0:T(2,128)(2,1)S(1)}, bf16[2,1024]{1,0:T(2,128)(2,1)S(1)}, u32[]{:S(2)}, u32[]{:S(2)}) collective-permute-start(bf16[2,1024]{1,0:T(2,128)(2,1)S(1)} %slice_bitcast_fusion.3), channel_id=1, source_target_pairs={{0,8},{8,16},{16,24},{24,32},{32,40},{40,48},{48,56},{56,64},{64,7... | collective-permute-start | bytes 12296 | tf_op jit(solution)/shard_map/ppermute | solution.py:10
  21.0 44.2 %collective-permute-start.11 = (bf16[2,1024]{1,0:T(2,128)(2,1)S(1)}, bf16[2,1024]{1,0:T(2,128)(2,1)S(1)}, u32[]{:S(2)}, u32[]{:S(2)}) collective-permute-start(bf16[2,1024]{1,0:T(2,128)(2,1)S(1)} %get-tuple-element.19), channel_id=1, source_target_pairs={{8,0},{16,8},{24,16},{32,24},{40,32},{48,40},{56,48},{64,56},{72,6... | collective-permute-start | bytes 12296 | tf_op jit(solution)/shard_map/ppermute | solution.py:10
  22.4 42.9 %collective-permute-start.6 = (bf16[2,1024]{1,0:T(2,128)(2,1)S(1)}, bf16[2,1024]{1,0:T(2,128)(2,1)S(1)}, u32[]{:S(2)}, u32[]{:S(2)}) collective-permute-start(bf16[2,1024]{1,0:T(2,128)(2,1)S(1)} %get-tuple-element.23), channel_id=1, source_target_pairs={{8,0},{16,8},{24,16},{32,24},{40,32},{48,40},{56,48},{64,56},{72,6... | collective-permute-start | bytes 12296 | tf_op jit(solution)/shard_map/ppermute | solution.py:10
  24.5 6.6 copy-start.29
  24.5 6.6 copy-start.31
  24.5 6.6 copy-start.33
  24.5 40.8 %copy-start.23 = (f32[1,1,1,1024]{3,0,2,1:T(1,128)}, f32[1,1,1,1024]{3,0,2,1:T(1,128)S(1)}, u32[]{:S(2)}) copy-start(f32[1,1,1,1024]{3,0,2,1:T(1,128)S(1)} %get-tuple-element.24) | copy-start | bytes 12292
  24.5 40.8 %copy-start.25 = (f32[1,1,1,1024]{3,0,2,1:T(1,128)}, f32[1,1,1,1024]{3,0,2,1:T(1,128)S(1)}, u32[]{:S(2)}) copy-start(f32[1,1,1,1024]{3,0,2,1:T(1,128)S(1)} %get-tuple-element.26) | copy-start | bytes 12292
  24.5 40.8 %copy-start.27 = (f32[1,1,1,1024]{3,0,2,1:T(1,128)}, f32[1,1,1,1024]{3,0,2,1:T(1,128)S(1)}, u32[]{:S(2)}) copy-start(f32[1,1,1,1024]{3,0,2,1:T(1,128)S(1)} %get-tuple-element.27) | copy-start | bytes 12292
  24.5 6.6 copy-start.14
  31.6 35.1 %collective-permute-start.5 = (bf16[129,1024]{1,0:T(8,128)(2,1)S(1)}, bf16[129,1024]{1,0:T(8,128)(2,1)S(1)}, u32[]{:S(2)}, u32[]{:S(2)}) collective-permute-start(bf16[129,1024]{1,0:T(8,128)(2,1)S(1)} %slice.413), channel_id=1, source_target_pairs={{8,0},{16,8},{24,16},{32,24},{40,32},{48,40},{56,48},{64,56},{72,6... | collective-permute-start | bytes 792584 | tf_op jit(solution)/shard_map/ppermute | solution.py:10
  33.2 1.0 copy-start.21
  34.3 14.2 %copy-start.7 = (bf16[383,1024]{1,0:T(8,128)(2,1)}, bf16[383,1024]{1,0:T(8,128)(2,1)S(1)}, u32[]{:S(2)}) copy-start(bf16[383,1024]{1,0:T(8,128)(2,1)S(1)} %get-tuple-element.9) | copy-start | bytes 2353156
  34.3 14.2 %copy-start.22 = (f32[1,1024]{1,0:T(1,128)S(1)}, f32[1,1024]{1,0:T(1,128)}, u32[]{:S(2)}) copy-start(f32[1,1024]{1,0:T(1,128)} %param.13) | copy-start | bytes 12292
  48.5 1.0 copy-start.11
  49.4 16.0 %copy-start.15 = (bf16[256,1024]{1,0:T(8,128)(2,1)}, bf16[256,1024]{1,0:T(8,128)(2,1)S(1)}, u32[]{:S(2)}) copy-start(bf16[256,1024]{1,0:T(8,128)(2,1)S(1)} %multiply_convert_fusion.5) | copy-start | bytes 1572868
  49.4 26.0 %collective-permute-start.3 = (bf16[256,1024]{1,0:T(8,128)(2,1)S(1)}, bf16[256,1024]{1,0:T(8,128)(2,1)S(1)}, u32[]{:S(2)}, u32[]{:S(2)}) collective-permute-start(bf16[256,1024]{1,0:T(8,128)(2,1)S(1)} %multiply_convert_fusion.5), channel_id=1, source_target_pairs={{0,256},{1,257},{2,258},{3,259},{4,260},{5,261},{6,262},{7,263},{8... | collective-permute-start | bytes 1572872 | tf_op jit(solution)/shard_map/ppermute | solution.py:10
  65.4 37.0 %copy-start = (f32[256,1024]{1,0:T(8,128)}, f32[256,1024]{1,0:T(8,128)S(1)}, u32[]{:S(2)}) copy-start(f32[256,1024]{1,0:T(8,128)S(1)} %slice.416) | copy-start | bytes 3145732
  66.6 10.2 %copy-start.19 = (bf16[1,128,1024]{2,1,0:T(8,128)(2,1)S(1)}, bf16[1,128,1024]{2,1,0:T(8,128)(2,1)}, u32[]{:S(2)}) copy-start(bf16[1,128,1024]{2,1,0:T(8,128)(2,1)} %param.12) | copy-start | bytes 786436
  75.5 22.1 %collective-permute-start.12 = (bf16[2,1024]{1,0:T(2,128)(2,1)S(1)}, bf16[2,1024]{1,0:T(2,128)(2,1)S(1)}, u32[]{:S(2)}, u32[]{:S(2)}) collective-permute-start(bf16[2,1024]{1,0:T(2,128)(2,1)S(1)} %get-tuple-element.21), channel_id=1, source_target_pairs={{8,0},{16,8},{24,16},{32,24},{40,32},{48,40},{56,48},{64,56},{72,6... | collective-permute-start | bytes 12296 | tf_op jit(solution)/shard_map/ppermute | solution.py:10
  91.4 10.2 %collective-permute-start.4 = (bf16[129,1024]{1,0:T(8,128)(2,1)S(1)}, bf16[129,1024]{1,0:T(8,128)(2,1)S(1)}, u32[]{:S(2)}, u32[]{:S(2)}) collective-permute-start(bf16[129,1024]{1,0:T(8,128)(2,1)S(1)} %slice.408), channel_id=1, source_target_pairs={{0,8},{8,16},{16,24},{24,32},{32,40},{40,48},{48,56},{56,64},{64,7... | collective-permute-start | bytes 792584 | tf_op jit(solution)/shard_map/ppermute | solution.py:10
  102.3 17.2 %copy-start.5 = (bf16[383,1024]{1,0:T(8,128)(2,1)}, bf16[383,1024]{1,0:T(8,128)(2,1)S(1)}, u32[]{:S(2)}) copy-start(bf16[383,1024]{1,0:T(8,128)(2,1)S(1)} %get-tuple-element.7) | copy-start | bytes 2353156
  104.2 38.8 %collective-permute-start.7 = (bf16[256,1024]{1,0:T(8,128)(2,1)}, bf16[256,1024]{1,0:T(8,128)(2,1)}, u32[]{:S(2)}, u32[]{:S(2)}) collective-permute-start(bf16[256,1024]{1,0:T(8,128)(2,1)} %fusion.40), channel_id=1, source_target_pairs={{256,0},{257,1},{258,2},{259,3},{260,4},{261,5},{262,6},{263,7},{2... | collective-permute-start | bytes 1572872 | tf_op jit(solution)/shard_map/ppermute | solution.py:10
  140.0 3.0 copy-start.6
  140.0 3.0 copy-start.8
  140.0 3.0 copy-start.9
  140.0 3.0 copy-start.12
  146.1 13.9 %copy-start.2 = (bf16[256,1024]{1,0:T(8,128)(2,1)}, bf16[256,1024]{1,0:T(8,128)(2,1)S(1)}, u32[]{:S(2)}) copy-start(bf16[256,1024]{1,0:T(8,128)(2,1)S(1)} %get-tuple-element.16) | copy-start | bytes 1572868
  160.1 6.7 copy-start.3
  163.5 4.7 copy-start.13
  163.5 6.1 collective-permute-start.8
  166.9 11.2 %collective-permute-start.10 = (bf16[129,1024]{1,0:T(8,128)(2,1)S(1)}, bf16[129,1024]{1,0:T(8,128)(2,1)S(1)}, u32[]{:S(2)}, u32[]{:S(2)}) collective-permute-start(bf16[129,1024]{1,0:T(8,128)(2,1)S(1)} %slice.431), channel_id=1, source_target_pairs={{8,0},{16,8},{24,16},{32,24},{40,32},{48,40},{56,48},{64,56},{72,6... | collective-permute-start | bytes 792584 | tf_op jit(solution)/shard_map/ppermute | solution.py:10
  168.2 8.3 %collective-permute-start.9 = (bf16[2,1024]{1,0:T(2,128)(2,1)S(1)}, bf16[2,1024]{1,0:T(2,128)(2,1)S(1)}, u32[]{:S(2)}, u32[]{:S(2)}) collective-permute-start(bf16[2,1024]{1,0:T(2,128)(2,1)S(1)} %slice.427), channel_id=1, source_target_pairs={{8,0},{16,8},{24,16},{32,24},{40,32},{48,40},{56,48},{64,56},{72,6... | collective-permute-start | bytes 12296 | tf_op jit(solution)/shard_map/ppermute | solution.py:10
  170.8 5.8 copy-start.30
  170.8 5.8 copy-start.32
  170.8 5.8 copy-start.34
  178.1 0.9 copy-start.20
  179.0 14.5 %copy-start.1 = (f32[256,1024]{1,0:T(8,128)S(1)}, f32[256,1024]{1,0:T(8,128)}, u32[]{:S(2)}) copy-start(f32[256,1024]{1,0:T(8,128)} %copy-done) | copy-start | bytes 3145732
  179.0 14.5 %copy-start.4 = (bf16[256,1024]{1,0:T(8,128)(2,1)S(1)}, bf16[256,1024]{1,0:T(8,128)(2,1)}, u32[]{:S(2)}) copy-start(bf16[256,1024]{1,0:T(8,128)(2,1)} %copy-done.2) | copy-start | bytes 1572868
  179.0 14.5 %copy-start.10 = (f32[256,1024]{1,0:T(8,128)S(1)}, f32[256,1024]{1,0:T(8,128)}, u32[]{:S(2)}) copy-start(f32[256,1024]{1,0:T(8,128)} %slice.434) | copy-start | bytes 3145732
  193.5 0.7 copy-start.24
  193.5 0.7 copy-start.26
  (1 other events, 0.7 us)
Sparse Core Ops, SparseCore 0:
  167.0 527.7 all-reduce.2
where the time goes:
time: 705 us; the launch traced here: 703 us
  waiting for transfers between devices  517 us (73%)
  matrix products  85.7 us (12%)
  starting transfers between devices  42.7 us (6%)
  local copies, waits for them, and re-layouts  23.7 us (3%)
  other arithmetic  18.6 us (3%)
  between operations  15.5 us (2%)
    unnamed x2, waiting for transfers between devices  498 us
    conv_general_dilated x6, matrix products, depthwise(): lax.conv_general_dilated(source[None], kernel[:, None, :], (1,), 'VALID',...  85.7 us
    ppermute x13, starting transfers between devices, shifted(): return lax.ppermute(value, axis, pairs)  42.7 us
    ppermute x13, waiting for transfers between devices, shifted(): return lax.ppermute(value, axis, pairs)  18.5 us
  transfers between devices with their start and end apart: 14, of which 5 were waited for; matrix products, arithmetic and copies ran while one was open for 14% of the time, Pallas kernels for 0%

commit v1 on v0

--- a/solution.py
+++ b/solution.py
@@ -8,6 +8,27 @@
     peers = lax.axis_size(axis)
     pairs = [(i, i + by) for i in range(peers) if 0 <= i + by < peers]
     return lax.ppermute(value, axis, pairs)
+
+
+def halving_scatter(part, axis):
+    peers = lax.axis_size(axis)
+    steps = peers.bit_length() - 1
+    if peers != 1 << steps or part.shape[0] % peers:
+        return lax.psum_scatter(part, axis, scatter_dimension=0, tiled=True)
+    me = lax.axis_index(axis)
+    rows = part.shape[0] // peers
+    held = part.reshape((2,) * steps + (rows,) + part.shape[1:])
+    remaining = [steps - 1 - k for k in range(steps)]
+    order = sorted(range(steps), key=lambda b: (b % 2, b))
+    for bit in order:
+        at = remaining.index(bit)
+        mine = (me >> bit) & 1
+        keep = lax.dynamic_index_in_dim(held, mine, axis=at, keepdims=False)
+        give = lax.dynamic_index_in_dim(held, 1 - mine, axis=at, keepdims=False)
+        got = lax.ppermute(give, axis, [(i, i ^ (1 << bit)) for i in range(peers)])
+        held = keep + got
+        remaining.pop(at)
+    return held.reshape((rows,) + part.shape[1:])
 
 
 def depthwise(source, kernel):
@@ -106,7 +127,7 @@
     def select(upper, lower):
         return jnp.where(leading, upper, lower)
 
-    tap_sum = lax.psum_scatter(select(earlier[3], later[3]), "ctx", scatter_dimension=0, tiled=True)
+    tap_sum = halving_scatter(select(earlier[3], later[3]), "ctx")
     outputs = select(first_out, second_out)[None]
     grad_q = select(earlier[0], later[0])[None]
     grad_k = select(earlier[1], later[1])[None]

time: 705 us -> 295 us (0.42)
  the two profiles are of different devices: /device:TPU:6 before, /device:TPU:356 now
where the time goes in v1:
time: 295 us; the launch traced here: 294 us
  starting transfers between devices  101 us (34%)
  matrix products  85.7 us (29%)
  waiting for transfers between devices  63.3 us (21%)
  local copies, waits for them, and re-layouts  25.1 us (9%)
  other arithmetic  17 us (6%)
    conv_general_dilated x6, matrix products, depthwise(): lax.conv_general_dilated(source[None], kernel[:, None, :], (1,), 'VALID',...  85.7 us
    ppermute x5, starting transfers between devices, halving_scatter(): got = lax.ppermute(give, axis, [(i, i ^ 1 << bit) for i in range(peers)])  54.6 us
    ppermute x13, waiting for transfers between devices, shifted(): return lax.ppermute(value, axis, pairs)  53.3 us
    ppermute x13, starting transfers between devices, shifted(): return lax.ppermute(value, axis, pairs)  46.2 us
    ppermute x5, waiting for transfers between devices, halving_scatter(): got = lax.ppermute(give, axis, [(i, i ^ 1 << bit) for i in range(peers)])  10 us
    rev x2, local copies, waits for them, and re-layouts, backward(): taps_part = depthwise(product_ext, grad_mix)[::-1]  8.19 us
  transfers between devices with their start and end apart: 18, of which 6 were waited for; matrix products, arithmetic and copies ran while one was open for 33% of the time, Pallas kernels for 0%

profile of v1, /device:TPU:356, one launch (start us, length us, event | category | flops | bytes accessed | tf_op | source)
XLA Modules:
  0.0 293.6 jit_solution(10662954176624512934)
XLA Ops:
  0.7 1.1 slice_bitcast_fusion
  1.8 3.5 %collective-permute-start.1 = (bf16[129,1024]{1,0:T(8,128)(2,1)S(1)}, bf16[129,1024]{1,0:T(8,128)(2,1)S(1)}, u32[]{:S(2)}, u32[]{:S(2)}) collective-permute-start(bf16[129,1024]{1,0:T(8,128)(2,1)S(1)} %slice_bitcast_fusion), channel_id=1, source_target_pairs={{0,8},{8,16},{16,24},{24,32},{32,40},{40,48},{48,56},{56,64},{64,7... | collective-permute-start | bytes 792584 | tf_op jit(solution)/shard_map/ppermute | solution.py:10
  5.3 1.7 slice.342
  7.0 3.5 %collective-permute-start.2 = (bf16[129,1024]{1,0:T(8,128)(2,1)}, bf16[129,1024]{1,0:T(8,128)(2,1)S(1)}, u32[]{:S(2)}, u32[]{:S(2)}) collective-permute-start(bf16[129,1024]{1,0:T(8,128)(2,1)} %slice.342), channel_id=1, source_target_pairs={{0,8},{8,16},{16,24},{24,32},{32,40},{40,48},{48,56},{56,64},{64,7... | collective-permute-start | bytes 792584 | tf_op jit(solution)/shard_map/ppermute | solution.py:10
  11.2 3.2 %collective-permute-start = (bf16[2,1024]{1,0:T(2,128)(2,1)S(1)}, bf16[2,1024]{1,0:T(2,128)(2,1)S(1)}, u32[]{:S(2)}, u32[]{:S(2)}) collective-permute-start(bf16[2,1024]{1,0:T(2,128)(2,1)S(1)} %slice_bitcast_fusion.3), channel_id=1, source_target_pairs={{0,8},{8,16},{16,24},{24,32},{32,40},{40,48},{48,56},{56,64},{64,7... | collective-permute-start | bytes 12296 | tf_op jit(solution)/shard_map/ppermute | solution.py:10
  14.5 4.8 %collective-permute-start.11 = (bf16[2,1024]{1,0:T(2,128)(2,1)S(1)}, bf16[2,1024]{1,0:T(2,128)(2,1)S(1)}, u32[]{:S(2)}, u32[]{:S(2)}) collective-permute-start(bf16[2,1024]{1,0:T(2,128)(2,1)S(1)} %get-tuple-element.21), channel_id=1, source_target_pairs={{8,0},{16,8},{24,16},{32,24},{40,32},{48,40},{56,48},{64,56},{72,6... | collective-permute-start | bytes 12296 | tf_op jit(solution)/shard_map/ppermute | solution.py:10
  19.3 2.4 collective-permute-start.6
  21.6 0.8 fusion.79
  22.5 4.4 %rev.10 = bf16[128,1024]{1,0:T(8,128)(2,1)} reverse(bf16[128,1024]{1,0:T(8,128)(2,1)} %bitcast.116), dimensions={0} | reverse | bytes 524288 | tf_op jit(solution)/shard_map/rev | solution.py:83
  27.6 2.4 collective-permute-start.5
  30.3 1.0 multiply_convert_fusion.1
  31.4 14.2 %fusion.16 = f32[1,256,1024]{2,0,1:T(1,128)S(1)} fusion(bf16[1,383,1024]{2,1,0:T(8,128)(2,1)S(1)} %bitcast.110, bf16[128,1,1024]{2,0,1:T(8,128)(2,1)S(1)} %bitcast.119), kind=kOutput, calls=%fused_computation.31 | convolution fusion | flops 67108864 | bytes 2095104 | tf_op jit(solution)/shard_map/conv_general_dilated | solution.py:35
  46.5 1.3 collective-permute-start.3
  48.1 1.2 slice.434
  49.4 42.3 %collective-permute-done.3 = bf16[256,1024]{1,0:T(8,128)(2,1)S(1)} collective-permute-done((bf16[256,1024]{1,0:T(8,128)(2,1)S(1)}, bf16[256,1024]{1,0:T(8,128)(2,1)S(1)}, u32[]{:S(2)}, u32[]{:S(2)}) %collective-permute-start.3) | collective-permute-done | bytes 524320 | tf_op jit(solution)/shard_map/ppermute | solution.py:10
  91.7 1.9 collective-permute-start.12
  93.6 14.5 %fusion.2 = f32[1,258,1024]{2,0,1:T(1,128)S(1)} fusion(bf16[1,385,1024]{2,1,0:T(8,128)(2,1)S(1)} %fusion.47, bf16[128,1,1024]{2,0,1:T(8,128)(2,1)S(1)} %bitcast.117), kind=kOutput, calls=%fused_computation.2 | convolution fusion | flops 67633152 | bytes 2107392 | tf_op jit(solution)/shard_map/conv_general_dilated | solution.py:35
  108.2 3.9 %collective-permute-start.4 = (bf16[129,1024]{1,0:T(8,128)(2,1)S(1)}, bf16[129,1024]{1,0:T(8,128)(2,1)S(1)}, u32[]{:S(2)}, u32[]{:S(2)}) collective-permute-start(bf16[129,1024]{1,0:T(8,128)(2,1)S(1)} %slice.408), channel_id=1, source_target_pairs={{0,8},{8,16},{16,24},{24,32},{32,40},{40,48},{48,56},{56,64},{64,7... | collective-permute-start | bytes 792584 | tf_op jit(solution)/shard_map/ppermute | solution.py:10
  112.2 7.6 %collective-permute-done.4 = bf16[129,1024]{1,0:T(8,128)(2,1)S(1)} collective-permute-done((bf16[129,1024]{1,0:T(8,128)(2,1)S(1)}, bf16[129,1024]{1,0:T(8,128)(2,1)S(1)}, u32[]{:S(2)}, u32[]{:S(2)}) %collective-permute-start.4) | collective-permute-done | bytes 264224 | tf_op jit(solution)/shard_map/ppermute | solution.py:10
  121.2 1.1 fusion.40
  122.4 2.3 collective-permute-start.7
  124.6 13.9 %fusion.10 = f32[1,128,1024]{2,0,1:T(1,128)S(1)} fusion(bf16[1,383,1024]{2,1,0:T(8,128)(2,1)S(1)} %bitcast.108, bf16[256,1,1024]{2,0,1:T(8,128)(2,1)S(1)} %bitcast.107), kind=kOutput, calls=%fused_computation.25 | convolution fusion | flops 67108864 | bytes 1832960 | tf_op jit(solution)/shard_map/conv_general_dilated | solution.py:35
  138.5 14.8 %fusion.12 = f32[1,256,1024]{2,0,1:T(1,128)} fusion(bf16[1,383,1024]{2,1,0:T(8,128)(2,1)S(1)} %bitcast.109, bf16[128,1,1024]{2,0,1:T(8,128)(2,1)S(1)} %bitcast.120), kind=kOutput, calls=%fused_computation.27 | convolution fusion | flops 67108864 | bytes 2095104 | tf_op jit(solution)/shard_map/conv_general_dilated | solution.py:35
  153.3 0.9 copy.104
  154.2 4.8 %rev.12 = f32[128,1024]{1,0:T(8,128)} reverse(f32[128,1024]{1,0:T(8,128)} %bitcast.112), dimensions={0} | reverse | bytes 1048576 | tf_op jit(solution)/shard_map/rev | solution.py:110
  159.0 2.8 fusion.55
  161.8 3.1 %fusion.23 = (bf16[256,1024]{1,0:T(8,128)(2,1)S(1)}, bf16[256,1024]{1,0:T(8,128)(2,1)}, bf16[256,1024]{1,0:T(8,128)(2,1)}) fusion(f32[256,1024]{1,0:T(8,128)S(1)} %get-tuple-element.6, bf16[256,1024]{1,0:T(8,128)(2,1)} %collective-permute-done.7, bf16[383,1024]{1,0:T(8,128)(2,1)S(1)} %copy-done.8, f32[1024]{0:T(1024)S(1)} %bitcast.140, ...), kind=kLoop, calls=%fused_computation.45 | loop fusion | flops 3670016 | bytes 6819840 | tf_op jit(solution)/shard_map/convert_element_type | solution.py:93
  165.0 13.9 %fusion.14 = f32[1,128,1024]{2,0,1:T(1,128)S(1)} fusion(bf16[1,383,1024]{2,1,0:T(8,128)(2,1)S(1)} %bitcast.111, bf16[256,1,1024]{2,0,1:T(8,128)(2,1)S(1)} %bitcast.106), kind=kOutput, calls=%fused_computation.29 | convolution fusion | flops 67108864 | bytes 1832960 | tf_op jit(solution)/shard_map/conv_general_dilated | solution.py:35
  178.9 0.9 copy.105
  179.8 3.4 %rev.11 = f32[128,1024]{1,0:T(8,128)S(1)} reverse(f32[128,1024]{1,0:T(8,128)} %bitcast.113), dimensions={0} | reverse | bytes 1048576 | tf_op jit(solution)/shard_map/rev | solution.py:110
  183.2 0.9 broadcast_select_fusion
  184.1 2.0 reshape.41
  186.9 1.9 collective-permute-start.8
  188.8 1.1 constant_dynamic-slice_fusion.1
  190.0 3.9 %collective-permute-start.13 = (f32[2,2,2,2,4,1024]{5,4,3,1,0,2:T(4,128)S(1)}, f32[2,2,2,2,4,1024]{5,4,3,1,0,2:T(4,128)S(1)}, u32[]{:S(2)}, u32[]{:S(2)}) collective-permute-start(f32[2,2,2,2,4,1024]{5,4,3,1,0,2:T(4,128)S(1)} %bitcast.121), channel_id=1, source_target_pairs={{0,8},{8,0},{16,24},{24,16},{32,40},{40,32},{48,56},{56,48},{64,72... | collective-permute-start | bytes 786440 | tf_op jit(solution)/shard_map/ppermute | solution.py:28
  193.9 13.4 %collective-permute-start.10 = (bf16[129,1024]{1,0:T(8,128)(2,1)S(1)}, bf16[129,1024]{1,0:T(8,128)(2,1)S(1)}, u32[]{:S(2)}, u32[]{:S(2)}) collective-permute-start(bf16[129,1024]{1,0:T(8,128)(2,1)S(1)} %slice.431), channel_id=1, source_target_pairs={{8,0},{16,8},{24,16},{32,24},{40,32},{48,40},{56,48},{64,56},{72,6... | collective-permute-start | bytes 792584 | tf_op jit(solution)/shard_map/ppermute | solution.py:10
  207.4 1.9 collective-permute-start.9
  209.5 3.4 %collective-permute-done.9 = bf16[2,1024]{1,0:T(2,128)(2,1)S(1)} collective-permute-done((bf16[2,1024]{1,0:T(2,128)(2,1)S(1)}, bf16[2,1024]{1,0:T(2,128)(2,1)S(1)}, u32[]{:S(2)}, u32[]{:S(2)}) %collective-permute-start.9) | collective-permute-done | bytes 4128 | tf_op jit(solution)/shard_map/ppermute | solution.py:10
  213.0 1.5 fusion.61
  214.6 6.7 %collective-permute-start.14 = (f32[2,2,2,4,1024]{4,3,2,1,0:T(4,128)S(1)}, f32[2,2,2,4,1024]{4,3,2,1,0:T(4,128)S(1)}, u32[]{:S(2)}, u32[]{:S(2)}) collective-permute-start(f32[2,2,2,4,1024]{4,3,2,1,0:T(4,128)S(1)} %dynamic-slice_bitcast_fusion), channel_id=1, source_target_pairs={{0,32},{8,40},{16,48},{24,56},{32,0},{40,8},{48,16},{56,24},{64,96... | collective-permute-start | bytes 393224 | tf_op jit(solution)/shard_map/ppermute | solution.py:28
  221.4 2.9 collective-permute-done.14
  224.4 40.0 %collective-permute-start.15 = (f32[2,2,4,1024]{3,2,1,0:T(4,128)S(1)}, f32[2,2,4,1024]{3,2,1,0:T(4,128)S(1)}, u32[]{:S(2)}, u32[]{:S(2)}) collective-permute-start(f32[2,2,4,1024]{3,2,1,0:T(4,128)S(1)} %dynamic-slice_bitcast_fusion.1), channel_id=1, source_target_pairs={{0,128},{8,136},{16,144},{24,152},{32,160},{40,168},{48,176},{56,1... | collective-permute-start | bytes 196616 | tf_op jit(solution)/shard_map/ppermute | solution.py:28
  264.4 14.5 %fusion = f32[1,258,1024]{2,0,1:T(1,128)S(1)} fusion(bf16[1,385,1024]{2,1,0:T(8,128)(2,1)S(1)} %fusion.46, bf16[128,1,1024]{2,0,1:T(8,128)(2,1)S(1)} %bitcast.118), kind=kOutput, calls=%fused_computation | convolution fusion | flops 67633152 | bytes 2107392 | tf_op jit(solution)/shard_map/conv_general_dilated | solution.py:35
  279.0 1.9 collective-permute-start.16
  281.5 4.8 %collective-permute-done.16 = f32[2,4,1024]{2,1,0:T(4,128)S(1)} collective-permute-done((f32[2,4,1024]{2,1,0:T(4,128)S(1)}, f32[2,4,1024]{2,1,0:T(4,128)S(1)}, u32[]{:S(2)}, u32[]{:S(2)}) %collective-permute-start.16) | collective-permute-done | bytes 32800 | tf_op jit(solution)/shard_map/ppermute | solution.py:28
  286.3 1.9 collective-permute-start.17
  288.3 2.3 fusion.59
  290.6 2.4 collective-permute-done.17
  (123 shorter events, 7.0 us)
Async XLA Ops:
  0.6 18.6 %copy-start.19 = (bf16[1,256,1024]{2,1,0:T(8,128)(2,1)S(1)}, bf16[1,256,1024]{2,1,0:T(8,128)(2,1)}, u32[]{:S(2)}) copy-start(bf16[1,256,1024]{2,1,0:T(8,128)(2,1)} %param.8) | copy-start | bytes 1572868
  0.6 13.8 %copy-start.18 = (bf16[256,1024]{1,0:T(8,128)(2,1)S(1)}, bf16[256,1024]{1,0:T(8,128)(2,1)}, u32[]{:S(2)}) copy-start(bf16[256,1024]{1,0:T(8,128)(2,1)} %param.9) | copy-start | bytes 1572868
  0.7 26.3 %copy-start.20 = (bf16[1,256,1024]{2,1,0:T(8,128)(2,1)S(1)}, bf16[1,256,1024]{2,1,0:T(8,128)(2,1)}, u32[]{:S(2)}) copy-start(bf16[1,256,1024]{2,1,0:T(8,128)(2,1)} %param.7) | copy-start | bytes 1572868
  1.8 28.3 %collective-permute-start.1 = (bf16[129,1024]{1,0:T(8,128)(2,1)S(1)}, bf16[129,1024]{1,0:T(8,128)(2,1)S(1)}, u32[]{:S(2)}, u32[]{:S(2)}) collective-permute-start(bf16[129,1024]{1,0:T(8,128)(2,1)S(1)} %slice_bitcast_fusion), channel_id=1, source_target_pairs={{0,8},{8,16},{16,24},{24,32},{32,40},{40,48},{48,56},{56,64},{64,7... | collective-permute-start | bytes 792584 | tf_op jit(solution)/shard_map/ppermute | solution.py:10
  7.0 22.9 %collective-permute-start.2 = (bf16[129,1024]{1,0:T(8,128)(2,1)}, bf16[129,1024]{1,0:T(8,128)(2,1)S(1)}, u32[]{:S(2)}, u32[]{:S(2)}) collective-permute-start(bf16[129,1024]{1,0:T(8,128)(2,1)} %slice.342), channel_id=1, source_target_pairs={{0,8},{8,16},{16,24},{24,32},{32,40},{40,48},{48,56},{56,64},{64,7... | collective-permute-start | bytes 792584 | tf_op jit(solution)/shard_map/ppermute | solution.py:10
  11.2 15.7 %collective-permute-start = (bf16[2,1024]{1,0:T(2,128)(2,1)S(1)}, bf16[2,1024]{1,0:T(2,128)(2,1)S(1)}, u32[]{:S(2)}, u32[]{:S(2)}) collective-permute-start(bf16[2,1024]{1,0:T(2,128)(2,1)S(1)} %slice_bitcast_fusion.3), channel_id=1, source_target_pairs={{0,8},{8,16},{16,24},{24,32},{32,40},{40,48},{48,56},{56,64},{64,7... | collective-permute-start | bytes 12296 | tf_op jit(solution)/shard_map/ppermute | solution.py:10
  14.5 33.4 %collective-permute-start.11 = (bf16[2,1024]{1,0:T(2,128)(2,1)S(1)}, bf16[2,1024]{1,0:T(2,128)(2,1)S(1)}, u32[]{:S(2)}, u32[]{:S(2)}) collective-permute-start(bf16[2,1024]{1,0:T(2,128)(2,1)S(1)} %get-tuple-element.21), channel_id=1, source_target_pairs={{8,0},{16,8},{24,16},{32,24},{40,32},{48,40},{56,48},{64,56},{72,6... | collective-permute-start | bytes 12296 | tf_op jit(solution)/shard_map/ppermute | solution.py:10
  19.3 28.6 %collective-permute-start.6 = (bf16[2,1024]{1,0:T(2,128)(2,1)S(1)}, bf16[2,1024]{1,0:T(2,128)(2,1)S(1)}, u32[]{:S(2)}, u32[]{:S(2)}) collective-permute-start(bf16[2,1024]{1,0:T(2,128)(2,1)S(1)} %get-tuple-element.25), channel_id=1, source_target_pairs={{8,0},{16,8},{24,16},{32,24},{40,32},{48,40},{56,48},{64,56},{72,6... | collective-permute-start | bytes 12296 | tf_op jit(solution)/shard_map/ppermute | solution.py:10
  22.5 4.7 %copy-start.30 = (f32[1,1,1,1024]{3,0,2,1:T(1,128)}, f32[1,1,1,1024]{3,0,2,1:T(1,128)S(1)}, u32[]{:S(2)}) copy-start(f32[1,1,1,1024]{3,0,2,1:T(1,128)S(1)} %get-tuple-element.30) | copy-start | bytes 12292
  22.5 4.7 %copy-start.32 = (f32[1,1,1,1024]{3,0,2,1:T(1,128)}, f32[1,1,1,1024]{3,0,2,1:T(1,128)S(1)}, u32[]{:S(2)}) copy-start(f32[1,1,1,1024]{3,0,2,1:T(1,128)S(1)} %get-tuple-element.31) | copy-start | bytes 12292
  22.5 4.7 %copy-start.34 = (f32[1,1,1,1024]{3,0,2,1:T(1,128)}, f32[1,1,1,1024]{3,0,2,1:T(1,128)S(1)}, u32[]{:S(2)}) copy-start(f32[1,1,1,1024]{3,0,2,1:T(1,128)S(1)} %get-tuple-element.32) | copy-start | bytes 12292
  22.5 25.4 %copy-start.24 = (f32[1,1,1,1024]{3,0,2,1:T(1,128)}, f32[1,1,1,1024]{3,0,2,1:T(1,128)S(1)}, u32[]{:S(2)}) copy-start(f32[1,1,1,1024]{3,0,2,1:T(1,128)S(1)} %get-tuple-element.26) | copy-start | bytes 12292
  22.5 25.4 %copy-start.26 = (f32[1,1,1,1024]{3,0,2,1:T(1,128)}, f32[1,1,1,1024]{3,0,2,1:T(1,128)S(1)}, u32[]{:S(2)}) copy-start(f32[1,1,1,1024]{3,0,2,1:T(1,128)S(1)} %get-tuple-element.28) | copy-start | bytes 12292
  22.5 25.4 %copy-start.28 = (f32[1,1,1,1024]{3,0,2,1:T(1,128)}, f32[1,1,1,1024]{3,0,2,1:T(1,128)S(1)}, u32[]{:S(2)}) copy-start(f32[1,1,1,1024]{3,0,2,1:T(1,128)S(1)} %get-tuple-element.29) | copy-start | bytes 12292
  22.5 4.6 %copy-start.15 = (bf16[256,1024]{1,0:T(8,128)(2,1)S(1)}, bf16[256,1024]{1,0:T(8,128)(2,1)}, u32[]{:S(2)}) copy-start(bf16[256,1024]{1,0:T(8,128)(2,1)} %param.10) | copy-start | bytes 1572868
  27.6 21.7 %collective-permute-start.5 = (bf16[129,1024]{1,0:T(8,128)(2,1)S(1)}, bf16[129,1024]{1,0:T(8,128)(2,1)S(1)}, u32[]{:S(2)}, u32[]{:S(2)}) collective-permute-start(bf16[129,1024]{1,0:T(8,128)(2,1)S(1)} %slice.413), channel_id=1, source_target_pairs={{8,0},{16,8},{24,16},{32,24},{40,32},{48,40},{56,48},{64,56},{72,6... | collective-permute-start | bytes 792584 | tf_op jit(solution)/shard_map/ppermute | solution.py:10
  31.4 14.2 %copy-start.7 = (bf16[383,1024]{1,0:T(8,128)(2,1)}, bf16[383,1024]{1,0:T(8,128)(2,1)S(1)}, u32[]{:S(2)}) copy-start(bf16[383,1024]{1,0:T(8,128)(2,1)S(1)} %get-tuple-element.9) | copy-start | bytes 2353156
  31.4 14.2 %copy-start.23 = (f32[1,1024]{1,0:T(1,128)S(1)}, f32[1,1024]{1,0:T(1,128)}, u32[]{:S(2)}) copy-start(f32[1,1024]{1,0:T(1,128)} %param.13) | copy-start | bytes 12292
  46.5 45.1 %collective-permute-start.3 = (bf16[256,1024]{1,0:T(8,128)(2,1)S(1)}, bf16[256,1024]{1,0:T(8,128)(2,1)S(1)}, u32[]{:S(2)}, u32[]{:S(2)}) collective-permute-start(bf16[256,1024]{1,0:T(8,128)(2,1)S(1)} %multiply_convert_fusion.5), channel_id=1, source_target_pairs={{0,256},{1,257},{2,258},{3,259},{4,260},{5,261},{6,262},{7,263},{8... | collective-permute-start | bytes 1572872 | tf_op jit(solution)/shard_map/ppermute | solution.py:10
  48.1 72.6 %copy-start = (f32[256,1024]{1,0:T(8,128)}, f32[256,1024]{1,0:T(8,128)S(1)}, u32[]{:S(2)}) copy-start(f32[256,1024]{1,0:T(8,128)S(1)} %slice.416) | copy-start | bytes 3145732
  49.3 44.3 %copy-start.21 = (bf16[1,128,1024]{2,1,0:T(8,128)(2,1)S(1)}, bf16[1,128,1024]{2,1,0:T(8,128)(2,1)}, u32[]{:S(2)}) copy-start(bf16[1,128,1024]{2,1,0:T(8,128)(2,1)} %param.12) | copy-start | bytes 786436
  91.7 20.4 %collective-permute-start.12 = (bf16[2,1024]{1,0:T(2,128)(2,1)S(1)}, bf16[2,1024]{1,0:T(2,128)(2,1)S(1)}, u32[]{:S(2)}, u32[]{:S(2)}) collective-permute-start(bf16[2,1024]{1,0:T(2,128)(2,1)S(1)} %get-tuple-element.23), channel_id=1, source_target_pairs={{8,0},{16,8},{24,16},{32,24},{40,32},{48,40},{56,48},{64,56},{72,6... | collective-permute-start | bytes 12296 | tf_op jit(solution)/shard_map/ppermute | solution.py:10
  108.2 11.6 %collective-permute-start.4 = (bf16[129,1024]{1,0:T(8,128)(2,1)S(1)}, bf16[129,1024]{1,0:T(8,128)(2,1)S(1)}, u32[]{:S(2)}, u32[]{:S(2)}) collective-permute-start(bf16[129,1024]{1,0:T(8,128)(2,1)S(1)} %slice.408), channel_id=1, source_target_pairs={{0,8},{8,16},{16,24},{24,32},{32,40},{40,48},{48,56},{56,64},{64,7... | collective-permute-start | bytes 792584 | tf_op jit(solution)/shard_map/ppermute | solution.py:10
  120.5 18.0 %copy-start.5 = (bf16[383,1024]{1,0:T(8,128)(2,1)}, bf16[383,1024]{1,0:T(8,128)(2,1)S(1)}, u32[]{:S(2)}) copy-start(bf16[383,1024]{1,0:T(8,128)(2,1)S(1)} %get-tuple-element.7) | copy-start | bytes 2353156
  122.4 39.4 %collective-permute-start.7 = (bf16[256,1024]{1,0:T(8,128)(2,1)}, bf16[256,1024]{1,0:T(8,128)(2,1)}, u32[]{:S(2)}, u32[]{:S(2)}) collective-permute-start(bf16[256,1024]{1,0:T(8,128)(2,1)} %fusion.40), channel_id=1, source_target_pairs={{256,0},{257,1},{258,2},{259,3},{260,4},{261,5},{262,6},{263,7},{2... | collective-permute-start | bytes 1572872 | tf_op jit(solution)/shard_map/ppermute | solution.py:10
  159.0 2.9 copy-start.12
  165.0 13.9 %copy-start.2 = (bf16[256,1024]{1,0:T(8,128)(2,1)}, bf16[256,1024]{1,0:T(8,128)(2,1)S(1)}, u32[]{:S(2)}) copy-start(bf16[256,1024]{1,0:T(8,128)(2,1)S(1)} %get-tuple-element.18) | copy-start | bytes 1572868
  178.9 4.3 %copy-start.17 = (f32[128,1024]{1,0:T(8,128)S(1)}, f32[128,1024]{1,0:T(8,128)}, u32[]{:S(2)}) copy-start(f32[128,1024]{1,0:T(8,128)} %rev.12) | copy-start | bytes 1572868
  184.1 5.9 %copy-start.3 = (bf16[256,1024]{1,0:T(8,128)(2,1)S(1)}, bf16[256,1024]{1,0:T(8,128)(2,1)}, u32[]{:S(2)}) copy-start(bf16[256,1024]{1,0:T(8,128)(2,1)} %copy-done.2) | copy-start | bytes 1572868
  186.1 21.3 %copy-start.13 = (bf16[256,1024]{1,0:T(8,128)(2,1)S(1)}, bf16[256,1024]{1,0:T(8,128)(2,1)}, u32[]{:S(2)}) copy-start(bf16[256,1024]{1,0:T(8,128)(2,1)} %get-tuple-element.37) | copy-start | bytes 1572868
  186.1 23.2 %copy-start.14 = (bf16[256,1024]{1,0:T(8,128)(2,1)S(1)}, bf16[256,1024]{1,0:T(8,128)(2,1)}, u32[]{:S(2)}) copy-start(bf16[256,1024]{1,0:T(8,128)(2,1)} %get-tuple-element.19) | copy-start | bytes 1572868
  186.9 22.4 %collective-permute-start.8 = (bf16[2,1024]{1,0:T(2,128)(2,1)S(1)}, bf16[2,1024]{1,0:T(2,128)(2,1)S(1)}, u32[]{:S(2)}, u32[]{:S(2)}) collective-permute-start(bf16[2,1024]{1,0:T(2,128)(2,1)S(1)} %slice.423), channel_id=1, source_target_pairs={{8,0},{16,8},{24,16},{32,24},{40,32},{48,40},{56,48},{64,56},{72,6... | collective-permute-start | bytes 12296 | tf_op jit(solution)/shard_map/ppermute | solution.py:10
  190.0 24.5 %collective-permute-start.13 = (f32[2,2,2,2,4,1024]{5,4,3,1,0,2:T(4,128)S(1)}, f32[2,2,2,2,4,1024]{5,4,3,1,0,2:T(4,128)S(1)}, u32[]{:S(2)}, u32[]{:S(2)}) collective-permute-start(f32[2,2,2,2,4,1024]{5,4,3,1,0,2:T(4,128)S(1)} %bitcast.121), channel_id=1, source_target_pairs={{0,8},{8,0},{16,24},{24,16},{32,40},{40,32},{48,56},{56,48},{64,72... | collective-permute-start | bytes 786440 | tf_op jit(solution)/shard_map/ppermute | solution.py:28
  193.9 27.4 %collective-permute-start.10 = (bf16[129,1024]{1,0:T(8,128)(2,1)S(1)}, bf16[129,1024]{1,0:T(8,128)(2,1)S(1)}, u32[]{:S(2)}, u32[]{:S(2)}) collective-permute-start(bf16[129,1024]{1,0:T(8,128)(2,1)S(1)} %slice.431), channel_id=1, source_target_pairs={{8,0},{16,8},{24,16},{32,24},{40,32},{48,40},{56,48},{64,56},{72,6... | collective-permute-start | bytes 792584 | tf_op jit(solution)/shard_map/ppermute | solution.py:10
  207.4 5.5 %collective-permute-start.9 = (bf16[2,1024]{1,0:T(2,128)(2,1)S(1)}, bf16[2,1024]{1,0:T(2,128)(2,1)S(1)}, u32[]{:S(2)}, u32[]{:S(2)}) collective-permute-start(bf16[2,1024]{1,0:T(2,128)(2,1)S(1)} %slice.427), channel_id=1, source_target_pairs={{8,0},{16,8},{24,16},{32,24},{40,32},{48,40},{56,48},{64,56},{72,6... | collective-permute-start | bytes 12296 | tf_op jit(solution)/shard_map/ppermute | solution.py:10
  209.4 3.6 %copy-start.31 = (f32[1,1,1,1024]{3,0,2,1:T(1,128)S(1)}, f32[1,1,1,1024]{3,0,2,1:T(1,128)}, u32[]{:S(2)}) copy-start(f32[1,1,1,1024]{3,0,2,1:T(1,128)} %copy-done.30) | copy-start | bytes 12292
  209.5 3.6 %copy-start.33 = (f32[1,1,1,1024]{3,0,2,1:T(1,128)S(1)}, f32[1,1,1,1024]{3,0,2,1:T(1,128)}, u32[]{:S(2)}) copy-start(f32[1,1,1,1024]{3,0,2,1:T(1,128)} %copy-done.32) | copy-start | bytes 12292
  209.5 3.6 %copy-start.35 = (f32[1,1,1,1024]{3,0,2,1:T(1,128)S(1)}, f32[1,1,1,1024]{3,0,2,1:T(1,128)}, u32[]{:S(2)}) copy-start(f32[1,1,1,1024]{3,0,2,1:T(1,128)} %copy-done.34) | copy-start | bytes 12292
  214.6 9.7 %collective-permute-start.14 = (f32[2,2,2,4,1024]{4,3,2,1,0:T(4,128)S(1)}, f32[2,2,2,4,1024]{4,3,2,1,0:T(4,128)S(1)}, u32[]{:S(2)}, u32[]{:S(2)}) collective-permute-start(f32[2,2,2,4,1024]{4,3,2,1,0:T(4,128)S(1)} %dynamic-slice_bitcast_fusion), channel_id=1, source_target_pairs={{0,32},{8,40},{16,48},{24,56},{32,0},{40,8},{48,16},{56,24},{64,96... | collective-permute-start | bytes 393224 | tf_op jit(solution)/shard_map/ppermute | solution.py:28
  224.3 56.6 %copy-start.1 = (f32[256,1024]{1,0:T(8,128)S(1)}, f32[256,1024]{1,0:T(8,128)}, u32[]{:S(2)}) copy-start(f32[256,1024]{1,0:T(8,128)} %copy-done) | copy-start | bytes 3145732
  224.3 56.6 %copy-start.4 = (bf16[256,1024]{1,0:T(8,128)(2,1)S(1)}, bf16[256,1024]{1,0:T(8,128)(2,1)}, u32[]{:S(2)}) copy-start(bf16[256,1024]{1,0:T(8,128)(2,1)} %copy-done.2) | copy-start | bytes 1572868
  224.4 56.6 %copy-start.10 = (f32[256,1024]{1,0:T(8,128)S(1)}, f32[256,1024]{1,0:T(8,128)}, u32[]{:S(2)}) copy-start(f32[256,1024]{1,0:T(8,128)} %slice.434) | copy-start | bytes 3145732
  224.4 54.5 %collective-permute-start.15 = (f32[2,2,4,1024]{3,2,1,0:T(4,128)S(1)}, f32[2,2,4,1024]{3,2,1,0:T(4,128)S(1)}, u32[]{:S(2)}, u32[]{:S(2)}) collective-permute-start(f32[2,2,4,1024]{3,2,1,0:T(4,128)S(1)} %dynamic-slice_bitcast_fusion.1), channel_id=1, source_target_pairs={{0,128},{8,136},{16,144},{24,152},{32,160},{40,168},{48,176},{56,1... | collective-permute-start | bytes 196616 | tf_op jit(solution)/shard_map/ppermute | solution.py:28
  279.0 7.3 %collective-permute-start.16 = (f32[2,4,1024]{2,1,0:T(4,128)S(1)}, f32[2,4,1024]{2,1,0:T(4,128)S(1)}, u32[]{:S(2)}, u32[]{:S(2)}) collective-permute-start(f32[2,4,1024]{2,1,0:T(4,128)S(1)} %dynamic-slice_bitcast_fusion.2), channel_id=1, source_target_pairs={{0,16},{8,24},{16,0},{24,8},{32,48},{40,56},{48,32},{56,40},{64,80... | collective-permute-start | bytes 98312 | tf_op jit(solution)/shard_map/ppermute | solution.py:28
  280.9 7.3 %copy-start.25 = (f32[1,1,1,1024]{3,0,2,1:T(1,128)S(1)}, f32[1,1,1,1024]{3,0,2,1:T(1,128)}, u32[]{:S(2)}) copy-start(f32[1,1,1,1024]{3,0,2,1:T(1,128)} %copy-done.24) | copy-start | bytes 12292
  280.9 7.3 %copy-start.27 = (f32[1,1,1,1024]{3,0,2,1:T(1,128)S(1)}, f32[1,1,1,1024]{3,0,2,1:T(1,128)}, u32[]{:S(2)}) copy-start(f32[1,1,1,1024]{3,0,2,1:T(1,128)} %copy-done.26) | copy-start | bytes 12292
  280.9 7.3 %copy-start.29 = (f32[1,1,1,1024]{3,0,2,1:T(1,128)S(1)}, f32[1,1,1,1024]{3,0,2,1:T(1,128)}, u32[]{:S(2)}) copy-start(f32[1,1,1,1024]{3,0,2,1:T(1,128)} %copy-done.28) | copy-start | bytes 12292
  286.3 6.6 %collective-permute-start.17 = (f32[4,1024]{1,0:T(4,128)S(1)}, f32[4,1024]{1,0:T(4,128)S(1)}, u32[]{:S(2)}, u32[]{:S(2)}) collective-permute-start(f32[4,1024]{1,0:T(4,128)S(1)} %dynamic-slice_bitcast_fusion.3), channel_id=1, source_target_pairs={{0,64},{8,72},{16,80},{24,88},{32,96},{40,104},{48,112},{56,120},{... | collective-permute-start | bytes 49160 | tf_op jit(solution)/shard_map/ppermute | solution.py:28
  (6 other events, 12.1 us)

commit v2 on v1

v2 whole, which is shorter than its diff:
```python
import jax
import jax.numpy as jnp
from jax import lax
from jax.sharding import PartitionSpec as P


def shifted(value, axis, by):
    peers = lax.axis_size(axis)
    pairs = [(i, i + by) for i in range(peers) if 0 <= i + by < peers]
    return lax.ppermute(value, axis, pairs)


def halving_scatter(part, axis):
    peers = lax.axis_size(axis)
    steps = peers.bit_length() - 1
    if peers != 1 << steps or part.shape[0] % peers:
        return lax.psum_scatter(part, axis, scatter_dimension=0, tiled=True)
    me = lax.axis_index(axis)
    rows = part.shape[0] // peers
    held = part.reshape((2,) * steps + (rows,) + part.shape[1:])
    remaining = [steps - 1 - k for k in range(steps)]
    order = [0, 2, 1, 3, 4] if steps == 5 else list(range(steps))
    for bit in order:
        at = remaining.index(bit)
        mine = (me >> bit) & 1
        keep = lax.dynamic_index_in_dim(held, mine, axis=at, keepdims=False)
        give = lax.dynamic_index_in_dim(held, 1 - mine, axis=at, keepdims=False)
        got = lax.ppermute(give, axis, [(i, i ^ (1 << bit)) for i in range(peers)])
        held = keep + got
        remaining.pop(at)
    return held.reshape((rows,) + part.shape[1:])


def depthwise(source, kernel):
    result = lax.conv_general_dilated(
        source[None],
        kernel[:, None, :],
        (1,),
        "VALID",
        dimension_numbers=("NWC", "WIO", "NWC"),
        feature_group_count=source.shape[1],
        preferred_element_type=jnp.float32,
    )
    return result[0]


def fwd_short(rows, weights):
    wide = rows.astype(jnp.float32)
    return weights[0] * wide[2:] + weights[1] * wide[1:-1] + weights[2] * wide[:-2]


def bwd_short(rows, weights):
    wide = rows.astype(jnp.float32)
    return weights[0] * wide[:-2] + weights[1] * wide[1:-1] + weights[2] * wide[2:]


def from_prev(value):
    return shifted(value, "ctx", 1)


def from_next(value):
    return shifted(value, "ctx", -1)


def body(queries, keys, values, cotangent, short_filter, mix_filter, skip):
    first = lax.axis_index("section") == 0
    q, k = queries[0], keys[0]
    w_q, w_k, w_v = short_filter[0][0], short_filter[0][1], short_filter[0][2]
    taps = mix_filter[0]
    extent = taps.shape[0]
    back = taps[::-1]
    skip_row = skip[0]
    rows = q.shape[0]
    reach = extent + 1

    prev_a = from_prev(jnp.concatenate([q[-2:], k[-reach:], values[-reach:]], axis=0))
    next_a = from_next(jnp.concatenate([q[:reach], k[:2], values[:2], cotangent[:reach]], axis=0))
    q_ext = jnp.concatenate([prev_a[:2], q, next_a[:reach]], axis=0)
    k_ext = jnp.concatenate([prev_a[2 : 2 + reach], k, next_a[reach : reach + 2]], axis=0)
    v_ext = jnp.concatenate([prev_a[2 + reach :], values, next_a[reach + 2 : reach + 4]], axis=0)
    g_ext = jnp.concatenate([cotangent, next_a[reach + 4 :]], axis=0)

    q_short = fwd_short(q_ext, w_q)
    k_short = fwd_short(k_ext, w_k)
    v_first = fwd_short(v_ext, w_v)
    u_first = (k_short * v_first).astype(jnp.bfloat16)
    gz_last = (g_ext.astype(jnp.float32) * q_short).astype(jnp.bfloat16)

    sig_a = jnp.where(first, u_first, gz_last)
    conv_a = depthwise(sig_a, jnp.where(first, back, taps)) + skip_row * jnp.where(
        first, u_first[extent - 1 :], gz_last[: rows + 2]
    ).astype(jnp.float32)
    out_first = (q_short[:rows] * conv_a[:rows]).astype(jnp.bfloat16)
    gvs_last = (conv_a * k_short[extent - 1 :]).astype(jnp.bfloat16)
    gin_last = bwd_short(gvs_last, w_v).astype(jnp.bfloat16)

    handed = lax.ppermute(jnp.where(first, out_first, gin_last), "section", [(0, 1), (1, 0)])
    prev_b = from_prev(handed[-reach:])
    next_b = from_next(handed[:reach])
    y_ext = jnp.concatenate([prev_b, handed, next_b], axis=0)

    gz_first = (y_ext[reach:].astype(jnp.float32) * q_short).astype(jnp.bfloat16)
    v_last = fwd_short(y_ext[: reach + rows + 2], w_v)
    u_last = (k_short * v_last).astype(jnp.bfloat16)
    sig_b = jnp.where(first, gz_first, u_last)
    conv_b = depthwise(sig_b, jnp.where(first, taps, back)) + skip_row * jnp.where(
        first, gz_first[: rows + 2], u_last[extent - 1 :]
    ).astype(jnp.float32)

    z = jnp.where(first, conv_a, conv_b)
    gu = jnp.where(first, conv_b, conv_a)
    v_short = jnp.where(first, v_first, v_last)
    u = jnp.where(first, u_first, u_last)
    g = jnp.where(first, y_ext[reach : reach + rows + 2], g_ext[: rows + 2]).astype(jnp.float32)
    gz = jnp.where(first, gz_first, gz_last)

    output = (q_short[:rows] * z[:rows]).astype(jnp.bfloat16)
    gqs = (g * z).astype(jnp.bfloat16)
    gks = (gu * v_short[extent - 1 :]).astype(jnp.bfloat16)
    gvs = (gu * k_short[extent - 1 :]).astype(jnp.bfloat16)
    grad_q = bwd_short(gqs, w_q).astype(jnp.bfloat16)
    grad_k = bwd_short(gks, w_k).astype(jnp.bfloat16)
    grad_input = bwd_short(gvs, w_v).astype(jnp.bfloat16)
    taps_part = depthwise(u[: rows + extent - 1], gz[:rows])[::-1]
    tap_sum = halving_scatter(taps_part, "ctx")
    return (output[None], grad_q[None], grad_k[None], grad_input[None], tap_sum[None])


def solution(mesh):
    return jax.shard_map(
        body,
        mesh=mesh,
        in_specs=(
            P("section", "ctx", "chan"),
            P("section", "ctx", "chan"),
            P("ctx", "chan"),
            P("ctx", "chan"),
            P("section", None, None, "chan"),
            P("section", None, "chan"),
            P("section", "chan"),
        ),
        out_specs=(
            P("section", "ctx", "chan"),
            P("section", "ctx", "chan"),
            P("section", "ctx", "chan"),
            P("section", "ctx", "chan"),
            P("section", "ctx", "chan"),
        ),
        check_vma=False,
    )
```

time: 295 us -> 207 us (0.70)
  the two profiles are of different devices: /device:TPU:356 before, /device:TPU:6 now
where the time goes in v2:
time: 207 us; the launch traced here: 206 us
  starting transfers between devices  88.9 us (43%)
  matrix products  43.9 us (21%)
  waiting for transfers between devices  36.2 us (17%)
  local copies, waits for them, and re-layouts  18.9 us (9%)
  other arithmetic  16.7 us (8%)
    ppermute x5, starting transfers between devices, halving_scatter(): got = lax.ppermute(give, axis, [(i, i ^ 1 << bit) for i in range(peers)])  61.9 us
    conv_general_dilated x3, matrix products, depthwise(): lax.conv_general_dilated(source[None], kernel[:, None, :], (1,), 'VALID',...  43.9 us
    ppermute x1, starting transfers between devices, body(): lax.ppermute(jnp.where(first, out_first, gin_last), 'section', [(0, 1), (...  15.7 us
    ppermute x1, waiting for transfers between devices, body(): lax.ppermute(jnp.where(first, out_first, gin_last), 'section', [(0, 1), (...  15.1 us
    ppermute x4, waiting for transfers between devices, shifted(): return lax.ppermute(value, axis, pairs)  14.8 us
    ppermute x4, starting transfers between devices, shifted(): return lax.ppermute(value, axis, pairs)  11.3 us
    ppermute x5, waiting for transfers between devices, halving_scatter(): got = lax.ppermute(give, axis, [(i, i ^ 1 << bit) for i in range(peers)])  6.32 us
    unnamed x50, local copies, waits for them, and re-layouts  5.72 us
  transfers between devices with their start and end apart: 10, of which 9 were waited for; matrix products, arithmetic and copies ran while one was open for 12% of the time, Pallas kernels for 0%

profile of v2, /device:TPU:6, one launch (start us, length us, event | category | flops | bytes accessed | tf_op | source)
XLA Modules:
  0.0 205.9 jit_solution(387879916918695683)
XLA Ops:
  0.7 1.1 slice.250
  1.8 1.0 slice_bitcast_fusion.1
  2.8 0.7 slice_bitcast_fusion.3
  3.6 1.0 pad_maximum_fusion.3
  4.6 3.5 %collective-permute-start = (bf16[260,1024]{1,0:T(8,128)(2,1)}, bf16[260,1024]{1,0:T(8,128)(2,1)S(1)}, u32[]{:S(2)}, u32[]{:S(2)}) collective-permute-start(bf16[260,1024]{1,0:T(8,128)(2,1)} %pad_maximum_fusion.3), channel_id=1, source_target_pairs={{0,8},{8,16},{16,24},{24,32},{32,40},{40,48},{48,56},{56,64},{64,7... | collective-permute-start | bytes 1597448 | tf_op jit(solution)/shard_map/ppermute | solution.py:10
  8.1 0.9 pad_maximum_fusion.4
  9.1 1.3 collective-permute-start.1
  10.7 0.7 select_bitcast_fusion.2
  11.5 8.4 %collective-permute-done = bf16[260,1024]{1,0:T(8,128)(2,1)S(1)} collective-permute-done((bf16[260,1024]{1,0:T(8,128)(2,1)}, bf16[260,1024]{1,0:T(8,128)(2,1)S(1)}, u32[]{:S(2)}, u32[]{:S(2)}) %collective-permute-start) | collective-permute-done | bytes 532512 | tf_op jit(solution)/shard_map/ppermute | solution.py:10
  20.0 4.9 %collective-permute-done.1 = bf16[262,1024]{1,0:T(8,128)(2,1)S(1)} collective-permute-done((bf16[262,1024]{1,0:T(8,128)(2,1)}, bf16[262,1024]{1,0:T(8,128)(2,1)S(1)}, u32[]{:S(2)}, u32[]{:S(2)}) %collective-permute-start.1) | collective-permute-done | bytes 536608 | tf_op jit(solution)/shard_map/ppermute | solution.py:10
  25.7 0.6 copy-done.16
  26.3 2.7 %select_bitcast_fusion.1 = (bf16[1,385,1024]{2,1,0:T(8,128)(2,1)S(1)}, bf16[385,1024]{1,0:T(8,128)(2,1)S(1)}, f32[385,1024]{1,0:T(8,128)S(1)}, bf16[385,1024]{1,...) fusion(pred[]{:T(512)S(6)} %eq.3, bf16[129,1024]{1,0:T(8,128)(2,1)S(1)} %get-tuple-element.28, ...), kind=kLoop, calls=%fused_computation.77 | loop fusion | flops 9461760 | bytes 22114304 | tf_op jit(solution)/shard_map/broadcast_in_dim | solution.py:36
  29.0 14.5 %fusion.10 = f32[1,258,1024]{2,0,1:T(1,128)S(1)} fusion(bf16[1,385,1024]{2,1,0:T(8,128)(2,1)S(1)} %get-tuple-element.13, bf16[128,1,1024]{2,0,1:T(8,128)(2,1)S(1)} %get-tuple-element.32), kind=kOutput, calls=%fused_computation.26 | convolution fusion | flops 67633152 | bytes 2107392 | tf_op jit(solution)/shard_map/conv_general_dilated | solution.py:35
  43.5 0.5 fusion.37
  44.4 0.6 copy-done
  45.0 15.7 %collective-permute-start.2 = (bf16[256,1024]{1,0:T(8,128)(2,1)S(1)}, bf16[256,1024]{1,0:T(8,128)(2,1)S(1)}, u32[]{:S(2)}, u32[]{:S(2)}) collective-permute-start(bf16[256,1024]{1,0:T(8,128)(2,1)S(1)} %fusion.41), channel_id=1, source_target_pairs={{0,256},{256,0},{1,257},{257,1},{2,258},{258,2},{3,259},{259,3},{4... | collective-permute-start | bytes 1572872 | tf_op jit(solution)/shard_map/ppermute | solution.py:97
  60.7 15.1 %collective-permute-done.2 = bf16[256,1024]{1,0:T(8,128)(2,1)S(1)} collective-permute-done((bf16[256,1024]{1,0:T(8,128)(2,1)S(1)}, bf16[256,1024]{1,0:T(8,128)(2,1)S(1)}, u32[]{:S(2)}, u32[]{:S(2)}) %collective-permute-start.2) | collective-permute-done | bytes 524320 | tf_op jit(solution)/shard_map/ppermute | solution.py:97
  75.9 0.8 copy-done.6
  76.7 0.9 fusion.58
  77.6 1.3 collective-permute-start.3
  78.8 5.3 %collective-permute-start.4 = (bf16[129,1024]{1,0:T(8,128)(2,1)}, bf16[129,1024]{1,0:T(8,128)(2,1)}, u32[]{:S(2)}, u32[]{:S(2)}) collective-permute-start(bf16[129,1024]{1,0:T(8,128)(2,1)} %get-tuple-element.33), channel_id=1, source_target_pairs={{0,8},{8,16},{16,24},{24,32},{32,40},{40,48},{48,56},{56,64},{64,7... | collective-permute-start | bytes 792584 | tf_op jit(solution)/shard_map/ppermute | solution.py:10
  84.1 1.1 constant_dynamic-update-slice_fusion.1
  85.3 1.0 collective-permute-done.3
  86.3 1.0 constant_dynamic-update-slice_fusion
  87.8 1.1 fusion.31
  88.9 2.3 %select_bitcast_fusion = (bf16[1,385,1024]{2,1,0:T(8,128)(2,1)}, bf16[385,1024]{1,0:T(8,128)(2,1)S(1)}, f32[385,1024]{1,0:T(8,128)}, bf16[385,1024]{1,0:T(8,128)(2,1)S(1)}) fusion(pred[]{:T(512)S(6)} %eq.3, f32[385,1024]{1,0:T(8,128)S(1)} %get-tuple-element.18, f32[387,1024]{1,0:T(8,128)S(1)} %fusion.31, f32[1024]{0:T(1024)S(1)} %bitcast.96, ...), kind=kLoop, calls=%fused_computation.76 | loop fusion | flops 4336640 | bytes 12627969 | tf_op jit(solution)/shard_map/broadcast_in_dim | solution.py:36
  91.3 1.6 copy-done.3
  93.1 13.9 %fusion.12 = f32[1,128,1024]{2,0,1:T(1,128)S(1)} fusion(bf16[1,383,1024]{2,1,0:T(8,128)(2,1)S(1)} %fusion.32, bf16[256,1,1024]{2,0,1:T(8,128)(2,1)S(1)} %fusion.46), kind=kOutput, calls=%fused_computation.28 | convolution fusion | flops 67108864 | bytes 1832960 | tf_op jit(solution)/shard_map/conv_general_dilated | solution.py:35
  107.0 0.9 copy.56
  107.9 4.7 %rev.7 = f32[128,1024]{1,0:T(8,128)} reverse(f32[128,1024]{1,0:T(8,128)} %bitcast.85), dimensions={0} | reverse | bytes 1048576 | tf_op jit(solution)/shard_map/rev | solution.py:124
  112.6 2.0 reshape.41
  114.6 1.1 constant_dynamic-slice_fusion.1
  115.7 4.6 %collective-permute-start.5 = (f32[2,2,2,2,4,1024]{5,4,3,1,0,2:T(4,128)S(1)}, f32[2,2,2,2,4,1024]{5,4,3,1,0,2:T(4,128)S(1)}, u32[]{:S(2)}, u32[]{:S(2)}) collective-permute-start(f32[2,2,2,2,4,1024]{5,4,3,1,0,2:T(4,128)S(1)} %bitcast.89), channel_id=1, source_target_pairs={{0,8},{8,0},{16,24},{24,16},{32,40},{40,32},{48,56},{56,48},{64,72... | collective-permute-start | bytes 786440 | tf_op jit(solution)/shard_map/ppermute | solution.py:28
  120.3 15.6 %fusion.8 = f32[1,258,1024]{2,0,1:T(1,128)S(1)} fusion(bf16[1,385,1024]{2,1,0:T(8,128)(2,1)} %get-tuple-element.7, bf16[128,1,1024]{2,0,1:T(8,128)(2,1)} %get-tuple-element.31), kind=kOutput, calls=%fused_computation.24 | convolution fusion | flops 67633152 | bytes 2107392 | tf_op jit(solution)/shard_map/conv_general_dilated | solution.py:35
  136.0 1.1 fusion.39
  137.2 33.8 %collective-permute-start.6 = (f32[2,2,2,4,1024]{4,3,2,1,0:T(4,128)S(1)}, f32[2,2,2,4,1024]{4,3,2,1,0:T(4,128)S(1)}, u32[]{:S(2)}, u32[]{:S(2)}) collective-permute-start(f32[2,2,2,4,1024]{4,3,2,1,0:T(4,128)S(1)} %dynamic-slice_bitcast_fusion), channel_id=1, source_target_pairs={{0,32},{8,40},{16,48},{24,56},{32,0},{40,8},{48,16},{56,24},{64,96... | collective-permute-start | bytes 393224 | tf_op jit(solution)/shard_map/ppermute | solution.py:28
  171.0 0.9 fusion.42
  172.0 2.0 collective-permute-done.6
  174.0 3.5 %collective-permute-start.7 = (f32[2,2,4,1024]{3,2,1,0:T(4,128)S(1)}, f32[2,2,4,1024]{3,2,1,0:T(4,128)S(1)}, u32[]{:S(2)}, u32[]{:S(2)}) collective-permute-start(f32[2,2,4,1024]{3,2,1,0:T(4,128)S(1)} %dynamic-slice_bitcast_fusion.1), channel_id=1, source_target_pairs={{0,16},{8,24},{16,0},{24,8},{32,48},{40,56},{48,32},{56,40},{64,80... | collective-permute-start | bytes 196616 | tf_op jit(solution)/shard_map/ppermute | solution.py:28
  177.6 1.1 fusion.43
  178.7 3.0 %collective-permute-done.7 = f32[2,2,4,1024]{3,2,1,0:T(4,128)S(1)} collective-permute-done((f32[2,2,4,1024]{3,2,1,0:T(4,128)S(1)}, f32[2,2,4,1024]{3,2,1,0:T(4,128)S(1)}, u32[]{:S(2)}, u32[]{:S(2)}) %collective-permute-start.7) | collective-permute-done | bytes 65568 | tf_op jit(solution)/shard_map/ppermute | solution.py:28
  181.7 9.1 %collective-permute-start.8 = (f32[2,4,1024]{2,1,0:T(4,128)S(1)}, f32[2,4,1024]{2,1,0:T(4,128)S(1)}, u32[]{:S(2)}, u32[]{:S(2)}) collective-permute-start(f32[2,4,1024]{2,1,0:T(4,128)S(1)} %dynamic-slice_bitcast_fusion.2), channel_id=1, source_target_pairs={{0,64},{8,72},{16,80},{24,88},{32,96},{40,104},{48,112},{56,120},{... | collective-permute-start | bytes 98312 | tf_op jit(solution)/shard_map/ppermute | solution.py:28
  190.9 1.1 fusion.44
  192.0 0.8 collective-permute-done.8
  192.8 10.8 %collective-permute-start.9 = (f32[4,1024]{1,0:T(4,128)S(1)}, f32[4,1024]{1,0:T(4,128)S(1)}, u32[]{:S(2)}, u32[]{:S(2)}) collective-permute-start(f32[4,1024]{1,0:T(4,128)S(1)} %dynamic-slice_bitcast_fusion.3), channel_id=1, source_target_pairs={{0,128},{8,136},{16,144},{24,152},{32,160},{40,168},{48,176},{56,1... | collective-permute-start | bytes 49160 | tf_op jit(solution)/shard_map/ppermute | solution.py:28
  203.6 1.1 fusion.45
  204.7 0.6 collective-permute-done.9
  205.3 0.6 fusion.49
  (72 shorter events, 2.6 us)
Async XLA Ops:
  0.6 7.5 %slice-start.1 = ((bf16[256,1024]{1,0:T(8,128)(2,1)}), bf16[2,1024]{1,0:T(2,128)(2,1)S(1)}, s32[]{:S(2)}) async-start(bf16[256,1024]{1,0:T(8,128)(2,1)} %param.9), calls=%async_computation.1 | async-start | bytes 8192 | tf_op jit(solution)/shard_map/slice | solution.py:77
  0.6 7.5 %copy-start.19 = (bf16[1,256,1024]{2,1,0:T(8,128)(2,1)S(1)}, bf16[1,256,1024]{2,1,0:T(8,128)(2,1)}, u32[]{:S(2)}) copy-start(bf16[1,256,1024]{2,1,0:T(8,128)(2,1)} %param.8) | copy-start | bytes 1572868
  0.7 7.4 %copy-start.20 = (bf16[1,256,1024]{2,1,0:T(8,128)(2,1)S(1)}, bf16[1,256,1024]{2,1,0:T(8,128)(2,1)}, u32[]{:S(2)}) copy-start(bf16[1,256,1024]{2,1,0:T(8,128)(2,1)} %param.7) | copy-start | bytes 1572868
  0.7 7.5 %slice-start = ((bf16[256,1024]{1,0:T(8,128)(2,1)}), bf16[129,1024]{1,0:T(8,128)(2,1)S(1)}, s32[]{:S(2)}) async-start(bf16[256,1024]{1,0:T(8,128)(2,1)} %param.10), calls=%async_computation | async-start | bytes 557056 | tf_op jit(solution)/shard_map/slice | solution.py:77
  3.6 6.8 %copy-start.22 = (f32[1,3,3,1024]{3,0,2,1:T(1,128)S(1)}, f32[1,3,3,1024]{3,0,2,1:T(1,128)}, u32[]{:S(2)}) copy-start(f32[1,3,3,1024]{3,0,2,1:T(1,128)} %param.11) | copy-start | bytes 110596
  3.6 6.8 %copy-start.21 = (bf16[1,128,1024]{2,1,0:T(8,128)(2,1)S(1)}, bf16[1,128,1024]{2,1,0:T(8,128)(2,1)}, u32[]{:S(2)}) copy-start(bf16[1,128,1024]{2,1,0:T(8,128)(2,1)} %param.12) | copy-start | bytes 786436
  4.6 15.3 %collective-permute-start = (bf16[260,1024]{1,0:T(8,128)(2,1)}, bf16[260,1024]{1,0:T(8,128)(2,1)S(1)}, u32[]{:S(2)}, u32[]{:S(2)}) collective-permute-start(bf16[260,1024]{1,0:T(8,128)(2,1)} %pad_maximum_fusion.3), channel_id=1, source_target_pairs={{0,8},{8,16},{16,24},{24,32},{32,40},{40,48},{48,56},{56,64},{64,7... | collective-permute-start | bytes 1597448 | tf_op jit(solution)/shard_map/ppermute | solution.py:10
  9.1 15.8 %collective-permute-start.1 = (bf16[262,1024]{1,0:T(8,128)(2,1)}, bf16[262,1024]{1,0:T(8,128)(2,1)S(1)}, u32[]{:S(2)}, u32[]{:S(2)}) collective-permute-start(bf16[262,1024]{1,0:T(8,128)(2,1)} %pad_maximum_fusion.4), channel_id=1, source_target_pairs={{8,0},{16,8},{24,16},{32,24},{40,32},{48,40},{56,48},{64,56},{72,6... | collective-permute-start | bytes 1609736 | tf_op jit(solution)/shard_map/ppermute | solution.py:10
  20.0 5.2 %copy-start.18 = (bf16[256,1024]{1,0:T(8,128)(2,1)S(1)}, bf16[256,1024]{1,0:T(8,128)(2,1)}, u32[]{:S(2)}) copy-start(bf16[256,1024]{1,0:T(8,128)(2,1)} %param.9) | copy-start | bytes 1572868
  25.2 1.0 copy-start.16
  29.0 14.5 %copy-start.2 = (bf16[385,1024]{1,0:T(8,128)(2,1)}, bf16[385,1024]{1,0:T(8,128)(2,1)S(1)}, u32[]{:S(2)}) copy-start(bf16[385,1024]{1,0:T(8,128)(2,1)S(1)} %get-tuple-element.16) | copy-start | bytes 2365444
  29.0 14.5 %copy-start.10 = (bf16[385,1024]{1,0:T(8,128)(2,1)}, bf16[385,1024]{1,0:T(8,128)(2,1)S(1)}, u32[]{:S(2)}) copy-start(bf16[385,1024]{1,0:T(8,128)(2,1)S(1)} %get-tuple-element.14) | copy-start | bytes 2365444
  29.0 14.5 %copy-start.23 = (f32[1,1024]{1,0:T(1,128)S(1)}, f32[1,1024]{1,0:T(1,128)}, u32[]{:S(2)}) copy-start(f32[1,1024]{1,0:T(1,128)} %param.13) | copy-start | bytes 12292
  44.0 1.0 copy-start
  45.0 30.9 %collective-permute-start.2 = (bf16[256,1024]{1,0:T(8,128)(2,1)S(1)}, bf16[256,1024]{1,0:T(8,128)(2,1)S(1)}, u32[]{:S(2)}, u32[]{:S(2)}) collective-permute-start(bf16[256,1024]{1,0:T(8,128)(2,1)S(1)} %fusion.41), channel_id=1, source_target_pairs={{0,256},{256,0},{1,257},{257,1},{2,258},{258,2},{3,259},{259,3},{4... | collective-permute-start | bytes 1572872 | tf_op jit(solution)/shard_map/ppermute | solution.py:97
  75.9 0.8 copy-start.6
  77.6 8.7 %collective-permute-start.3 = (bf16[129,1024]{1,0:T(8,128)(2,1)}, bf16[129,1024]{1,0:T(8,128)(2,1)}, u32[]{:S(2)}, u32[]{:S(2)}) collective-permute-start(bf16[129,1024]{1,0:T(8,128)(2,1)} %get-tuple-element.34), channel_id=1, source_target_pairs={{8,0},{16,8},{24,16},{32,24},{40,32},{48,40},{56,48},{64,56},{72,6... | collective-permute-start | bytes 792584 | tf_op jit(solution)/shard_map/ppermute | solution.py:10
  78.8 8.9 %collective-permute-start.4 = (bf16[129,1024]{1,0:T(8,128)(2,1)}, bf16[129,1024]{1,0:T(8,128)(2,1)}, u32[]{:S(2)}, u32[]{:S(2)}) collective-permute-start(bf16[129,1024]{1,0:T(8,128)(2,1)} %get-tuple-element.33), channel_id=1, source_target_pairs={{0,8},{8,16},{16,24},{24,32},{32,40},{40,48},{48,56},{56,64},{64,7... | collective-permute-start | bytes 792584 | tf_op jit(solution)/shard_map/ppermute | solution.py:10
  84.1 3.7 %copy-start.7 = (bf16[256,1024]{1,0:T(8,128)(2,1)S(1)}, bf16[256,1024]{1,0:T(8,128)(2,1)}, u32[]{:S(2)}) copy-start(bf16[256,1024]{1,0:T(8,128)(2,1)} %copy-done.6) | copy-start | bytes 1572868
  87.3 4.0 %copy-start.14 = (bf16[385,1024]{1,0:T(8,128)(2,1)}, bf16[385,1024]{1,0:T(8,128)(2,1)S(1)}, u32[]{:S(2)}) copy-start(bf16[385,1024]{1,0:T(8,128)(2,1)S(1)} %constant_dynamic-update-slice_fusion) | copy-start | bytes 2365444
  88.9 2.3 %copy-start.11 = (bf16[385,1024]{1,0:T(8,128)(2,1)S(1)}, bf16[385,1024]{1,0:T(8,128)(2,1)}, u32[]{:S(2)}) copy-start(bf16[385,1024]{1,0:T(8,128)(2,1)} %copy-done.10) | copy-start | bytes 2365444
  91.2 1.8 copy-start.4
  91.2 1.8 copy-start.12
  91.2 1.7 copy-start.3
  115.7 21.4 %collective-permute-start.5 = (f32[2,2,2,2,4,1024]{5,4,3,1,0,2:T(4,128)S(1)}, f32[2,2,2,2,4,1024]{5,4,3,1,0,2:T(4,128)S(1)}, u32[]{:S(2)}, u32[]{:S(2)}) collective-permute-start(f32[2,2,2,2,4,1024]{5,4,3,1,0,2:T(4,128)S(1)} %bitcast.89), channel_id=1, source_target_pairs={{0,8},{8,0},{16,24},{24,16},{32,40},{40,32},{48,56},{56,48},{64,72... | collective-permute-start | bytes 786440 | tf_op jit(solution)/shard_map/ppermute | solution.py:28
  120.3 15.7 %copy-start.1 = (f32[258,1024]{1,0:T(8,128)S(1)}, f32[258,1024]{1,0:T(8,128)}, u32[]{:S(2)}) copy-start(f32[258,1024]{1,0:T(8,128)} %copy-done) | copy-start | bytes 3170308
  120.3 15.7 %copy-start.5 = (bf16[385,1024]{1,0:T(8,128)(2,1)S(1)}, bf16[385,1024]{1,0:T(8,128)(2,1)}, u32[]{:S(2)}) copy-start(bf16[385,1024]{1,0:T(8,128)(2,1)} %copy-done.4) | copy-start | bytes 2365444
  120.3 15.7 %copy-start.8 = (f32[385,1024]{1,0:T(8,128)S(1)}, f32[385,1024]{1,0:T(8,128)}, u32[]{:S(2)}) copy-start(f32[385,1024]{1,0:T(8,128)} %get-tuple-element.9) | copy-start | bytes 4730884
  120.3 15.7 %copy-start.9 = (f32[385,1024]{1,0:T(8,128)S(1)}, f32[385,1024]{1,0:T(8,128)}, u32[]{:S(2)}) copy-start(f32[385,1024]{1,0:T(8,128)} %get-tuple-element.17) | copy-start | bytes 4730884
  120.3 15.7 %copy-start.13 = (bf16[385,1024]{1,0:T(8,128)(2,1)S(1)}, bf16[385,1024]{1,0:T(8,128)(2,1)}, u32[]{:S(2)}) copy-start(bf16[385,1024]{1,0:T(8,128)(2,1)} %copy-done.12) | copy-start | bytes 2365444
  120.3 15.7 %copy-start.15 = (bf16[385,1024]{1,0:T(8,128)(2,1)S(1)}, bf16[385,1024]{1,0:T(8,128)(2,1)}, u32[]{:S(2)}) copy-start(bf16[385,1024]{1,0:T(8,128)(2,1)} %copy-done.14) | copy-start | bytes 2365444
  120.3 15.7 %copy-start.17 = (bf16[256,1024]{1,0:T(8,128)(2,1)S(1)}, bf16[256,1024]{1,0:T(8,128)(2,1)}, u32[]{:S(2)}) copy-start(bf16[256,1024]{1,0:T(8,128)(2,1)} %param.10) | copy-start | bytes 1572868
  137.2 36.8 %collective-permute-start.6 = (f32[2,2,2,4,1024]{4,3,2,1,0:T(4,128)S(1)}, f32[2,2,2,4,1024]{4,3,2,1,0:T(4,128)S(1)}, u32[]{:S(2)}, u32[]{:S(2)}) collective-permute-start(f32[2,2,2,4,1024]{4,3,2,1,0:T(4,128)S(1)} %dynamic-slice_bitcast_fusion), channel_id=1, source_target_pairs={{0,32},{8,40},{16,48},{24,56},{32,0},{40,8},{48,16},{56,24},{64,96... | collective-permute-start | bytes 393224 | tf_op jit(solution)/shard_map/ppermute | solution.py:28
  174.0 7.7 %collective-permute-start.7 = (f32[2,2,4,1024]{3,2,1,0:T(4,128)S(1)}, f32[2,2,4,1024]{3,2,1,0:T(4,128)S(1)}, u32[]{:S(2)}, u32[]{:S(2)}) collective-permute-start(f32[2,2,4,1024]{3,2,1,0:T(4,128)S(1)} %dynamic-slice_bitcast_fusion.1), channel_id=1, source_target_pairs={{0,16},{8,24},{16,0},{24,8},{32,48},{40,56},{48,32},{56,40},{64,80... | collective-permute-start | bytes 196616 | tf_op jit(solution)/shard_map/ppermute | solution.py:28
  181.7 11.0 %collective-permute-start.8 = (f32[2,4,1024]{2,1,0:T(4,128)S(1)}, f32[2,4,1024]{2,1,0:T(4,128)S(1)}, u32[]{:S(2)}, u32[]{:S(2)}) collective-permute-start(f32[2,4,1024]{2,1,0:T(4,128)S(1)} %dynamic-slice_bitcast_fusion.2), channel_id=1, source_target_pairs={{0,64},{8,72},{16,80},{24,88},{32,96},{40,104},{48,112},{56,120},{... | collective-permute-start | bytes 98312 | tf_op jit(solution)/shard_map/ppermute | solution.py:28
  192.8 12.5 %collective-permute-start.9 = (f32[4,1024]{1,0:T(4,128)S(1)}, f32[4,1024]{1,0:T(4,128)S(1)}, u32[]{:S(2)}, u32[]{:S(2)}) collective-permute-start(f32[4,1024]{1,0:T(4,128)S(1)} %dynamic-slice_bitcast_fusion.3), channel_id=1, source_target_pairs={{0,128},{8,136},{16,144},{24,152},{32,160},{40,168},{48,176},{56,1... | collective-permute-start | bytes 49160 | tf_op jit(solution)/shard_map/ppermute | solution.py:28

commit v3 on v2

--- a/solution.py
+++ b/solution.py
@@ -126,9 +126,20 @@
     return (output[None], grad_q[None], grad_k[None], grad_input[None], tap_sum[None])
 
 
+def chunked(*args, pieces=2):
+    width = args[0].shape[-1]
+    if width % (pieces * 128):
+        return body(*args)
+    step = width // pieces
+    parts = []
+    for i in range(pieces):
+        parts.append(body(*(a[..., i * step : (i + 1) * step] for a in args)))
+    return tuple(jnp.concatenate(group, axis=-1) for group in zip(*parts))
+
+
 def solution(mesh):
     return jax.shard_map(
-        body,
+        chunked,
         mesh=mesh,
         in_specs=(
             P("section", "ctx", "chan"),

time: 207 us -> 207 us (level)
  waiting for transfers between devices: 36.2 us -> 31.6 us
  other arithmetic: 16.7 us -> 20.2 us
  starting transfers between devices: 88.9 us -> 91.5 us
    ppermute x4 -> x8, starting transfers between devices: 11.3 us -> 29.8 us  [shifted(): return lax.ppermute(value, axis, pairs)]
    ppermute x5 -> x10, starting transfers between devices: 61.9 us -> 44.1 us  [halving_scatter(): got = lax.ppermute(give, axis, [(i, i ^ 1 << bit) for i in range(peers)])]
    ppermute x4 -> x8, waiting for transfers between devices: 14.8 us -> 3.02 us  [shifted(): return lax.ppermute(value, axis, pairs)]
    ppermute x1 -> x2, waiting for transfers between devices: 15.1 us -> 23.1 us  [body(): lax.ppermute(jnp.where(first, out_first, gin_last), 'section', [(0, 1), (...]
    rev x1 -> x2, local copies, waits for them, and re-layouts: 4.74 us -> 0.28 us  [body(): taps_part = depthwise(u[:rows + extent - 1], gz[:rows])[::-1]]
    concatenate x0 -> x5, other arithmetic: none -> 4.07 us  [chunked(): return tuple((jnp.concatenate(group, axis=-1) for group in zip(*parts)))]
    slice x2 -> x4, local copies, waits for them, and re-layouts: 0.07 us -> 3.48 us  [body(): q_ext = jnp.concatenate([prev_a[:2], q, next_a[:reach]], axis=0)]
    ppermute x1 -> x2, starting transfers between devices: 15.7 us -> 17.6 us  [body(): lax.ppermute(jnp.where(first, out_first, gin_last), 'section', [(0, 1), (...]
  transfers between devices with their start and end apart: 10 -> 20, of which waited for: 9 -> 4; matrix products, arithmetic and copies ran while one was open for 12% -> 21% of each run, Pallas kernels for 0% -> 0%
where the time goes in v3:
time: 207 us; the launch traced here: 206 us
  starting transfers between devices  91.5 us (44%)
  matrix products  42.3 us (20%)
  waiting for transfers between devices  31.6 us (15%)
  other arithmetic  20.2 us (10%)
  local copies, waits for them, and re-layouts  18.3 us (9%)
    ppermute x10, starting transfers between devices, halving_scatter(): got = lax.ppermute(give, axis, [(i, i ^ 1 << bit) for i in range(peers)])  44.1 us
    conv_general_dilated x6, matrix products, depthwise(): lax.conv_general_dilated(source[None], kernel[:, None, :], (1,), 'VALID',...  42.3 us
    ppermute x8, starting transfers between devices, shifted(): return lax.ppermute(value, axis, pairs)  29.8 us
    ppermute x2, waiting for transfers between devices, body(): lax.ppermute(jnp.where(first, out_first, gin_last), 'section', [(0, 1), (...  23.1 us
    ppermute x2, starting transfers between devices, body(): lax.ppermute(jnp.where(first, out_first, gin_last), 'section', [(0, 1), (...  17.6 us
    unnamed x72, local copies, waits for them, and re-layouts  5.6 us
    ppermute x10, waiting for transfers between devices, halving_scatter(): got = lax.ppermute(give, axis, [(i, i ^ 1 << bit) for i in range(peers)])  5.46 us
    broadcast_in_dim x6, other arithmetic, depthwise(): source[None]  4.5 us
  transfers between devices with their start and end apart: 20, of which 4 were waited for; matrix products, arithmetic and copies ran while one was open for 21% of the time, Pallas kernels for 0%

profile of v3, /device:TPU:6, one launch (start us, length us, event | category | flops | bytes accessed | tf_op | source)
XLA Modules:
  0.0 205.6 jit_solution(2587744471149506129)
XLA Ops:
  0.6 1.1 fusion.114
  3.9 1.3 collective-permute-start.6
  6.0 1.3 collective-permute-start.1
  7.5 0.8 pad_maximum_fusion.10
  8.3 5.9 %collective-permute-start = (bf16[260,512]{1,0:T(8,128)(2,1)}, bf16[260,512]{1,0:T(8,128)(2,1)}, u32[]{:S(2)}, u32[]{:S(2)}) collective-permute-start(bf16[260,512]{1,0:T(8,128)(2,1)} %pad_maximum_fusion.10), channel_id=1, source_target_pairs={{0,8},{8,16},{16,24},{24,32},{32,40},{40,48},{48,56},{56,64},{64,7... | collective-permute-start | bytes 798728 | tf_op jit(solution)/shard_map/ppermute | solution.py:10
  14.9 3.9 %collective-permute-start.5 = (bf16[260,512]{1,0:T(8,128)(2,1)}, bf16[260,512]{1,0:T(8,128)(2,1)}, u32[]{:S(2)}, u32[]{:S(2)}) collective-permute-start(bf16[260,512]{1,0:T(8,128)(2,1)} %pad_maximum_fusion.12), channel_id=1, source_target_pairs={{0,8},{8,16},{16,24},{24,32},{32,40},{40,48},{48,56},{56,64},{64,7... | collective-permute-start | bytes 798728 | tf_op jit(solution)/shard_map/ppermute | solution.py:10
  22.0 3.0 %collective-permute-done.5 = bf16[260,512]{1,0:T(8,128)(2,1)} collective-permute-done((bf16[260,512]{1,0:T(8,128)(2,1)}, bf16[260,512]{1,0:T(8,128)(2,1)}, u32[]{:S(2)}, u32[]{:S(2)}) %collective-permute-start.5) | collective-permute-done | bytes 266272 | tf_op jit(solution)/shard_map/ppermute | solution.py:10
  25.0 1.0 fusion.118
  26.1 1.1 fusion.115
  28.5 1.0 fusion.120
  29.6 1.1 fusion.117
  31.9 1.8 select_bitcast_fusion.1
  33.7 7.1 %fusion.18 = f32[1,258,512]{2,0,1:T(1,128)S(1)} fusion(bf16[1,385,512]{2,1,0:T(8,128)(2,1)S(1)} %get-tuple-element.27, bf16[128,1,512]{2,0,1:T(8,128)(2,1)S(1)} %get-tuple-element.83), kind=kOutput, calls=%fused_computation.50 | convolution fusion | flops 33816576 | bytes 1053696 | tf_op jit(solution)/shard_map/conv_general_dilated | solution.py:35
  41.0 0.9 fusion.84
  41.9 15.7 %collective-permute-start.7 = (bf16[256,512]{1,0:T(8,128)(2,1)}, bf16[256,512]{1,0:T(8,128)(2,1)}, u32[]{:S(2)}, u32[]{:S(2)}) collective-permute-start(bf16[256,512]{1,0:T(8,128)(2,1)} %fusion.84), channel_id=1, source_target_pairs={{0,256},{256,0},{1,257},{257,1},{2,258},{258,2},{3,259},{259,3},{4... | collective-permute-start | bytes 786440 | tf_op jit(solution)/shard_map/ppermute | solution.py:97
  58.7 1.8 select_bitcast_fusion.3
  60.5 7.1 %fusion.22 = f32[1,258,512]{2,0,1:T(1,128)S(1)} fusion(bf16[1,385,512]{2,1,0:T(8,128)(2,1)S(1)} %get-tuple-element.15, bf16[128,1,512]{2,0,1:T(8,128)(2,1)S(1)} %get-tuple-element.64), kind=kOutput, calls=%fused_computation.54 | convolution fusion | flops 33816576 | bytes 1053696 | tf_op jit(solution)/shard_map/conv_general_dilated | solution.py:35
  67.8 0.9 fusion.82
  68.7 1.9 collective-permute-start.2
  70.7 1.0 fusion.122
  71.7 1.3 collective-permute-start.8
  73.0 5.0 %collective-permute-start.9 = (bf16[129,512]{1,0:T(8,128)(2,1)S(1)}, bf16[129,512]{1,0:T(8,128)(2,1)S(1)}, u32[]{:S(2)}, u32[]{:S(2)}) collective-permute-start(bf16[129,512]{1,0:T(8,128)(2,1)S(1)} %get-tuple-element.89), channel_id=1, source_target_pairs={{0,8},{8,16},{16,24},{24,32},{32,40},{40,48},{48,56},{56,64},{64,7... | collective-permute-start | bytes 396296 | tf_op jit(solution)/shard_map/ppermute | solution.py:10
  78.0 23.1 %collective-permute-done.2 = bf16[256,512]{1,0:T(8,128)(2,1)S(1)} collective-permute-done((bf16[256,512]{1,0:T(8,128)(2,1)}, bf16[256,512]{1,0:T(8,128)(2,1)S(1)}, u32[]{:S(2)}, u32[]{:S(2)}) %collective-permute-start.2) | collective-permute-done | bytes 262176 | tf_op jit(solution)/shard_map/ppermute | solution.py:97
  101.1 1.3 collective-permute-start.3
  102.4 9.8 %collective-permute-start.4 = (bf16[129,512]{1,0:T(8,128)(2,1)S(1)}, bf16[129,512]{1,0:T(8,128)(2,1)S(1)}, u32[]{:S(2)}, u32[]{:S(2)}) collective-permute-start(bf16[129,512]{1,0:T(8,128)(2,1)S(1)} %get-tuple-element.85), channel_id=1, source_target_pairs={{0,8},{8,16},{16,24},{24,32},{32,40},{40,48},{48,56},{56,64},{64,7... | collective-permute-start | bytes 396296 | tf_op jit(solution)/shard_map/ppermute | solution.py:10
  112.2 1.0 constant_dynamic-update-slice_fusion.3
  113.3 1.0 fusion.62
  115.4 0.9 copy-done.31
  116.2 7.1 %fusion.16 = f32[1,258,512]{2,0,1:T(1,128)S(1)} fusion(bf16[1,385,512]{2,1,0:T(8,128)(2,1)S(1)} %get-tuple-element.21, bf16[128,1,512]{2,0,1:T(8,128)(2,1)S(1)} %copy-done.31), kind=kOutput, calls=%fused_computation.48 | convolution fusion | flops 33816576 | bytes 1053696 | tf_op jit(solution)/shard_map/conv_general_dilated | solution.py:35
  126.2 0.9 copy-done.17
  128.0 7.1 %fusion.20 = f32[1,258,512]{2,0,1:T(1,128)S(1)} fusion(bf16[1,385,512]{2,1,0:T(8,128)(2,1)S(1)} %get-tuple-element.9, bf16[128,1,512]{2,0,1:T(8,128)(2,1)S(1)} %copy-done.30), kind=kOutput, calls=%fused_computation.52 | convolution fusion | flops 33816576 | bytes 1053696 | tf_op jit(solution)/shard_map/conv_general_dilated | solution.py:35
  136.8 7.0 %fusion.24 = f32[1,128,512]{2,0,1:T(1,128)S(1)} fusion(bf16[1,383,512]{2,1,0:T(8,128)(2,1)S(1)} %fusion.64, bf16[256,1,512]{2,0,1:T(8,128)(2,1)S(1)} %fusion.92), kind=kOutput, calls=%fused_computation.56 | convolution fusion | flops 33554432 | bytes 916480 | tf_op jit(solution)/shard_map/conv_general_dilated | solution.py:35
  144.1 4.0 %collective-permute-start.15 = (f32[2,2,2,2,4,512]{5,4,3,1,0,2:T(4,128)S(1)}, f32[2,2,2,2,4,512]{5,4,3,1,0,2:T(4,128)S(1)}, u32[]{:S(2)}, u32[]{:S(2)}) collective-permute-start(f32[2,2,2,2,4,512]{5,4,3,1,0,2:T(4,128)S(1)} %bitcast.182), channel_id=1, source_target_pairs={{0,8},{8,0},{16,24},{24,16},{32,40},{40,32},{48,56},{56,48},{64,72... | collective-permute-start | bytes 393224 | tf_op jit(solution)/shard_map/ppermute | solution.py:28
  148.2 6.9 %fusion.26 = f32[1,128,512]{2,0,1:T(1,128)S(1)} fusion(bf16[1,383,512]{2,1,0:T(8,128)(2,1)S(1)} %fusion.65, bf16[256,1,512]{2,0,1:T(8,128)(2,1)S(1)} %copy-done.29), kind=kOutput, calls=%fused_computation.58 | convolution fusion | flops 33554432 | bytes 916480 | tf_op jit(solution)/shard_map/conv_general_dilated | solution.py:35
  155.5 2.1 %collective-permute-start.10 = (f32[2,2,2,2,4,512]{5,4,3,1,0,2:T(4,128)S(1)}, f32[2,2,2,2,4,512]{5,4,3,1,0,2:T(4,128)S(1)}, u32[]{:S(2)}, u32[]{:S(2)}) collective-permute-start(f32[2,2,2,2,4,512]{5,4,3,1,0,2:T(4,128)S(1)} %bitcast.183), channel_id=1, source_target_pairs={{0,8},{8,0},{16,24},{24,16},{32,40},{40,32},{48,56},{56,48},{64,72... | collective-permute-start | bytes 393224 | tf_op jit(solution)/shard_map/ppermute | solution.py:28
  157.5 0.9 pad_maximum_fusion
  158.4 0.9 pad_maximum_fusion.1
  159.3 0.9 pad_maximum_fusion.2
  160.1 0.9 pad_maximum_fusion.3
  161.0 6.7 %collective-permute-start.16 = (f32[2,2,2,4,512]{4,3,2,1,0:T(4,128)S(1)}, f32[2,2,2,4,512]{4,3,2,1,0:T(4,128)S(1)}, u32[]{:S(2)}, u32[]{:S(2)}) collective-permute-start(f32[2,2,2,4,512]{4,3,2,1,0:T(4,128)S(1)} %dynamic-slice_bitcast_fusion), channel_id=1, source_target_pairs={{0,32},{8,40},{16,48},{24,56},{32,0},{40,8},{48,16},{56,24},{64,96... | collective-permute-start | bytes 196616 | tf_op jit(solution)/shard_map/ppermute | solution.py:28
  167.8 1.9 collective-permute-start.11
  170.1 6.5 %collective-permute-start.17 = (f32[2,2,4,512]{3,2,1,0:T(4,128)S(1)}, f32[2,2,4,512]{3,2,1,0:T(4,128)S(1)}, u32[]{:S(2)}, u32[]{:S(2)}) collective-permute-start(f32[2,2,4,512]{3,2,1,0:T(4,128)S(1)} %dynamic-slice_bitcast_fusion.2), channel_id=1, source_target_pairs={{0,16},{8,24},{16,0},{24,8},{32,48},{40,56},{48,32},{56,40},{64,80... | collective-permute-start | bytes 98312 | tf_op jit(solution)/shard_map/ppermute | solution.py:28
  176.7 1.9 collective-permute-start.12
  178.7 7.0 %collective-permute-start.18 = (f32[2,4,512]{2,1,0:T(4,128)S(1)}, f32[2,4,512]{2,1,0:T(4,128)S(1)}, u32[]{:S(2)}, u32[]{:S(2)}) collective-permute-start(f32[2,4,512]{2,1,0:T(4,128)S(1)} %dynamic-slice_bitcast_fusion.4), channel_id=1, source_target_pairs={{0,64},{8,72},{16,80},{24,88},{32,96},{40,104},{48,112},{56,120},{... | collective-permute-start | bytes 49160 | tf_op jit(solution)/shard_map/ppermute | solution.py:28
  185.7 4.2 %collective-permute-start.13 = (f32[2,4,512]{2,1,0:T(4,128)S(1)}, f32[2,4,512]{2,1,0:T(4,128)S(1)}, u32[]{:S(2)}, u32[]{:S(2)}) collective-permute-start(f32[2,4,512]{2,1,0:T(4,128)S(1)} %dynamic-slice_bitcast_fusion.5), channel_id=1, source_target_pairs={{0,64},{8,72},{16,80},{24,88},{32,96},{40,104},{48,112},{56,120},{... | collective-permute-start | bytes 49160 | tf_op jit(solution)/shard_map/ppermute | solution.py:28
  190.0 5.4 %collective-permute-start.19 = (f32[4,512]{1,0:T(4,128)S(1)}, f32[4,512]{1,0:T(4,128)S(1)}, u32[]{:S(2)}, u32[]{:S(2)}) collective-permute-start(f32[4,512]{1,0:T(4,128)S(1)} %dynamic-slice_bitcast_fusion.6), channel_id=1, source_target_pairs={{0,128},{8,136},{16,144},{24,152},{32,160},{40,168},{48,176},{56,1... | collective-permute-start | bytes 24584 | tf_op jit(solution)/shard_map/ppermute | solution.py:28
  195.5 4.3 %collective-permute-start.14 = (f32[4,512]{1,0:T(4,128)S(1)}, f32[4,512]{1,0:T(4,128)S(1)}, u32[]{:S(2)}, u32[]{:S(2)}) collective-permute-start(f32[4,512]{1,0:T(4,128)S(1)} %dynamic-slice_bitcast_fusion.7), channel_id=1, source_target_pairs={{0,128},{8,136},{16,144},{24,152},{32,160},{40,168},{48,176},{56,1... | collective-permute-start | bytes 24584 | tf_op jit(solution)/shard_map/ppermute | solution.py:28
  199.8 5.1 %collective-permute-done.14 = f32[4,512]{1,0:T(4,128)S(1)} collective-permute-done((f32[4,512]{1,0:T(4,128)S(1)}, f32[4,512]{1,0:T(4,128)S(1)}, u32[]{:S(2)}, u32[]{:S(2)}) %collective-permute-start.14) | collective-permute-done | bytes 8224 | tf_op jit(solution)/shard_map/ppermute | solution.py:28
  (161 shorter events, 19.2 us)
Async XLA Ops:
  0.6 2.5 %copy-start.22 = (bf16[1,256,1024]{2,1,0:T(8,128)(2,1)S(1)}, bf16[1,256,1024]{2,1,0:T(8,128)(2,1)}, u32[]{:S(2)}) copy-start(bf16[1,256,1024]{2,1,0:T(8,128)(2,1)} %param.7) | copy-start | bytes 1572868
  3.2 4.1 %copy-start.24 = (bf16[256,1024]{1,0:T(8,128)(2,1)S(1)}, bf16[256,1024]{1,0:T(8,128)(2,1)}, u32[]{:S(2)}) copy-start(bf16[256,1024]{1,0:T(8,128)(2,1)} %param.9) | copy-start | bytes 1572868
  3.9 24.6 %collective-permute-start.6 = (bf16[262,512]{1,0:T(8,128)(2,1)}, bf16[262,512]{1,0:T(8,128)(2,1)}, u32[]{:S(2)}, u32[]{:S(2)}) collective-permute-start(bf16[262,512]{1,0:T(8,128)(2,1)} %pad_maximum_fusion.13), channel_id=1, source_target_pairs={{8,0},{16,8},{24,16},{32,24},{40,32},{48,40},{56,48},{64,56},{72,6... | collective-permute-start | bytes 804872 | tf_op jit(solution)/shard_map/ppermute | solution.py:10
  5.2 2.1 %copy-start.23 = (bf16[1,256,1024]{2,1,0:T(8,128)(2,1)S(1)}, bf16[1,256,1024]{2,1,0:T(8,128)(2,1)}, u32[]{:S(2)}) copy-start(bf16[1,256,1024]{2,1,0:T(8,128)(2,1)} %param.8) | copy-start | bytes 1572868
  6.0 23.5 %collective-permute-start.1 = (bf16[262,512]{1,0:T(8,128)(2,1)}, bf16[262,512]{1,0:T(8,128)(2,1)}, u32[]{:S(2)}, u32[]{:S(2)}) collective-permute-start(bf16[262,512]{1,0:T(8,128)(2,1)} %pad_maximum_fusion.11), channel_id=1, source_target_pairs={{8,0},{16,8},{24,16},{32,24},{40,32},{48,40},{56,48},{64,56},{72,6... | collective-permute-start | bytes 804872 | tf_op jit(solution)/shard_map/ppermute | solution.py:10
  7.5 11.4 %copy-start.25 = (bf16[256,1024]{1,0:T(8,128)(2,1)S(1)}, bf16[256,1024]{1,0:T(8,128)(2,1)}, u32[]{:S(2)}) copy-start(bf16[256,1024]{1,0:T(8,128)(2,1)} %param.10) | copy-start | bytes 1572868
  8.3 17.8 %collective-permute-start = (bf16[260,512]{1,0:T(8,128)(2,1)}, bf16[260,512]{1,0:T(8,128)(2,1)}, u32[]{:S(2)}, u32[]{:S(2)}) collective-permute-start(bf16[260,512]{1,0:T(8,128)(2,1)} %pad_maximum_fusion.10), channel_id=1, source_target_pairs={{0,8},{8,16},{16,24},{24,32},{32,40},{40,48},{48,56},{56,64},{64,7... | collective-permute-start | bytes 798728 | tf_op jit(solution)/shard_map/ppermute | solution.py:10
  14.9 10.1 %collective-permute-start.5 = (bf16[260,512]{1,0:T(8,128)(2,1)}, bf16[260,512]{1,0:T(8,128)(2,1)}, u32[]{:S(2)}, u32[]{:S(2)}) collective-permute-start(bf16[260,512]{1,0:T(8,128)(2,1)} %pad_maximum_fusion.12), channel_id=1, source_target_pairs={{0,8},{8,16},{16,24},{24,32},{32,40},{40,48},{48,56},{56,64},{64,7... | collective-permute-start | bytes 798728 | tf_op jit(solution)/shard_map/ppermute | solution.py:10
  18.9 13.0 %copy-start.10 = (bf16[256,512]{1,0:T(8,128)(2,1)}, bf16[256,512]{1,0:T(8,128)(2,1)S(1)}, u32[]{:S(2)}) copy-start(bf16[256,512]{1,0:T(8,128)(2,1)S(1)} %get-tuple-element.54) | copy-start | bytes 786436
  18.9 39.8 %copy-start.8 = (bf16[256,512]{1,0:T(8,128)(2,1)}, bf16[256,512]{1,0:T(8,128)(2,1)S(1)}, u32[]{:S(2)}) copy-start(bf16[256,512]{1,0:T(8,128)(2,1)S(1)} %get-tuple-element.53) | copy-start | bytes 786436
  19.0 1.1 copy-start.28
  29.5 2.4 %copy-start.20 = (bf16[129,512]{1,0:T(8,128)(2,1)}, bf16[129,512]{1,0:T(8,128)(2,1)S(1)}, u32[]{:S(2)}) copy-start(bf16[129,512]{1,0:T(8,128)(2,1)S(1)} %get-tuple-element.78) | copy-start | bytes 396292
  30.6 28.1 %copy-start.18 = (bf16[129,512]{1,0:T(8,128)(2,1)}, bf16[129,512]{1,0:T(8,128)(2,1)S(1)}, u32[]{:S(2)}) copy-start(bf16[129,512]{1,0:T(8,128)(2,1)S(1)} %get-tuple-element.72) | copy-start | bytes 396292
  33.7 7.1 %copy-start.6 = (bf16[385,512]{1,0:T(8,128)(2,1)}, bf16[385,512]{1,0:T(8,128)(2,1)S(1)}, u32[]{:S(2)}) copy-start(bf16[385,512]{1,0:T(8,128)(2,1)S(1)} %get-tuple-element.30) | copy-start | bytes 1182724
  33.7 7.1 %copy-start.14 = (bf16[385,512]{1,0:T(8,128)(2,1)}, bf16[385,512]{1,0:T(8,128)(2,1)S(1)}, u32[]{:S(2)}) copy-start(bf16[385,512]{1,0:T(8,128)(2,1)S(1)} %get-tuple-element.28) | copy-start | bytes 1182724
  41.0 17.4 %copy-start.26 = (bf16[256,512]{1,0:T(8,128)(2,1)S(1)}, bf16[256,512]{1,0:T(8,128)(2,1)}, u32[]{:S(2)}) copy-start(bf16[256,512]{1,0:T(8,128)(2,1)} %get-tuple-element.43) | copy-start | bytes 786436
  41.9 28.7 %collective-permute-start.7 = (bf16[256,512]{1,0:T(8,128)(2,1)}, bf16[256,512]{1,0:T(8,128)(2,1)}, u32[]{:S(2)}, u32[]{:S(2)}) collective-permute-start(bf16[256,512]{1,0:T(8,128)(2,1)} %fusion.84), channel_id=1, source_target_pairs={{0,256},{256,0},{1,257},{257,1},{2,258},{258,2},{3,259},{259,3},{4... | collective-permute-start | bytes 786440 | tf_op jit(solution)/shard_map/ppermute | solution.py:97
  60.5 7.1 %copy-start.4 = (bf16[385,512]{1,0:T(8,128)(2,1)}, bf16[385,512]{1,0:T(8,128)(2,1)S(1)}, u32[]{:S(2)}) copy-start(bf16[385,512]{1,0:T(8,128)(2,1)S(1)} %get-tuple-element.18) | copy-start | bytes 1182724
  60.5 7.1 %copy-start.16 = (bf16[385,512]{1,0:T(8,128)(2,1)}, bf16[385,512]{1,0:T(8,128)(2,1)S(1)}, u32[]{:S(2)}) copy-start(bf16[385,512]{1,0:T(8,128)(2,1)S(1)} %get-tuple-element.16) | copy-start | bytes 1182724
  68.7 32.4 %collective-permute-start.2 = (bf16[256,512]{1,0:T(8,128)(2,1)}, bf16[256,512]{1,0:T(8,128)(2,1)S(1)}, u32[]{:S(2)}, u32[]{:S(2)}) collective-permute-start(bf16[256,512]{1,0:T(8,128)(2,1)} %fusion.82), channel_id=1, source_target_pairs={{0,256},{256,0},{1,257},{257,1},{2,258},{258,2},{3,259},{259,3},{4... | collective-permute-start | bytes 786440 | tf_op jit(solution)/shard_map/ppermute | solution.py:97
  71.7 41.6 %collective-permute-start.8 = (bf16[129,512]{1,0:T(8,128)(2,1)S(1)}, bf16[129,512]{1,0:T(8,128)(2,1)S(1)}, u32[]{:S(2)}, u32[]{:S(2)}) collective-permute-start(bf16[129,512]{1,0:T(8,128)(2,1)S(1)} %get-tuple-element.90), channel_id=1, source_target_pairs={{8,0},{16,8},{24,16},{32,24},{40,32},{48,40},{56,48},{64,56},{72,6... | collective-permute-start | bytes 396296 | tf_op jit(solution)/shard_map/ppermute | solution.py:10
  73.0 40.3 %collective-permute-start.9 = (bf16[129,512]{1,0:T(8,128)(2,1)S(1)}, bf16[129,512]{1,0:T(8,128)(2,1)S(1)}, u32[]{:S(2)}, u32[]{:S(2)}) collective-permute-start(bf16[129,512]{1,0:T(8,128)(2,1)S(1)} %get-tuple-element.89), channel_id=1, source_target_pairs={{0,8},{8,16},{16,24},{24,32},{32,40},{40,48},{48,56},{56,64},{64,7... | collective-permute-start | bytes 396296 | tf_op jit(solution)/shard_map/ppermute | solution.py:10
  101.1 23.8 %collective-permute-start.3 = (bf16[129,512]{1,0:T(8,128)(2,1)S(1)}, bf16[129,512]{1,0:T(8,128)(2,1)S(1)}, u32[]{:S(2)}, u32[]{:S(2)}) collective-permute-start(bf16[129,512]{1,0:T(8,128)(2,1)S(1)} %get-tuple-element.86), channel_id=1, source_target_pairs={{8,0},{16,8},{24,16},{32,24},{40,32},{48,40},{56,48},{64,56},{72,6... | collective-permute-start | bytes 396296 | tf_op jit(solution)/shard_map/ppermute | solution.py:10
  102.4 22.5 %collective-permute-start.4 = (bf16[129,512]{1,0:T(8,128)(2,1)S(1)}, bf16[129,512]{1,0:T(8,128)(2,1)S(1)}, u32[]{:S(2)}, u32[]{:S(2)}) collective-permute-start(bf16[129,512]{1,0:T(8,128)(2,1)S(1)} %get-tuple-element.85), channel_id=1, source_target_pairs={{0,8},{8,16},{16,24},{24,32},{32,40},{40,48},{48,56},{56,64},{64,7... | collective-permute-start | bytes 396296 | tf_op jit(solution)/shard_map/ppermute | solution.py:10
  114.3 1.0 copy-start.7
  116.2 7.1 %copy-start.3 = (f32[258,512]{1,0:T(8,128)S(1)}, f32[258,512]{1,0:T(8,128)}, u32[]{:S(2)}) copy-start(f32[258,512]{1,0:T(8,128)} %copy-done.2) | copy-start | bytes 1585156
  116.2 7.1 %copy-start.11 = (bf16[256,512]{1,0:T(8,128)(2,1)S(1)}, bf16[256,512]{1,0:T(8,128)(2,1)}, u32[]{:S(2)}) copy-start(bf16[256,512]{1,0:T(8,128)(2,1)} %copy-done.10) | copy-start | bytes 786436
  116.2 7.1 %copy-start.13 = (f32[385,512]{1,0:T(8,128)S(1)}, f32[385,512]{1,0:T(8,128)}, u32[]{:S(2)}) copy-start(f32[385,512]{1,0:T(8,128)} %get-tuple-element.31) | copy-start | bytes 2365444
  116.2 7.1 %copy-start.21 = (bf16[129,512]{1,0:T(8,128)(2,1)S(1)}, bf16[129,512]{1,0:T(8,128)(2,1)}, u32[]{:S(2)}) copy-start(bf16[129,512]{1,0:T(8,128)(2,1)} %copy-done.20) | copy-start | bytes 396292
  123.9 1.0 copy-start.15
  125.1 1.0 copy-start.5
  126.1 1.0 copy-start.17
  128.0 7.1 %copy-start.1 = (f32[258,512]{1,0:T(8,128)S(1)}, f32[258,512]{1,0:T(8,128)}, u32[]{:S(2)}) copy-start(f32[258,512]{1,0:T(8,128)} %copy-done) | copy-start | bytes 1585156
  128.0 7.1 %copy-start.9 = (bf16[256,512]{1,0:T(8,128)(2,1)S(1)}, bf16[256,512]{1,0:T(8,128)(2,1)}, u32[]{:S(2)}) copy-start(bf16[256,512]{1,0:T(8,128)(2,1)} %copy-done.8) | copy-start | bytes 786436
  128.0 7.1 %copy-start.12 = (f32[385,512]{1,0:T(8,128)S(1)}, f32[385,512]{1,0:T(8,128)}, u32[]{:S(2)}) copy-start(f32[385,512]{1,0:T(8,128)} %get-tuple-element.19) | copy-start | bytes 2365444
  128.0 7.1 %copy-start.19 = (bf16[129,512]{1,0:T(8,128)(2,1)S(1)}, bf16[129,512]{1,0:T(8,128)(2,1)}, u32[]{:S(2)}) copy-start(bf16[129,512]{1,0:T(8,128)(2,1)} %copy-done.18) | copy-start | bytes 396292
  144.1 4.1 %copy-start.29 = (bf16[256,1,512]{2,0,1:T(8,128)(2,1)S(1)}, bf16[256,1,512]{2,0,1:T(8,128)(2,1)}, u32[]{:S(2)}) copy-start(bf16[256,1,512]{2,0,1:T(8,128)(2,1)} %fusion.93) | copy-start | bytes 786436
  144.1 16.9 %collective-permute-start.15 = (f32[2,2,2,2,4,512]{5,4,3,1,0,2:T(4,128)S(1)}, f32[2,2,2,2,4,512]{5,4,3,1,0,2:T(4,128)S(1)}, u32[]{:S(2)}, u32[]{:S(2)}) collective-permute-start(f32[2,2,2,2,4,512]{5,4,3,1,0,2:T(4,128)S(1)} %bitcast.182), channel_id=1, source_target_pairs={{0,8},{8,0},{16,24},{24,16},{32,40},{40,32},{48,56},{56,48},{64,72... | collective-permute-start | bytes 393224 | tf_op jit(solution)/shard_map/ppermute | solution.py:28
  155.4 2.1 %copy-start.27 = (bf16[1,256,512]{2,1,0:T(8,128)(2,1)S(1)}, bf16[1,256,512]{2,1,0:T(8,128)(2,1)}, u32[]{:S(2)}) copy-start(bf16[1,256,512]{2,1,0:T(8,128)(2,1)} %fusion.85) | copy-start | bytes 786436
  155.5 12.3 %collective-permute-start.10 = (f32[2,2,2,2,4,512]{5,4,3,1,0,2:T(4,128)S(1)}, f32[2,2,2,2,4,512]{5,4,3,1,0,2:T(4,128)S(1)}, u32[]{:S(2)}, u32[]{:S(2)}) collective-permute-start(f32[2,2,2,2,4,512]{5,4,3,1,0,2:T(4,128)S(1)} %bitcast.183), channel_id=1, source_target_pairs={{0,8},{8,0},{16,24},{24,16},{32,40},{40,32},{48,56},{56,48},{64,72... | collective-permute-start | bytes 393224 | tf_op jit(solution)/shard_map/ppermute | solution.py:28
  161.0 9.1 %collective-permute-start.16 = (f32[2,2,2,4,512]{4,3,2,1,0:T(4,128)S(1)}, f32[2,2,2,4,512]{4,3,2,1,0:T(4,128)S(1)}, u32[]{:S(2)}, u32[]{:S(2)}) collective-permute-start(f32[2,2,2,4,512]{4,3,2,1,0:T(4,128)S(1)} %dynamic-slice_bitcast_fusion), channel_id=1, source_target_pairs={{0,32},{8,40},{16,48},{24,56},{32,0},{40,8},{48,16},{56,24},{64,96... | collective-permute-start | bytes 196616 | tf_op jit(solution)/shard_map/ppermute | solution.py:28
  167.8 8.8 %collective-permute-start.11 = (f32[2,2,2,4,512]{4,3,2,1,0:T(4,128)S(1)}, f32[2,2,2,4,512]{4,3,2,1,0:T(4,128)S(1)}, u32[]{:S(2)}, u32[]{:S(2)}) collective-permute-start(f32[2,2,2,4,512]{4,3,2,1,0:T(4,128)S(1)} %dynamic-slice_bitcast_fusion.1), channel_id=1, source_target_pairs={{0,32},{8,40},{16,48},{24,56},{32,0},{40,8},{48,16},{56,24},{64,96... | collective-permute-start | bytes 196616 | tf_op jit(solution)/shard_map/ppermute | solution.py:28
  170.1 8.5 %collective-permute-start.17 = (f32[2,2,4,512]{3,2,1,0:T(4,128)S(1)}, f32[2,2,4,512]{3,2,1,0:T(4,128)S(1)}, u32[]{:S(2)}, u32[]{:S(2)}) collective-permute-start(f32[2,2,4,512]{3,2,1,0:T(4,128)S(1)} %dynamic-slice_bitcast_fusion.2), channel_id=1, source_target_pairs={{0,16},{8,24},{16,0},{24,8},{32,48},{40,56},{48,32},{56,40},{64,80... | collective-permute-start | bytes 98312 | tf_op jit(solution)/shard_map/ppermute | solution.py:28
  176.7 8.9 %collective-permute-start.12 = (f32[2,2,4,512]{3,2,1,0:T(4,128)S(1)}, f32[2,2,4,512]{3,2,1,0:T(4,128)S(1)}, u32[]{:S(2)}, u32[]{:S(2)}) collective-permute-start(f32[2,2,4,512]{3,2,1,0:T(4,128)S(1)} %dynamic-slice_bitcast_fusion.3), channel_id=1, source_target_pairs={{0,16},{8,24},{16,0},{24,8},{32,48},{40,56},{48,32},{56,40},{64,80... | collective-permute-start | bytes 98312 | tf_op jit(solution)/shard_map/ppermute | solution.py:28
  178.7 11.2 %collective-permute-start.18 = (f32[2,4,512]{2,1,0:T(4,128)S(1)}, f32[2,4,512]{2,1,0:T(4,128)S(1)}, u32[]{:S(2)}, u32[]{:S(2)}) collective-permute-start(f32[2,4,512]{2,1,0:T(4,128)S(1)} %dynamic-slice_bitcast_fusion.4), channel_id=1, source_target_pairs={{0,64},{8,72},{16,80},{24,88},{32,96},{40,104},{48,112},{56,120},{... | collective-permute-start | bytes 49160 | tf_op jit(solution)/shard_map/ppermute | solution.py:28
  185.7 9.7 %collective-permute-start.13 = (f32[2,4,512]{2,1,0:T(4,128)S(1)}, f32[2,4,512]{2,1,0:T(4,128)S(1)}, u32[]{:S(2)}, u32[]{:S(2)}) collective-permute-start(f32[2,4,512]{2,1,0:T(4,128)S(1)} %dynamic-slice_bitcast_fusion.5), channel_id=1, source_target_pairs={{0,64},{8,72},{16,80},{24,88},{32,96},{40,104},{48,112},{56,120},{... | collective-permute-start | bytes 49160 | tf_op jit(solution)/shard_map/ppermute | solution.py:28
  190.0 9.8 %collective-permute-start.19 = (f32[4,512]{1,0:T(4,128)S(1)}, f32[4,512]{1,0:T(4,128)S(1)}, u32[]{:S(2)}, u32[]{:S(2)}) collective-permute-start(f32[4,512]{1,0:T(4,128)S(1)} %dynamic-slice_bitcast_fusion.6), channel_id=1, source_target_pairs={{0,128},{8,136},{16,144},{24,152},{32,160},{40,168},{48,176},{56,1... | collective-permute-start | bytes 24584 | tf_op jit(solution)/shard_map/ppermute | solution.py:28
  195.5 9.5 %collective-permute-start.14 = (f32[4,512]{1,0:T(4,128)S(1)}, f32[4,512]{1,0:T(4,128)S(1)}, u32[]{:S(2)}, u32[]{:S(2)}) collective-permute-start(f32[4,512]{1,0:T(4,128)S(1)} %dynamic-slice_bitcast_fusion.7), channel_id=1, source_target_pairs={{0,128},{8,136},{16,144},{24,152},{32,160},{40,168},{48,176},{56,1... | collective-permute-start | bytes 24584 | tf_op jit(solution)/shard_map/ppermute | solution.py:28
  (6 other events, 5.2 us)

commit v4 on v2

--- a/solution.py
+++ b/solution.py
@@ -29,6 +29,16 @@
         held = keep + got
         remaining.pop(at)
     return held.reshape((rows,) + part.shape[1:])
+
+
+def exchange_scatter(part, axis):
+    peers = lax.axis_size(axis)
+    if part.shape[0] % peers:
+        return lax.psum_scatter(part, axis, scatter_dimension=0, tiled=True)
+    rows = part.shape[0] // peers
+    pieces = part.reshape((peers, rows) + part.shape[1:])
+    got = lax.all_to_all(pieces, axis, 0, 0)
+    return jnp.sum(got, axis=0)
 
 
 def depthwise(source, kernel):
@@ -122,7 +132,7 @@
     grad_k = bwd_short(gks, w_k).astype(jnp.bfloat16)
     grad_input = bwd_short(gvs, w_v).astype(jnp.bfloat16)
     taps_part = depthwise(u[: rows + extent - 1], gz[:rows])[::-1]
-    tap_sum = halving_scatter(taps_part, "ctx")
+    tap_sum = exchange_scatter(taps_part, "ctx")
     return (output[None], grad_q[None], grad_k[None], grad_input[None], tap_sum[None])
 
 

time: 207 us -> 189 us (0.913)
  starting transfers between devices: 88.9 us -> 73.9 us
  local copies, waits for them, and re-layouts: 18.9 us -> 13.5 us
  waiting for transfers between devices: 36.2 us -> 39.5 us
    ppermute x5 -> x0, starting transfers between devices: 61.9 us -> none  [halving_scatter(): got = lax.ppermute(give, axis, [(i, i ^ 1 << bit) for i in range(peers)])]
    all_to_all x0 -> x1, starting transfers between devices: none -> 47.6 us  [exchange_scatter(): got = lax.all_to_all(pieces, axis, 0, 0)]
    all_to_all x0 -> x1, waiting for transfers between devices: none -> 7.14 us  [exchange_scatter(): got = lax.all_to_all(pieces, axis, 0, 0)]
    ppermute x5 -> x0, waiting for transfers between devices: 6.32 us -> none  [halving_scatter(): got = lax.ppermute(give, axis, [(i, i ^ 1 << bit) for i in range(peers)])]
    unnamed x50 -> x38, local copies, waits for them, and re-layouts: 5.72 us -> 3.2 us
    ppermute x4, waiting for transfers between devices: 14.8 us -> 17.2 us  [shifted(): return lax.ppermute(value, axis, pairs)]
  transfers between devices with their start and end apart: 10 -> 6, of which waited for: 9 -> 6; matrix products, arithmetic and copies ran while one was open for 12% -> 12% of each run, Pallas kernels for 0% -> 0%
where the time goes in v4:
time: 189 us
  starting transfers between devices  73.9 us (39%)
  matrix products  43.9 us (23%)
  waiting for transfers between devices  39.5 us (21%)
  other arithmetic  16.6 us (9%)
  local copies, waits for them, and re-layouts  13.5 us (7%)
    all_to_all x1, starting transfers between devices, exchange_scatter(): got = lax.all_to_all(pieces, axis, 0, 0)  47.6 us
    conv_general_dilated x3, matrix products, depthwise(): lax.conv_general_dilated(source[None], kernel[:, None, :], (1,), 'VALID',...  43.9 us
    ppermute x4, waiting for transfers between devices, shifted(): return lax.ppermute(value, axis, pairs)  17.2 us
    ppermute x1, starting transfers between devices, body(): lax.ppermute(jnp.where(first, out_first, gin_last), 'section', [(0, 1), (...  15.7 us
    ppermute x1, waiting for transfers between devices, body(): lax.ppermute(jnp.where(first, out_first, gin_last), 'section', [(0, 1), (...  15.1 us
    ppermute x4, starting transfers between devices, shifted(): return lax.ppermute(value, axis, pairs)  10.6 us
    all_to_all x1, waiting for transfers between devices, exchange_scatter(): got = lax.all_to_all(pieces, axis, 0, 0)  7.14 us
    broadcast_in_dim x3, other arithmetic, depthwise(): source[None]  5.08 us
  transfers between devices with their start and end apart: 6, of which 6 were waited for; matrix products, arithmetic and copies ran while one was open for 12% of the time, Pallas kernels for 0%

profile of v4, /device:TPU:6, one launch (start us, length us, event | category | flops | bytes accessed | tf_op | source)
XLA Modules:
  0.0 188.6 jit_solution(14716757240195351866)
XLA Ops:
  0.6 0.0 slice-start.1
  0.7 1.1 slice.250
  1.8 1.0 slice_bitcast_fusion.1
  2.8 0.7 slice_bitcast_fusion.3
  3.6 1.0 pad_maximum_fusion.3
  4.6 3.5 %collective-permute-start = (bf16[260,1024]{1,0:T(8,128)(2,1)}, bf16[260,1024]{1,0:T(8,128)(2,1)S(1)}, u32[]{:S(2)}, u32[]{:S(2)}) collective-permute-start(bf16[260,1024]{1,0:T(8,128)(2,1)} %pad_maximum_fusion.3), channel_id=1, source_target_pairs={{0,8},{8,16},{16,24},{24,32},{32,40},{40,48},{48,56},{56,64},{64,7... | collective-permute-start | bytes 1597448 | tf_op jit(solution)/shard_map/ppermute | solution.py:10
  8.1 0.9 pad_maximum_fusion.4
  9.1 1.3 collective-permute-start.1
  10.4 0.3 rev.6
  10.7 0.7 select_bitcast_fusion.2
  11.5 8.4 %collective-permute-done = bf16[260,1024]{1,0:T(8,128)(2,1)S(1)} collective-permute-done((bf16[260,1024]{1,0:T(8,128)(2,1)}, bf16[260,1024]{1,0:T(8,128)(2,1)S(1)}, u32[]{:S(2)}, u32[]{:S(2)}) %collective-permute-start) | collective-permute-done | bytes 532512 | tf_op jit(solution)/shard_map/ppermute | solution.py:10
  19.9 0.1 fusion.54
  20.0 4.9 %collective-permute-done.1 = bf16[262,1024]{1,0:T(8,128)(2,1)S(1)} collective-permute-done((bf16[262,1024]{1,0:T(8,128)(2,1)}, bf16[262,1024]{1,0:T(8,128)(2,1)S(1)}, u32[]{:S(2)}, u32[]{:S(2)}) %collective-permute-start.1) | collective-permute-done | bytes 536608 | tf_op jit(solution)/shard_map/ppermute | solution.py:10
  24.9 0.1 fusion.56
  25.0 0.2 maximum_convert_fusion
  25.2 0.4 maximum_convert_fusion.1
  25.7 0.6 copy-done.10
  26.3 2.7 %select_bitcast_fusion.1 = (bf16[1,385,1024]{2,1,0:T(8,128)(2,1)S(1)}, bf16[385,1024]{1,0:T(8,128)(2,1)S(1)}, f32[385,1024]{1,0:T(8,128)S(1)}, bf16[385,1024]{1,...) fusion(pred[]{:T(512)S(6)} %eq.3, bf16[129,1024]{1,0:T(8,128)(2,1)S(1)} %get-tuple-element.28, ...), kind=kLoop, calls=%fused_computation.77 | loop fusion | flops 9461760 | bytes 22114304 | tf_op jit(solution)/shard_map/broadcast_in_dim | solution.py:46
  29.0 14.5 %fusion.10 = f32[1,258,1024]{2,0,1:T(1,128)S(1)} fusion(bf16[1,385,1024]{2,1,0:T(8,128)(2,1)S(1)} %get-tuple-element.13, bf16[128,1,1024]{2,0,1:T(8,128)(2,1)S(1)} %get-tuple-element.30), kind=kOutput, calls=%fused_computation.26 | convolution fusion | flops 67633152 | bytes 2107392 | tf_op jit(solution)/shard_map/conv_general_dilated | solution.py:45
  43.4 0.6 fusion.37
  44.0 0.4 fusion.41
  44.4 0.6 copy-done
  45.0 15.7 %collective-permute-start.2 = (bf16[256,1024]{1,0:T(8,128)(2,1)S(1)}, bf16[256,1024]{1,0:T(8,128)(2,1)S(1)}, u32[]{:S(2)}, u32[]{:S(2)}) collective-permute-start(bf16[256,1024]{1,0:T(8,128)(2,1)S(1)} %fusion.41), channel_id=1, source_target_pairs={{0,256},{256,0},{1,257},{257,1},{2,258},{258,2},{3,259},{259,3},{4... | collective-permute-start | bytes 1572872 | tf_op jit(solution)/shard_map/ppermute | solution.py:107
  60.7 15.1 %collective-permute-done.2 = bf16[256,1024]{1,0:T(8,128)(2,1)S(1)} collective-permute-done((bf16[256,1024]{1,0:T(8,128)(2,1)S(1)}, bf16[256,1024]{1,0:T(8,128)(2,1)S(1)}, u32[]{:S(2)}, u32[]{:S(2)}) %collective-permute-start.2) | collective-permute-done | bytes 524320 | tf_op jit(solution)/shard_map/ppermute | solution.py:107
  75.9 0.1 fusion.57
  75.9 1.3 collective-permute-start.3
  77.2 4.6 %collective-permute-start.4 = (bf16[129,1024]{1,0:T(8,128)(2,1)S(1)}, bf16[129,1024]{1,0:T(8,128)(2,1)S(1)}, u32[]{:S(2)}, u32[]{:S(2)}) collective-permute-start(bf16[129,1024]{1,0:T(8,128)(2,1)S(1)} %get-tuple-element.31), channel_id=1, source_target_pairs={{0,8},{8,16},{16,24},{24,32},{32,40},{40,48},{48,56},{56,64},{64,7... | collective-permute-start | bytes 792584 | tf_op jit(solution)/shard_map/ppermute | solution.py:10
  81.9 2.5 %collective-permute-done.3 = bf16[129,1024]{1,0:T(8,128)(2,1)S(1)} collective-permute-done((bf16[129,1024]{1,0:T(8,128)(2,1)S(1)}, bf16[129,1024]{1,0:T(8,128)(2,1)S(1)}, u32[]{:S(2)}, u32[]{:S(2)}) %collective-permute-start.3) | collective-permute-done | bytes 264224 | tf_op jit(solution)/shard_map/ppermute | solution.py:10
  84.4 1.4 collective-permute-done.4
  85.8 0.2 fusion.31
  86.0 2.3 %select_bitcast_fusion = (bf16[1,385,1024]{2,1,0:T(8,128)(2,1)}, bf16[385,1024]{1,0:T(8,128)(2,1)S(1)}, f32[385,1024]{1,0:T(8,128)}, bf16[385,1024]{1,0:T(8,128)(2,1)S(1)}) fusion(pred[]{:T(512)S(6)} %eq.3, f32[385,1024]{1,0:T(8,128)S(1)} %get-tuple-element.18, f32[387,1024]{1,0:T(8,128)S(1)} %fusion.31, f32[1024]{0:T(1024)S(1)} %bitcast.71, ...), kind=kLoop, calls=%fused_computation.76 | loop fusion | flops 4336640 | bytes 12627969 | tf_op jit(solution)/shard_map/broadcast_in_dim | solution.py:46
  88.3 0.1 fusion.46
  88.4 0.1 fusion.32
  88.5 0.7 copy-done.2
  89.2 0.3 copy-done.6
  89.5 13.9 %fusion.12 = f32[1,128,1024]{2,0,1:T(1,128)S(1)} fusion(bf16[1,383,1024]{2,1,0:T(8,128)(2,1)S(1)} %fusion.32, bf16[256,1,1024]{2,0,1:T(8,128)(2,1)S(1)} %fusion.46), kind=kOutput, calls=%fused_computation.28 | convolution fusion | flops 67108864 | bytes 1832960 | tf_op jit(solution)/shard_map/conv_general_dilated | solution.py:45
  103.4 0.9 copy.46
  104.3 4.7 %rev.7 = f32[128,1024]{1,0:T(8,128)} reverse(f32[128,1024]{1,0:T(8,128)} %bitcast.61), dimensions={0} | reverse | bytes 1048576 | tf_op jit(solution)/shard_map/rev | solution.py:134
  109.0 2.0 %reshape.41 = f32[32,4,1024]{2,1,0:T(4,128)} reshape(f32[128,1024]{1,0:T(8,128)} %rev.7) | data formatting | bytes 1048576 | tf_op jit(solution)/shard_map/reshape | solution.py:39
  111.1 47.6 %all-to-all-start = ((f32[32,4,1024]{2,1,0:T(4,128)}), f32[32,4,1024]{2,1,0:T(4,128)}, u32[]{:S(2)}, u32[]{:S(2)}) async-start(f32[32,4,1024]{2,1,0:T(4,128)} %reshape.41), calls=%async_computation | async-start | bytes 1048576 | tf_op jit(solution)/shard_map/all_to_all | solution.py:40
  158.7 15.6 %fusion.8 = f32[1,258,1024]{2,0,1:T(1,128)S(1)} fusion(bf16[1,385,1024]{2,1,0:T(8,128)(2,1)} %get-tuple-element.7, bf16[128,1,1024]{2,0,1:T(8,128)(2,1)} %get-tuple-element.29), kind=kOutput, calls=%fused_computation.24 | convolution fusion | flops 67633152 | bytes 2107392 | tf_op jit(solution)/shard_map/conv_general_dilated | solution.py:45
  174.4 1.1 fusion.39
  175.4 1.1 fusion.43
  176.6 1.1 fusion.44
  177.7 1.1 fusion.45
  178.8 0.9 fusion.42
  179.7 7.1 %all-to-all-done = f32[32,4,1024]{2,1,0:T(4,128)} async-done(((f32[32,4,1024]{2,1,0:T(4,128)}), f32[32,4,1024]{2,1,0:T(4,128)}, u32[]{:S(2)}, u32[]{:S(2)}) %all-to-all-start) | async-done | bytes 524320 | tf_op jit(solution)/shard_map/all_to_all | solution.py:40
  186.9 1.7 reduce_sum.9
  (42 shorter events, 0.2 us)
Async XLA Ops:
  0.6 7.5 %slice-start.1 = ((bf16[256,1024]{1,0:T(8,128)(2,1)}), bf16[2,1024]{1,0:T(2,128)(2,1)S(1)}, s32[]{:S(2)}) async-start(bf16[256,1024]{1,0:T(8,128)(2,1)} %param.9), calls=%async_computation.2 | async-start | bytes 8192 | tf_op jit(solution)/shard_map/slice | solution.py:87
  0.6 7.5 %copy-start.13 = (bf16[1,256,1024]{2,1,0:T(8,128)(2,1)S(1)}, bf16[1,256,1024]{2,1,0:T(8,128)(2,1)}, u32[]{:S(2)}) copy-start(bf16[1,256,1024]{2,1,0:T(8,128)(2,1)} %param.8) | copy-start | bytes 1572868
  0.7 7.4 %copy-start.14 = (bf16[1,256,1024]{2,1,0:T(8,128)(2,1)S(1)}, bf16[1,256,1024]{2,1,0:T(8,128)(2,1)}, u32[]{:S(2)}) copy-start(bf16[1,256,1024]{2,1,0:T(8,128)(2,1)} %param.7) | copy-start | bytes 1572868
  0.7 7.5 %slice-start = ((bf16[256,1024]{1,0:T(8,128)(2,1)}), bf16[129,1024]{1,0:T(8,128)(2,1)S(1)}, s32[]{:S(2)}) async-start(bf16[256,1024]{1,0:T(8,128)(2,1)} %param.10), calls=%async_computation.1 | async-start | bytes 557056 | tf_op jit(solution)/shard_map/slice | solution.py:87
  3.6 6.8 %copy-start.16 = (f32[1,3,3,1024]{3,0,2,1:T(1,128)S(1)}, f32[1,3,3,1024]{3,0,2,1:T(1,128)}, u32[]{:S(2)}) copy-start(f32[1,3,3,1024]{3,0,2,1:T(1,128)} %param.11) | copy-start | bytes 110596
  3.6 6.8 %copy-start.15 = (bf16[1,128,1024]{2,1,0:T(8,128)(2,1)S(1)}, bf16[1,128,1024]{2,1,0:T(8,128)(2,1)}, u32[]{:S(2)}) copy-start(bf16[1,128,1024]{2,1,0:T(8,128)(2,1)} %param.12) | copy-start | bytes 786436
  4.6 15.3 %collective-permute-start = (bf16[260,1024]{1,0:T(8,128)(2,1)}, bf16[260,1024]{1,0:T(8,128)(2,1)S(1)}, u32[]{:S(2)}, u32[]{:S(2)}) collective-permute-start(bf16[260,1024]{1,0:T(8,128)(2,1)} %pad_maximum_fusion.3), channel_id=1, source_target_pairs={{0,8},{8,16},{16,24},{24,32},{32,40},{40,48},{48,56},{56,64},{64,7... | collective-permute-start | bytes 1597448 | tf_op jit(solution)/shard_map/ppermute | solution.py:10
  9.1 15.8 %collective-permute-start.1 = (bf16[262,1024]{1,0:T(8,128)(2,1)}, bf16[262,1024]{1,0:T(8,128)(2,1)S(1)}, u32[]{:S(2)}, u32[]{:S(2)}) collective-permute-start(bf16[262,1024]{1,0:T(8,128)(2,1)} %pad_maximum_fusion.4), channel_id=1, source_target_pairs={{8,0},{16,8},{24,16},{32,24},{40,32},{48,40},{56,48},{64,56},{72,6... | collective-permute-start | bytes 1609736 | tf_op jit(solution)/shard_map/ppermute | solution.py:10
  20.0 5.2 %copy-start.12 = (bf16[256,1024]{1,0:T(8,128)(2,1)S(1)}, bf16[256,1024]{1,0:T(8,128)(2,1)}, u32[]{:S(2)}) copy-start(bf16[256,1024]{1,0:T(8,128)(2,1)} %param.9) | copy-start | bytes 1572868
  25.2 1.0 copy-start.10
  29.0 14.5 %copy-start.17 = (f32[1,1024]{1,0:T(1,128)S(1)}, f32[1,1024]{1,0:T(1,128)}, u32[]{:S(2)}) copy-start(f32[1,1024]{1,0:T(1,128)} %param.13) | copy-start | bytes 12292
  44.0 1.0 copy-start
  45.0 30.9 %collective-permute-start.2 = (bf16[256,1024]{1,0:T(8,128)(2,1)S(1)}, bf16[256,1024]{1,0:T(8,128)(2,1)S(1)}, u32[]{:S(2)}, u32[]{:S(2)}) collective-permute-start(bf16[256,1024]{1,0:T(8,128)(2,1)S(1)} %fusion.41), channel_id=1, source_target_pairs={{0,256},{256,0},{1,257},{257,1},{2,258},{258,2},{3,259},{259,3},{4... | collective-permute-start | bytes 1572872 | tf_op jit(solution)/shard_map/ppermute | solution.py:107
  75.9 8.4 %collective-permute-start.3 = (bf16[129,1024]{1,0:T(8,128)(2,1)S(1)}, bf16[129,1024]{1,0:T(8,128)(2,1)S(1)}, u32[]{:S(2)}, u32[]{:S(2)}) collective-permute-start(bf16[129,1024]{1,0:T(8,128)(2,1)S(1)} %get-tuple-element.32), channel_id=1, source_target_pairs={{8,0},{16,8},{24,16},{32,24},{40,32},{48,40},{56,48},{64,56},{72,6... | collective-permute-start | bytes 792584 | tf_op jit(solution)/shard_map/ppermute | solution.py:10
  77.2 8.6 %collective-permute-start.4 = (bf16[129,1024]{1,0:T(8,128)(2,1)S(1)}, bf16[129,1024]{1,0:T(8,128)(2,1)S(1)}, u32[]{:S(2)}, u32[]{:S(2)}) collective-permute-start(bf16[129,1024]{1,0:T(8,128)(2,1)S(1)} %get-tuple-element.31), channel_id=1, source_target_pairs={{0,8},{8,16},{16,24},{24,32},{32,40},{40,48},{48,56},{56,64},{64,7... | collective-permute-start | bytes 792584 | tf_op jit(solution)/shard_map/ppermute | solution.py:10
  84.4 3.9 %copy-start.8 = (bf16[385,1024]{1,0:T(8,128)(2,1)}, bf16[385,1024]{1,0:T(8,128)(2,1)S(1)}, u32[]{:S(2)}) copy-start(bf16[385,1024]{1,0:T(8,128)(2,1)S(1)} %constant_dynamic-update-slice_fusion) | copy-start | bytes 2365444
  88.3 0.9 copy-start.2
  88.3 1.2 copy-start.6
  111.1 75.8 %all-to-all-start = ((f32[32,4,1024]{2,1,0:T(4,128)}), f32[32,4,1024]{2,1,0:T(4,128)}, u32[]{:S(2)}, u32[]{:S(2)}) async-start(f32[32,4,1024]{2,1,0:T(4,128)} %reshape.41), calls=%async_computation | async-start | bytes 1048576 | tf_op jit(solution)/shard_map/all_to_all | solution.py:40
  158.6 15.7 %copy-start.1 = (f32[258,1024]{1,0:T(8,128)S(1)}, f32[258,1024]{1,0:T(8,128)}, u32[]{:S(2)}) copy-start(f32[258,1024]{1,0:T(8,128)} %copy-done) | copy-start | bytes 3170308
  158.6 15.7 %copy-start.3 = (bf16[385,1024]{1,0:T(8,128)(2,1)S(1)}, bf16[385,1024]{1,0:T(8,128)(2,1)}, u32[]{:S(2)}) copy-start(bf16[385,1024]{1,0:T(8,128)(2,1)} %copy-done.2) | copy-start | bytes 2365444
  158.7 15.7 %copy-start.4 = (f32[385,1024]{1,0:T(8,128)S(1)}, f32[385,1024]{1,0:T(8,128)}, u32[]{:S(2)}) copy-start(f32[385,1024]{1,0:T(8,128)} %get-tuple-element.9) | copy-start | bytes 4730884
  158.7 15.7 %copy-start.5 = (f32[385,1024]{1,0:T(8,128)S(1)}, f32[385,1024]{1,0:T(8,128)}, u32[]{:S(2)}) copy-start(f32[385,1024]{1,0:T(8,128)} %get-tuple-element.17) | copy-start | bytes 4730884
  158.7 15.7 %copy-start.7 = (bf16[385,1024]{1,0:T(8,128)(2,1)S(1)}, bf16[385,1024]{1,0:T(8,128)(2,1)}, u32[]{:S(2)}) copy-start(bf16[385,1024]{1,0:T(8,128)(2,1)} %copy-done.6) | copy-start | bytes 2365444
  158.7 15.7 %copy-start.9 = (bf16[385,1024]{1,0:T(8,128)(2,1)S(1)}, bf16[385,1024]{1,0:T(8,128)(2,1)}, u32[]{:S(2)}) copy-start(bf16[385,1024]{1,0:T(8,128)(2,1)} %copy-done.8) | copy-start | bytes 2365444
  158.7 15.7 %copy-start.11 = (bf16[256,1024]{1,0:T(8,128)(2,1)S(1)}, bf16[256,1024]{1,0:T(8,128)(2,1)}, u32[]{:S(2)}) copy-start(bf16[256,1024]{1,0:T(8,128)(2,1)} %param.10) | copy-start | bytes 1572868

commit v5 on v4

--- a/solution.py
+++ b/solution.py
@@ -34,11 +34,11 @@
 def exchange_scatter(part, axis):
     peers = lax.axis_size(axis)
     if part.shape[0] % peers:
-        return lax.psum_scatter(part, axis, scatter_dimension=0, tiled=True)
+        return lax.psum_scatter(part[::-1], axis, scatter_dimension=0, tiled=True)
     rows = part.shape[0] // peers
-    pieces = part.reshape((peers, rows) + part.shape[1:])
+    pieces = part.reshape((peers, rows) + part.shape[1:])[::-1]
     got = lax.all_to_all(pieces, axis, 0, 0)
-    return jnp.sum(got, axis=0)
+    return jnp.sum(got, axis=0)[::-1]
 
 
 def depthwise(source, kernel):
@@ -131,8 +131,11 @@
     grad_q = bwd_short(gqs, w_q).astype(jnp.bfloat16)
     grad_k = bwd_short(gks, w_k).astype(jnp.bfloat16)
     grad_input = bwd_short(gvs, w_v).astype(jnp.bfloat16)
-    taps_part = depthwise(u[: rows + extent - 1], gz[:rows])[::-1]
-    tap_sum = exchange_scatter(taps_part, "ctx")
+    lags = depthwise(u[: rows + extent - 1], gz[:rows])
+    lags, output, grad_q, grad_k, grad_input = lax.optimization_barrier(
+        (lags, output, grad_q, grad_k, grad_input)
+    )
+    tap_sum = exchange_scatter(lags, "ctx")
     return (output[None], grad_q[None], grad_k[None], grad_input[None], tap_sum[None])
 
 

time: 189 us -> 197 us (1.042)
  blocking collectives: 0 us -> 75.5 us
  starting transfers between devices: 73.9 us -> 26.6 us
  waiting for transfers between devices: 39.5 us -> 32.9 us
  local copies, waits for them, and re-layouts: 13.5 us -> 6.97 us
  other arithmetic: 16.6 us -> 11.1 us
    all_to_all x0 -> x1, blocking collectives: none -> 75.5 us  [exchange_scatter(): got = lax.all_to_all(pieces, axis, 0, 0)]
    all_to_all x1 -> x0, starting transfers between devices: 47.6 us -> none  [exchange_scatter(): got = lax.all_to_all(pieces, axis, 0, 0)]
    all_to_all x1 -> x0, waiting for transfers between devices: 7.14 us -> none  [exchange_scatter(): got = lax.all_to_all(pieces, axis, 0, 0)]
    broadcast_in_dim x4 -> x0, other arithmetic: 4.3 us -> none  [the longest x1 1.12 us: body(): grad_q[None]]
    convert_element_type x0 -> x4, other arithmetic: none -> 4.29 us  [the longest x1 1.12 us: body(): grad_k = bwd_short(gks, w_k).astype(jnp.bfloat16)]
    unnamed x38 -> x16, local copies, waits for them, and re-layouts: 3.2 us -> 0.76 us
    broadcast_in_dim x3, other arithmetic: 5.08 us -> 2.78 us  [depthwise(): source[None]]
    rev x1 -> x2, local copies, waits for them, and re-layouts: 4.74 us -> 2.46 us  [the longest x1 2.43 us: exchange_scatter(): return jnp.sum(got, axis=0)[::-1]]
  transfers between devices with their start and end apart: 6 -> 5, of which waited for: 6 -> 5; matrix products, arithmetic and copies ran while one was open for 12% -> 1% of each run, Pallas kernels for 0% -> 0%
where the time goes in v5:
time: 197 us
  blocking collectives  75.5 us (38%)
  matrix products  42.9 us (22%)
  waiting for transfers between devices  32.9 us (17%)
  starting transfers between devices  26.6 us (14%)
  other arithmetic  11.1 us (6%)
  local copies, waits for them, and re-layouts  6.97 us (4%)
    all_to_all x1, blocking collectives, exchange_scatter(): got = lax.all_to_all(pieces, axis, 0, 0)  75.5 us
    conv_general_dilated x3, matrix products, depthwise(): lax.conv_general_dilated(source[None], kernel[:, None, :], (1,), 'VALID',...  42.9 us
    ppermute x4, waiting for transfers between devices, shifted(): return lax.ppermute(value, axis, pairs)  17.7 us
    ppermute x1, starting transfers between devices, body(): lax.ppermute(jnp.where(first, out_first, gin_last), 'section', [(0, 1), (...  15.7 us
    ppermute x1, waiting for transfers between devices, body(): lax.ppermute(jnp.where(first, out_first, gin_last), 'section', [(0, 1), (...  15.1 us
    ppermute x4, starting transfers between devices, shifted(): return lax.ppermute(value, axis, pairs)  10.8 us
  transfers between devices with their start and end apart: 5, of which 5 were waited for; matrix products, arithmetic and copies ran while one was open for 1% of the time, Pallas kernels for 0%

profile of v5, /device:TPU:6, one launch (start us, length us, event | category | flops | bytes accessed | tf_op | source)
XLA Modules:
  0.0 196.9 jit_solution(23403637938013117)
XLA Ops:
  0.6 0.0 copy-start.2
  0.7 0.8 slice_bitcast_fusion.3
  1.5 0.0 slice-start.1
  1.5 1.1 slice_bitcast_fusion.1
  2.6 1.0 slice.250
  3.6 0.0 copy-start.4
  3.6 0.1 pad_maximum_fusion.3
  3.8 3.5 %collective-permute-start = (bf16[260,1024]{1,0:T(8,128)(2,1)S(1)}, bf16[260,1024]{1,0:T(8,128)(2,1)S(1)}, u32[]{:S(2)}, u32[]{:S(2)}) collective-permute-start(bf16[260,1024]{1,0:T(8,128)(2,1)S(1)} %pad_maximum_fusion.3), channel_id=1, source_target_pairs={{0,8},{8,16},{16,24},{24,32},{32,40},{40,48},{48,56},{56,64},{64,7... | collective-permute-start | bytes 1597448 | tf_op jit(solution)/shard_map/ppermute | solution.py:10
  7.4 0.9 pad_maximum_fusion.4
  8.3 1.3 collective-permute-start.1
  9.6 0.3 rev.9
  10.0 8.8 %collective-permute-done = bf16[260,1024]{1,0:T(8,128)(2,1)S(1)} collective-permute-done((bf16[260,1024]{1,0:T(8,128)(2,1)S(1)}, bf16[260,1024]{1,0:T(8,128)(2,1)S(1)}, u32[]{:S(2)}, u32[]{:S(2)}) %collective-permute-start) | collective-permute-done | bytes 532512 | tf_op jit(solution)/shard_map/ppermute | solution.py:10
  18.8 0.1 fusion.50
  18.9 0.0 copy-start.1
  18.9 5.2 %collective-permute-done.1 = bf16[262,1024]{1,0:T(8,128)(2,1)S(1)} collective-permute-done((bf16[262,1024]{1,0:T(8,128)(2,1)}, bf16[262,1024]{1,0:T(8,128)(2,1)S(1)}, u32[]{:S(2)}, u32[]{:S(2)}) %collective-permute-start.1) | collective-permute-done | bytes 536608 | tf_op jit(solution)/shard_map/ppermute | solution.py:10
  24.1 0.1 fusion.52
  24.2 0.2 maximum_convert_fusion.2
  24.4 0.0 copy-start
  24.4 0.4 maximum_convert_fusion
  24.9 0.6 copy-done
  25.5 1.8 select_bitcast_fusion.1
  27.3 0.0 copy-start.6
  27.3 14.5 %fusion.10 = f32[1,258,1024]{2,0,1:T(1,128)S(1)} fusion(bf16[1,385,1024]{2,1,0:T(8,128)(2,1)S(1)} %get-tuple-element.23, bf16[128,1,1024]{2,0,1:T(8,128)(2,1)S(1)} %get-tuple-element.40), kind=kOutput, calls=%fused_computation.26 | convolution fusion | flops 67633152 | bytes 2107392 | tf_op jit(solution)/shard_map/conv_general_dilated | solution.py:45
  41.8 0.5 fusion.37
  42.3 0.4 fusion.41
  42.7 15.7 %collective-permute-start.2 = (bf16[256,1024]{1,0:T(8,128)(2,1)S(1)}, bf16[256,1024]{1,0:T(8,128)(2,1)S(1)}, u32[]{:S(2)}, u32[]{:S(2)}) collective-permute-start(bf16[256,1024]{1,0:T(8,128)(2,1)S(1)} %fusion.41), channel_id=1, source_target_pairs={{0,256},{256,0},{1,257},{257,1},{2,258},{258,2},{3,259},{259,3},{4... | collective-permute-start | bytes 1572872 | tf_op jit(solution)/shard_map/ppermute | solution.py:107
  58.5 15.1 %collective-permute-done.2 = bf16[256,1024]{1,0:T(8,128)(2,1)S(1)} collective-permute-done((bf16[256,1024]{1,0:T(8,128)(2,1)S(1)}, bf16[256,1024]{1,0:T(8,128)(2,1)S(1)}, u32[]{:S(2)}, u32[]{:S(2)}) %collective-permute-start.2) | collective-permute-done | bytes 524320 | tf_op jit(solution)/shard_map/ppermute | solution.py:107
  73.6 0.1 fusion.53
  73.7 1.3 collective-permute-start.4
  75.0 4.7 %collective-permute-start.3 = (bf16[129,1024]{1,0:T(8,128)(2,1)S(1)}, bf16[129,1024]{1,0:T(8,128)(2,1)S(1)}, u32[]{:S(2)}, u32[]{:S(2)}) collective-permute-start(bf16[129,1024]{1,0:T(8,128)(2,1)S(1)} %get-tuple-element.41), channel_id=1, source_target_pairs={{0,8},{8,16},{16,24},{24,32},{32,40},{40,48},{48,56},{56,64},{64,7... | collective-permute-start | bytes 792584 | tf_op jit(solution)/shard_map/ppermute | solution.py:10
  79.8 2.3 %collective-permute-done.4 = bf16[129,1024]{1,0:T(8,128)(2,1)S(1)} collective-permute-done((bf16[129,1024]{1,0:T(8,128)(2,1)S(1)}, bf16[129,1024]{1,0:T(8,128)(2,1)S(1)}, u32[]{:S(2)}, u32[]{:S(2)}) %collective-permute-start.4) | collective-permute-done | bytes 264224 | tf_op jit(solution)/shard_map/ppermute | solution.py:10
  82.2 1.4 collective-permute-done.3
  83.6 0.2 fusion.31
  83.8 0.9 select_bitcast_fusion
  84.7 0.1 fusion.32
  84.8 0.1 fusion.42
  84.8 13.9 %fusion.12 = f32[1,128,1024]{2,0,1:T(1,128)S(1)} fusion(bf16[1,383,1024]{2,1,0:T(8,128)(2,1)S(1)} %fusion.32, bf16[256,1,1024]{2,0,1:T(8,128)(2,1)S(1)} %fusion.42), kind=kOutput, calls=%fused_computation.28 | convolution fusion | flops 67108864 | bytes 1832960 | tf_op jit(solution)/shard_map/conv_general_dilated | solution.py:45
  98.7 0.1 copy.46
  98.8 14.5 %fusion.8 = f32[1,258,1024]{2,0,1:T(1,128)S(1)} fusion(bf16[1,385,1024]{2,1,0:T(8,128)(2,1)S(1)} %get-tuple-element.17, bf16[128,1,1024]{2,0,1:T(8,128)(2,1)S(1)} %get-tuple-element.39), kind=kOutput, calls=%fused_computation.24 | convolution fusion | flops 67633152 | bytes 2107392 | tf_op jit(solution)/shard_map/conv_general_dilated | solution.py:45
  113.3 1.1 fusion.39
  114.4 0.9 fusion.25
  115.3 1.1 fusion.17
  116.4 1.1 fusion.20
  117.6 1.1 fusion.23
  118.7 0.1 reshape.41
  118.9 75.5 %all_to_all.5 = f32[32,4,1024]{2,1,0:T(4,128)S(1)} all-to-all(f32[32,4,1024]{2,1,0:T(4,128)S(1)} %rev.10), channel_id=1, replica_groups=mesh['section'=2,'ctx'=32,'chan'=8] {'ctx'}, dimensions={0} | all-to-all | bytes 1048576 | tf_op jit(solution)/shard_map/all_to_all | solution.py:40
  194.4 0.1 reduce_sum.9
  194.5 2.4 %rev.11 = f32[4,1024]{1,0:T(4,128)} reverse(f32[4,1024]{1,0:T(4,128)S(1)} %reduce_sum.9), dimensions={0} | reverse | bytes 32768 | tf_op jit(solution)/shard_map/rev | solution.py:41
  (20 shorter events, 0.2 us)
Async XLA Ops:
  0.6 6.7 %copy-start.3 = (bf16[1,256,1024]{2,1,0:T(8,128)(2,1)S(1)}, bf16[1,256,1024]{2,1,0:T(8,128)(2,1)}, u32[]{:S(2)}) copy-start(bf16[1,256,1024]{2,1,0:T(8,128)(2,1)} %param.7) | copy-start | bytes 1572868
  0.6 6.6 %copy-start.2 = (bf16[1,256,1024]{2,1,0:T(8,128)(2,1)S(1)}, bf16[1,256,1024]{2,1,0:T(8,128)(2,1)}, u32[]{:S(2)}) copy-start(bf16[1,256,1024]{2,1,0:T(8,128)(2,1)} %param.8) | copy-start | bytes 1572868
  1.5 5.9 %slice-start = ((bf16[256,1024]{1,0:T(8,128)(2,1)}), bf16[129,1024]{1,0:T(8,128)(2,1)S(1)}, s32[]{:S(2)}) async-start(bf16[256,1024]{1,0:T(8,128)(2,1)} %param.10), calls=%async_computation.1 | async-start | bytes 557056 | tf_op jit(solution)/shard_map/slice | solution.py:87
  1.5 5.9 %slice-start.1 = ((bf16[256,1024]{1,0:T(8,128)(2,1)}), bf16[2,1024]{1,0:T(2,128)(2,1)S(1)}, s32[]{:S(2)}) async-start(bf16[256,1024]{1,0:T(8,128)(2,1)} %param.9), calls=%async_computation.2 | async-start | bytes 8192 | tf_op jit(solution)/shard_map/slice | solution.py:87
  3.6 6.0 %copy-start.5 = (f32[1,3,3,1024]{3,0,2,1:T(1,128)S(1)}, f32[1,3,3,1024]{3,0,2,1:T(1,128)}, u32[]{:S(2)}) copy-start(f32[1,3,3,1024]{3,0,2,1:T(1,128)} %param.11) | copy-start | bytes 110596
  3.6 6.0 %copy-start.4 = (bf16[1,128,1024]{2,1,0:T(8,128)(2,1)S(1)}, bf16[1,128,1024]{2,1,0:T(8,128)(2,1)}, u32[]{:S(2)}) copy-start(bf16[1,128,1024]{2,1,0:T(8,128)(2,1)} %param.12) | copy-start | bytes 786436
  3.8 15.0 %collective-permute-start = (bf16[260,1024]{1,0:T(8,128)(2,1)S(1)}, bf16[260,1024]{1,0:T(8,128)(2,1)S(1)}, u32[]{:S(2)}, u32[]{:S(2)}) collective-permute-start(bf16[260,1024]{1,0:T(8,128)(2,1)S(1)} %pad_maximum_fusion.3), channel_id=1, source_target_pairs={{0,8},{8,16},{16,24},{24,32},{32,40},{40,48},{48,56},{56,64},{64,7... | collective-permute-start | bytes 1597448 | tf_op jit(solution)/shard_map/ppermute | solution.py:10
  8.3 15.8 %collective-permute-start.1 = (bf16[262,1024]{1,0:T(8,128)(2,1)}, bf16[262,1024]{1,0:T(8,128)(2,1)S(1)}, u32[]{:S(2)}, u32[]{:S(2)}) collective-permute-start(bf16[262,1024]{1,0:T(8,128)(2,1)} %pad_maximum_fusion.4), channel_id=1, source_target_pairs={{8,0},{16,8},{24,16},{32,24},{40,32},{48,40},{56,48},{64,56},{72,6... | collective-permute-start | bytes 1609736 | tf_op jit(solution)/shard_map/ppermute | solution.py:10
  18.9 5.5 %copy-start.1 = (bf16[256,1024]{1,0:T(8,128)(2,1)S(1)}, bf16[256,1024]{1,0:T(8,128)(2,1)}, u32[]{:S(2)}) copy-start(bf16[256,1024]{1,0:T(8,128)(2,1)} %param.9) | copy-start | bytes 1572868
  24.4 1.0 copy-start
  27.3 14.5 %copy-start.6 = (f32[1,1024]{1,0:T(1,128)S(1)}, f32[1,1024]{1,0:T(1,128)}, u32[]{:S(2)}) copy-start(f32[1,1024]{1,0:T(1,128)} %param.13) | copy-start | bytes 12292
  42.7 30.9 %collective-permute-start.2 = (bf16[256,1024]{1,0:T(8,128)(2,1)S(1)}, bf16[256,1024]{1,0:T(8,128)(2,1)S(1)}, u32[]{:S(2)}, u32[]{:S(2)}) collective-permute-start(bf16[256,1024]{1,0:T(8,128)(2,1)S(1)} %fusion.41), channel_id=1, source_target_pairs={{0,256},{256,0},{1,257},{257,1},{2,258},{258,2},{3,259},{259,3},{4... | collective-permute-start | bytes 1572872 | tf_op jit(solution)/shard_map/ppermute | solution.py:107
  73.7 8.4 %collective-permute-start.4 = (bf16[129,1024]{1,0:T(8,128)(2,1)S(1)}, bf16[129,1024]{1,0:T(8,128)(2,1)S(1)}, u32[]{:S(2)}, u32[]{:S(2)}) collective-permute-start(bf16[129,1024]{1,0:T(8,128)(2,1)S(1)} %get-tuple-element.42), channel_id=1, source_target_pairs={{8,0},{16,8},{24,16},{32,24},{40,32},{48,40},{56,48},{64,56},{72,6... | collective-permute-start | bytes 792584 | tf_op jit(solution)/shard_map/ppermute | solution.py:10
  75.0 8.6 %collective-permute-start.3 = (bf16[129,1024]{1,0:T(8,128)(2,1)S(1)}, bf16[129,1024]{1,0:T(8,128)(2,1)S(1)}, u32[]{:S(2)}, u32[]{:S(2)}) collective-permute-start(bf16[129,1024]{1,0:T(8,128)(2,1)S(1)} %get-tuple-element.41), channel_id=1, source_target_pairs={{0,8},{8,16},{16,24},{24,32},{32,40},{40,48},{48,56},{56,64},{64,7... | collective-permute-start | bytes 792584 | tf_op jit(solution)/shard_map/ppermute | solution.py:10

commit v6 on v5

--- a/solution.py
+++ b/solution.py
@@ -132,9 +132,6 @@
     grad_k = bwd_short(gks, w_k).astype(jnp.bfloat16)
     grad_input = bwd_short(gvs, w_v).astype(jnp.bfloat16)
     lags = depthwise(u[: rows + extent - 1], gz[:rows])
-    lags, output, grad_q, grad_k, grad_input = lax.optimization_barrier(
-        (lags, output, grad_q, grad_k, grad_input)
-    )
     tap_sum = exchange_scatter(lags, "ctx")
     return (output[None], grad_q[None], grad_k[None], grad_input[None], tap_sum[None])
 

time: 197 us -> 190 us (0.964)
  blocking collectives: 75.5 us -> 0 us
  starting transfers between devices: 26.6 us -> 73.9 us
  waiting for transfers between devices: 32.9 us -> 39.5 us
  local copies, waits for them, and re-layouts: 6.97 us -> 12.2 us
  other arithmetic: 11.1 us -> 16 us
  matrix products: 42.9 us -> 47 us
    all_to_all x1 -> x0, blocking collectives: 75.5 us -> none  [exchange_scatter(): got = lax.all_to_all(pieces, axis, 0, 0)]
    all_to_all x0 -> x1, starting transfers between devices: none -> 47.6 us  [exchange_scatter(): got = lax.all_to_all(pieces, axis, 0, 0)]
    all_to_all x0 -> x1, waiting for transfers between devices: none -> 7.14 us  [exchange_scatter(): got = lax.all_to_all(pieces, axis, 0, 0)]
    broadcast_in_dim x0 -> x4, other arithmetic: none -> 4.3 us  [the longest x1 1.12 us: body(): grad_q[None]]
    convert_element_type x4 -> x0, other arithmetic: 4.29 us -> none  [the longest x1 1.12 us: body(): grad_k = bwd_short(gks, w_k).astype(jnp.bfloat16)]
    conv_general_dilated x3, matrix products: 42.9 us -> 47 us  [depthwise(): lax.conv_general_dilated(source[None], kernel[:, None, :], (1,), 'VALID',...]
    broadcast_in_dim x3, other arithmetic: 2.78 us -> 5.04 us  [depthwise(): source[None]]
    another operation x0 -> x1, local copies, waits for them, and re-layouts: none -> 1.98 us  [exchange_scatter(): pieces = part.reshape((peers, rows) + part.shape[1:])[::-1]]
  transfers between devices with their start and end apart: 5 -> 6, of which waited for: 5 -> 6; matrix products, arithmetic and copies ran while one was open for 1% -> 12% of each run, Pallas kernels for 0% -> 0%
where the time goes in v6:
time: 190 us
  starting transfers between devices  73.9 us (39%)
  matrix products  47 us (25%)
  waiting for transfers between devices  39.5 us (21%)
  other arithmetic  16 us (8%)
  local copies, waits for them, and re-layouts  12.2 us (6%)
    all_to_all x1, starting transfers between devices, exchange_scatter(): got = lax.all_to_all(pieces, axis, 0, 0)  47.6 us
    conv_general_dilated x3, matrix products, depthwise(): lax.conv_general_dilated(source[None], kernel[:, None, :], (1,), 'VALID',...  47 us
    ppermute x4, waiting for transfers between devices, shifted(): return lax.ppermute(value, axis, pairs)  17.2 us
    ppermute x1, starting transfers between devices, body(): lax.ppermute(jnp.where(first, out_first, gin_last), 'section', [(0, 1), (...  15.7 us
    ppermute x1, waiting for transfers between devices, body(): lax.ppermute(jnp.where(first, out_first, gin_last), 'section', [(0, 1), (...  15.1 us
    ppermute x4, starting transfers between devices, shifted(): return lax.ppermute(value, axis, pairs)  10.6 us
    all_to_all x1, waiting for transfers between devices, exchange_scatter(): got = lax.all_to_all(pieces, axis, 0, 0)  7.14 us
    broadcast_in_dim x3, other arithmetic, depthwise(): source[None]  5.04 us
  transfers between devices with their start and end apart: 6, of which 6 were waited for; matrix products, arithmetic and copies ran while one was open for 12% of the time, Pallas kernels for 0%

profile of v6, /device:TPU:6, one launch (start us, length us, event | category | flops | bytes accessed | tf_op | source)
XLA Modules:
  0.0 189.7 jit_solution(5640173167349043167)
XLA Ops:
  0.6 0.0 slice-start.1
  0.7 1.1 slice.250
  1.8 1.0 slice_bitcast_fusion.1
  2.8 0.7 slice_bitcast_fusion.3
  3.6 1.0 pad_maximum_fusion.3
  4.6 3.5 %collective-permute-start = (bf16[260,1024]{1,0:T(8,128)(2,1)}, bf16[260,1024]{1,0:T(8,128)(2,1)S(1)}, u32[]{:S(2)}, u32[]{:S(2)}) collective-permute-start(bf16[260,1024]{1,0:T(8,128)(2,1)} %pad_maximum_fusion.3), channel_id=1, source_target_pairs={{0,8},{8,16},{16,24},{24,32},{32,40},{40,48},{48,56},{56,64},{64,7... | collective-permute-start | bytes 1597448 | tf_op jit(solution)/shard_map/ppermute | solution.py:10
  8.1 0.9 pad_maximum_fusion.4
  9.0 1.3 collective-permute-start.1
  10.4 0.3 rev.9
  10.7 0.7 select_bitcast_fusion.2
  11.5 8.4 %collective-permute-done = bf16[260,1024]{1,0:T(8,128)(2,1)S(1)} collective-permute-done((bf16[260,1024]{1,0:T(8,128)(2,1)}, bf16[260,1024]{1,0:T(8,128)(2,1)S(1)}, u32[]{:S(2)}, u32[]{:S(2)}) %collective-permute-start) | collective-permute-done | bytes 532512 | tf_op jit(solution)/shard_map/ppermute | solution.py:10
  19.9 0.1 fusion.57
  20.0 4.9 %collective-permute-done.1 = bf16[262,1024]{1,0:T(8,128)(2,1)S(1)} collective-permute-done((bf16[262,1024]{1,0:T(8,128)(2,1)}, bf16[262,1024]{1,0:T(8,128)(2,1)S(1)}, u32[]{:S(2)}, u32[]{:S(2)}) %collective-permute-start.1) | collective-permute-done | bytes 536608 | tf_op jit(solution)/shard_map/ppermute | solution.py:10
  24.9 0.1 fusion.59
  24.9 0.2 maximum_convert_fusion
  25.2 0.4 maximum_convert_fusion.1
  25.7 0.6 copy-done.10
  26.2 2.7 %select_bitcast_fusion.1 = (bf16[1,385,1024]{2,1,0:T(8,128)(2,1)S(1)}, bf16[385,1024]{1,0:T(8,128)(2,1)S(1)}, f32[385,1024]{1,0:T(8,128)S(1)}, bf16[385,1024]{1,...) fusion(pred[]{:T(512)S(6)} %eq.3, bf16[129,1024]{1,0:T(8,128)(2,1)S(1)} %get-tuple-element.28, ...), kind=kLoop, calls=%fused_computation.78 | loop fusion | flops 9461760 | bytes 22114304 | tf_op jit(solution)/shard_map/broadcast_in_dim | solution.py:46
  28.9 14.5 %fusion.10 = f32[1,258,1024]{2,0,1:T(1,128)S(1)} fusion(bf16[1,385,1024]{2,1,0:T(8,128)(2,1)S(1)} %get-tuple-element.13, bf16[128,1,1024]{2,0,1:T(8,128)(2,1)S(1)} %get-tuple-element.30), kind=kOutput, calls=%fused_computation.26 | convolution fusion | flops 67633152 | bytes 2107392 | tf_op jit(solution)/shard_map/conv_general_dilated | solution.py:45
  43.4 0.6 fusion.40
  44.0 0.4 fusion.44
  44.4 0.6 copy-done
  45.0 15.7 %collective-permute-start.2 = (bf16[256,1024]{1,0:T(8,128)(2,1)S(1)}, bf16[256,1024]{1,0:T(8,128)(2,1)S(1)}, u32[]{:S(2)}, u32[]{:S(2)}) collective-permute-start(bf16[256,1024]{1,0:T(8,128)(2,1)S(1)} %fusion.44), channel_id=1, source_target_pairs={{0,256},{256,0},{1,257},{257,1},{2,258},{258,2},{3,259},{259,3},{4... | collective-permute-start | bytes 1572872 | tf_op jit(solution)/shard_map/ppermute | solution.py:107
  60.7 15.1 %collective-permute-done.2 = bf16[256,1024]{1,0:T(8,128)(2,1)S(1)} collective-permute-done((bf16[256,1024]{1,0:T(8,128)(2,1)S(1)}, bf16[256,1024]{1,0:T(8,128)(2,1)S(1)}, u32[]{:S(2)}, u32[]{:S(2)}) %collective-permute-start.2) | collective-permute-done | bytes 524320 | tf_op jit(solution)/shard_map/ppermute | solution.py:107
  75.8 0.1 fusion.60
  75.9 1.3 collective-permute-start.3
  77.2 4.6 %collective-permute-start.4 = (bf16[129,1024]{1,0:T(8,128)(2,1)S(1)}, bf16[129,1024]{1,0:T(8,128)(2,1)S(1)}, u32[]{:S(2)}, u32[]{:S(2)}) collective-permute-start(bf16[129,1024]{1,0:T(8,128)(2,1)S(1)} %get-tuple-element.31), channel_id=1, source_target_pairs={{0,8},{8,16},{16,24},{24,32},{32,40},{40,48},{48,56},{56,64},{64,7... | collective-permute-start | bytes 792584 | tf_op jit(solution)/shard_map/ppermute | solution.py:10
  81.8 2.5 %collective-permute-done.3 = bf16[129,1024]{1,0:T(8,128)(2,1)S(1)} collective-permute-done((bf16[129,1024]{1,0:T(8,128)(2,1)S(1)}, bf16[129,1024]{1,0:T(8,128)(2,1)S(1)}, u32[]{:S(2)}, u32[]{:S(2)}) %collective-permute-start.3) | collective-permute-done | bytes 264224 | tf_op jit(solution)/shard_map/ppermute | solution.py:10
  84.4 1.4 collective-permute-done.4
  85.8 0.2 fusion.34
  86.0 2.3 %select_bitcast_fusion = (bf16[1,385,1024]{2,1,0:T(8,128)(2,1)}, bf16[385,1024]{1,0:T(8,128)(2,1)S(1)}, f32[385,1024]{1,0:T(8,128)}, bf16[385,1024]{1,0:T(8,128)(2,1)S(1)}) fusion(pred[]{:T(512)S(6)} %eq.3, f32[385,1024]{1,0:T(8,128)S(1)} %get-tuple-element.18, f32[387,1024]{1,0:T(8,128)S(1)} %fusion.34, f32[1024]{0:T(1024)S(1)} %bitcast.67, ...), kind=kLoop, calls=%fused_computation.77 | loop fusion | flops 4336640 | bytes 12627969 | tf_op jit(solution)/shard_map/broadcast_in_dim | solution.py:46
  88.3 0.1 fusion.49
  88.4 0.1 fusion.35
  88.5 0.7 copy-done.2
  89.2 0.3 copy-done.6
  89.5 17.0 %fusion.14 = f32[128,1024]{1,0:T(8,128)} fusion(bf16[1,383,1024]{2,1,0:T(8,128)(2,1)S(1)} %fusion.35, bf16[256,1,1024]{2,0,1:T(8,128)(2,1)S(1)} %fusion.49), kind=kOutput, calls=%fused_computation.30 | convolution fusion | flops 67108864 | bytes 1832960 | tf_op jit(solution)/shard_map/conv_general_dilated | solution.py:45
  106.4 2.0 %reshape_squeeze.3 = f32[32,4,1024]{2,1,0:T(4,128)} reshape(f32[128,1024]{1,0:T(8,128)} %fusion.14) | data formatting | bytes 1048576 | tf_op jit(solution)/shard_map/reshape;squeeze | solution.py:39
  108.4 1.9 rev.10
  110.3 47.6 %all-to-all-start = ((f32[32,4,1024]{2,1,0:T(4,128)}), f32[32,4,1024]{2,1,0:T(4,128)}, u32[]{:S(2)}, u32[]{:S(2)}) async-start(f32[32,4,1024]{2,1,0:T(4,128)} %rev.10), calls=%async_computation | async-start | bytes 1048576 | tf_op jit(solution)/shard_map/all_to_all | solution.py:40
  158.0 15.6 %fusion.8 = f32[1,258,1024]{2,0,1:T(1,128)S(1)} fusion(bf16[1,385,1024]{2,1,0:T(8,128)(2,1)} %get-tuple-element.7, bf16[128,1,1024]{2,0,1:T(8,128)(2,1)} %get-tuple-element.29), kind=kOutput, calls=%fused_computation.24 | convolution fusion | flops 67633152 | bytes 2107392 | tf_op jit(solution)/shard_map/conv_general_dilated | solution.py:45
  173.6 1.1 fusion.42
  174.7 1.1 fusion.46
  175.8 1.1 fusion.47
  176.9 1.1 fusion.48
  178.1 0.9 fusion.45
  179.0 7.1 %all-to-all-done = f32[32,4,1024]{2,1,0:T(4,128)} async-done(((f32[32,4,1024]{2,1,0:T(4,128)}), f32[32,4,1024]{2,1,0:T(4,128)}, u32[]{:S(2)}, u32[]{:S(2)}) %all-to-all-start) | async-done | bytes 524320 | tf_op jit(solution)/shard_map/all_to_all | solution.py:40
  186.1 1.1 reduce_sum.9
  187.3 2.4 %rev.11 = f32[4,1024]{1,0:T(4,128)} reverse(f32[4,1024]{1,0:T(4,128)S(1)} %reduce_sum.9), dimensions={0} | reverse | bytes 32768 | tf_op jit(solution)/shard_map/rev | solution.py:41
  (42 shorter events, 0.2 us)
Async XLA Ops:
  0.6 7.5 %slice-start.1 = ((bf16[256,1024]{1,0:T(8,128)(2,1)}), bf16[2,1024]{1,0:T(2,128)(2,1)S(1)}, s32[]{:S(2)}) async-start(bf16[256,1024]{1,0:T(8,128)(2,1)} %param.9), calls=%async_computation.2 | async-start | bytes 8192 | tf_op jit(solution)/shard_map/slice | solution.py:87
  0.6 7.5 %copy-start.13 = (bf16[1,256,1024]{2,1,0:T(8,128)(2,1)S(1)}, bf16[1,256,1024]{2,1,0:T(8,128)(2,1)}, u32[]{:S(2)}) copy-start(bf16[1,256,1024]{2,1,0:T(8,128)(2,1)} %param.8) | copy-start | bytes 1572868
  0.7 7.4 %copy-start.14 = (bf16[1,256,1024]{2,1,0:T(8,128)(2,1)S(1)}, bf16[1,256,1024]{2,1,0:T(8,128)(2,1)}, u32[]{:S(2)}) copy-start(bf16[1,256,1024]{2,1,0:T(8,128)(2,1)} %param.7) | copy-start | bytes 1572868
  0.7 7.5 %slice-start = ((bf16[256,1024]{1,0:T(8,128)(2,1)}), bf16[129,1024]{1,0:T(8,128)(2,1)S(1)}, s32[]{:S(2)}) async-start(bf16[256,1024]{1,0:T(8,128)(2,1)} %param.10), calls=%async_computation.1 | async-start | bytes 557056 | tf_op jit(solution)/shard_map/slice | solution.py:87
  3.6 6.8 %copy-start.16 = (f32[1,3,3,1024]{3,0,2,1:T(1,128)S(1)}, f32[1,3,3,1024]{3,0,2,1:T(1,128)}, u32[]{:S(2)}) copy-start(f32[1,3,3,1024]{3,0,2,1:T(1,128)} %param.11) | copy-start | bytes 110596
  3.6 6.8 %copy-start.15 = (bf16[1,128,1024]{2,1,0:T(8,128)(2,1)S(1)}, bf16[1,128,1024]{2,1,0:T(8,128)(2,1)}, u32[]{:S(2)}) copy-start(bf16[1,128,1024]{2,1,0:T(8,128)(2,1)} %param.12) | copy-start | bytes 786436
  4.6 15.3 %collective-permute-start = (bf16[260,1024]{1,0:T(8,128)(2,1)}, bf16[260,1024]{1,0:T(8,128)(2,1)S(1)}, u32[]{:S(2)}, u32[]{:S(2)}) collective-permute-start(bf16[260,1024]{1,0:T(8,128)(2,1)} %pad_maximum_fusion.3), channel_id=1, source_target_pairs={{0,8},{8,16},{16,24},{24,32},{32,40},{40,48},{48,56},{56,64},{64,7... | collective-permute-start | bytes 1597448 | tf_op jit(solution)/shard_map/ppermute | solution.py:10
  9.0 15.8 %collective-permute-start.1 = (bf16[262,1024]{1,0:T(8,128)(2,1)}, bf16[262,1024]{1,0:T(8,128)(2,1)S(1)}, u32[]{:S(2)}, u32[]{:S(2)}) collective-permute-start(bf16[262,1024]{1,0:T(8,128)(2,1)} %pad_maximum_fusion.4), channel_id=1, source_target_pairs={{8,0},{16,8},{24,16},{32,24},{40,32},{48,40},{56,48},{64,56},{72,6... | collective-permute-start | bytes 1609736 | tf_op jit(solution)/shard_map/ppermute | solution.py:10
  20.0 5.2 %copy-start.12 = (bf16[256,1024]{1,0:T(8,128)(2,1)S(1)}, bf16[256,1024]{1,0:T(8,128)(2,1)}, u32[]{:S(2)}) copy-start(bf16[256,1024]{1,0:T(8,128)(2,1)} %param.9) | copy-start | bytes 1572868
  25.2 1.0 copy-start.10
  28.9 14.5 %copy-start.17 = (f32[1,1024]{1,0:T(1,128)S(1)}, f32[1,1024]{1,0:T(1,128)}, u32[]{:S(2)}) copy-start(f32[1,1024]{1,0:T(1,128)} %param.13) | copy-start | bytes 12292
  44.0 1.0 copy-start
  45.0 30.9 %collective-permute-start.2 = (bf16[256,1024]{1,0:T(8,128)(2,1)S(1)}, bf16[256,1024]{1,0:T(8,128)(2,1)S(1)}, u32[]{:S(2)}, u32[]{:S(2)}) collective-permute-start(bf16[256,1024]{1,0:T(8,128)(2,1)S(1)} %fusion.44), channel_id=1, source_target_pairs={{0,256},{256,0},{1,257},{257,1},{2,258},{258,2},{3,259},{259,3},{4... | collective-permute-start | bytes 1572872 | tf_op jit(solution)/shard_map/ppermute | solution.py:107
  75.9 8.4 %collective-permute-start.3 = (bf16[129,1024]{1,0:T(8,128)(2,1)S(1)}, bf16[129,1024]{1,0:T(8,128)(2,1)S(1)}, u32[]{:S(2)}, u32[]{:S(2)}) collective-permute-start(bf16[129,1024]{1,0:T(8,128)(2,1)S(1)} %get-tuple-element.32), channel_id=1, source_target_pairs={{8,0},{16,8},{24,16},{32,24},{40,32},{48,40},{56,48},{64,56},{72,6... | collective-permute-start | bytes 792584 | tf_op jit(solution)/shard_map/ppermute | solution.py:10
  77.2 8.6 %collective-permute-start.4 = (bf16[129,1024]{1,0:T(8,128)(2,1)S(1)}, bf16[129,1024]{1,0:T(8,128)(2,1)S(1)}, u32[]{:S(2)}, u32[]{:S(2)}) collective-permute-start(bf16[129,1024]{1,0:T(8,128)(2,1)S(1)} %get-tuple-element.31), channel_id=1, source_target_pairs={{0,8},{8,16},{16,24},{24,32},{32,40},{40,48},{48,56},{56,64},{64,7... | collective-permute-start | bytes 792584 | tf_op jit(solution)/shard_map/ppermute | solution.py:10
  84.4 3.9 %copy-start.8 = (bf16[385,1024]{1,0:T(8,128)(2,1)}, bf16[385,1024]{1,0:T(8,128)(2,1)S(1)}, u32[]{:S(2)}) copy-start(bf16[385,1024]{1,0:T(8,128)(2,1)S(1)} %constant_dynamic-update-slice_fusion) | copy-start | bytes 2365444
  88.3 0.9 copy-start.2
  88.3 1.2 copy-start.6
  110.3 75.8 %all-to-all-start = ((f32[32,4,1024]{2,1,0:T(4,128)}), f32[32,4,1024]{2,1,0:T(4,128)}, u32[]{:S(2)}, u32[]{:S(2)}) async-start(f32[32,4,1024]{2,1,0:T(4,128)} %rev.10), calls=%async_computation | async-start | bytes 1048576 | tf_op jit(solution)/shard_map/all_to_all | solution.py:40
  157.9 15.7 %copy-start.1 = (f32[258,1024]{1,0:T(8,128)S(1)}, f32[258,1024]{1,0:T(8,128)}, u32[]{:S(2)}) copy-start(f32[258,1024]{1,0:T(8,128)} %copy-done) | copy-start | bytes 3170308
  157.9 15.7 %copy-start.3 = (bf16[385,1024]{1,0:T(8,128)(2,1)S(1)}, bf16[385,1024]{1,0:T(8,128)(2,1)}, u32[]{:S(2)}) copy-start(bf16[385,1024]{1,0:T(8,128)(2,1)} %copy-done.2) | copy-start | bytes 2365444
  157.9 15.7 %copy-start.4 = (f32[385,1024]{1,0:T(8,128)S(1)}, f32[385,1024]{1,0:T(8,128)}, u32[]{:S(2)}) copy-start(f32[385,1024]{1,0:T(8,128)} %get-tuple-element.9) | copy-start | bytes 4730884
  157.9 15.7 %copy-start.5 = (f32[385,1024]{1,0:T(8,128)S(1)}, f32[385,1024]{1,0:T(8,128)}, u32[]{:S(2)}) copy-start(f32[385,1024]{1,0:T(8,128)} %get-tuple-element.17) | copy-start | bytes 4730884
  157.9 15.7 %copy-start.7 = (bf16[385,1024]{1,0:T(8,128)(2,1)S(1)}, bf16[385,1024]{1,0:T(8,128)(2,1)}, u32[]{:S(2)}) copy-start(bf16[385,1024]{1,0:T(8,128)(2,1)} %copy-done.6) | copy-start | bytes 2365444
  157.9 15.7 %copy-start.9 = (bf16[385,1024]{1,0:T(8,128)(2,1)S(1)}, bf16[385,1024]{1,0:T(8,128)(2,1)}, u32[]{:S(2)}) copy-start(bf16[385,1024]{1,0:T(8,128)(2,1)} %copy-done.8) | copy-start | bytes 2365444
  157.9 15.7 %copy-start.11 = (bf16[256,1024]{1,0:T(8,128)(2,1)S(1)}, bf16[256,1024]{1,0:T(8,128)(2,1)}, u32[]{:S(2)}) copy-start(bf16[256,1024]{1,0:T(8,128)(2,1)} %param.10) | copy-start | bytes 1572868

commit v7 on v4

--- a/solution.py
+++ b/solution.py
@@ -105,8 +105,21 @@
     gin_last = bwd_short(gvs_last, w_v).astype(jnp.bfloat16)
 
     handed = lax.ppermute(jnp.where(first, out_first, gin_last), "section", [(0, 1), (1, 0)])
-    prev_b = from_prev(handed[-reach:])
-    next_b = from_next(handed[:reach])
+    sections = lax.axis_size("section")
+    peers = lax.axis_size("ctx")
+    both = ("section", "ctx")
+    rim = lax.ppermute(
+        jnp.where(first, out_first[-reach:], gin_last[:reach]),
+        both,
+        [(i, peers + i + 1) for i in range(peers - 1)] + [(peers + i, i - 1) for i in range(1, peers)],
+    ) if sections == 2 else None
+    if rim is None:
+        prev_b = from_prev(handed[-reach:])
+        next_b = from_next(handed[:reach])
+    else:
+        ahead = lax.ppermute(out_first[:2], both, [(i + 1, peers + i) for i in range(peers - 1)])
+        prev_b = rim
+        next_b = jnp.concatenate([jnp.where(first, rim[:2], ahead), rim[2:]], axis=0)
     y_ext = jnp.concatenate([prev_b, handed, next_b], axis=0)
 
     gz_first = (y_ext[reach:].astype(jnp.float32) * q_short).astype(jnp.bfloat16)

time: 189 us -> 215 us (1.14)
  starting transfers between devices: 73.9 us -> 94.2 us
  waiting for transfers between devices: 39.5 us -> 44.9 us
    ppermute x0 -> x2, waiting for transfers between devices: none -> 23.1 us  [the longest x1 23.1 us: body(): lax.ppermute(jnp.where(first, out_first[-reach:], gin_last[:reach]), both...]
    all_to_all x1, starting transfers between devices: 47.6 us -> 70.1 us  [exchange_scatter(): got = lax.all_to_all(pieces, axis, 0, 0)]
    ppermute x1, waiting for transfers between devices: 15.1 us -> 0.01 us  [body(): lax.ppermute(jnp.where(first, out_first, gin_last), 'section', [(0, 1), (...]
    ppermute x4 -> x2, starting transfers between devices: 10.6 us -> 4.78 us  [shifted(): return lax.ppermute(value, axis, pairs)]
    ppermute x4 -> x2, waiting for transfers between devices: 17.2 us -> 13.2 us  [shifted(): return lax.ppermute(value, axis, pairs)]
    ppermute x0 -> x2, starting transfers between devices: none -> 3.57 us  [the longest x1 2.9 us: body(): lax.ppermute(jnp.where(first, out_first[-reach:], gin_last[:reach]), both...]
  transfers between devices with their start and end apart: 6 -> 6, of which waited for: 6 -> 4; matrix products, arithmetic and copies ran while one was open for 12% -> 11% of each run, Pallas kernels for 0% -> 0%
where the time goes in v7:
time: 215 us; the launch traced here: 214 us
  starting transfers between devices  94.2 us (44%)
  waiting for transfers between devices  44.9 us (21%)
  matrix products  43.9 us (20%)
  other arithmetic  16.8 us (8%)
  local copies, waits for them, and re-layouts  13.4 us (6%)
    all_to_all x1, starting transfers between devices, exchange_scatter(): got = lax.all_to_all(pieces, axis, 0, 0)  70.1 us
    conv_general_dilated x3, matrix products, depthwise(): lax.conv_general_dilated(source[None], kernel[:, None, :], (1,), 'VALID',...  43.9 us
    ppermute x1, waiting for transfers between devices, body(): lax.ppermute(jnp.where(first, out_first[-reach:], gin_last[:reach]), both...  23.1 us
    ppermute x1, starting transfers between devices, body(): lax.ppermute(jnp.where(first, out_first, gin_last), 'section', [(0, 1), (...  15.7 us
    ppermute x2, waiting for transfers between devices, shifted(): return lax.ppermute(value, axis, pairs)  13.2 us
    all_to_all x1, waiting for transfers between devices, exchange_scatter(): got = lax.all_to_all(pieces, axis, 0, 0)  8.47 us
    broadcast_in_dim x3, other arithmetic, depthwise(): source[None]  5.14 us
    ppermute x2, starting transfers between devices, shifted(): return lax.ppermute(value, axis, pairs)  4.78 us
  transfers between devices with their start and end apart: 6, of which 4 were waited for; matrix products, arithmetic and copies ran while one was open for 11% of the time, Pallas kernels for 0%

profile of v7, /device:TPU:6, one launch (start us, length us, event | category | flops | bytes accessed | tf_op | source)
XLA Modules:
  0.0 214.3 jit_solution(4051553969896794837)
XLA Ops:
  0.6 0.0 slice-start.1
  0.7 0.0 slice-start
  0.7 1.1 slice.256
  1.8 1.0 slice_bitcast_fusion.1
  2.8 0.7 slice_bitcast_fusion.3
  3.6 1.0 pad_maximum_fusion.1
  4.6 3.5 %collective-permute-start = (bf16[260,1024]{1,0:T(8,128)(2,1)}, bf16[260,1024]{1,0:T(8,128)(2,1)S(1)}, u32[]{:S(2)}, u32[]{:S(2)}) collective-permute-start(bf16[260,1024]{1,0:T(8,128)(2,1)} %pad_maximum_fusion.1), channel_id=1, source_target_pairs={{0,8},{8,16},{16,24},{24,32},{32,40},{40,48},{48,56},{56,64},{64,7... | collective-permute-start | bytes 1597448 | tf_op jit(solution)/shard_map/ppermute | solution.py:10
  8.1 0.9 pad_maximum_fusion.2
  9.1 1.3 collective-permute-start.1
  10.4 0.3 rev.6
  10.7 0.7 select_bitcast_fusion.2
  11.5 8.4 %collective-permute-done = bf16[260,1024]{1,0:T(8,128)(2,1)S(1)} collective-permute-done((bf16[260,1024]{1,0:T(8,128)(2,1)}, bf16[260,1024]{1,0:T(8,128)(2,1)S(1)}, u32[]{:S(2)}, u32[]{:S(2)}) %collective-permute-start) | collective-permute-done | bytes 532512 | tf_op jit(solution)/shard_map/ppermute | solution.py:10
  19.9 0.1 fusion.54
  20.0 4.9 %collective-permute-done.1 = bf16[262,1024]{1,0:T(8,128)(2,1)S(1)} collective-permute-done((bf16[262,1024]{1,0:T(8,128)(2,1)}, bf16[262,1024]{1,0:T(8,128)(2,1)S(1)}, u32[]{:S(2)}, u32[]{:S(2)}) %collective-permute-start.1) | collective-permute-done | bytes 536608 | tf_op jit(solution)/shard_map/ppermute | solution.py:10
  24.9 0.1 fusion.56
  25.0 0.2 maximum_convert_fusion
  25.2 0.4 maximum_convert_fusion.1
  25.7 0.6 copy-done.10
  26.3 2.7 %select_bitcast_fusion.1 = (bf16[1,385,1024]{2,1,0:T(8,128)(2,1)S(1)}, bf16[385,1024]{1,0:T(8,128)(2,1)S(1)}, f32[385,1024]{1,0:T(8,128)S(1)}, bf16[385,1024]{1,...) fusion(pred[]{:T(512)S(6)} %eq.3, bf16[129,1024]{1,0:T(8,128)(2,1)S(1)} %get-tuple-element.31, ...), kind=kLoop, calls=%fused_computation.75 | loop fusion | flops 9461760 | bytes 22114304 | tf_op jit(solution)/shard_map/broadcast_in_dim | solution.py:46
  29.0 14.5 %fusion.10 = f32[1,258,1024]{2,0,1:T(1,128)S(1)} fusion(bf16[1,385,1024]{2,1,0:T(8,128)(2,1)S(1)} %get-tuple-element.16, bf16[128,1,1024]{2,0,1:T(8,128)(2,1)S(1)} %get-tuple-element.33), kind=kOutput, calls=%fused_computation.26 | convolution fusion | flops 67633152 | bytes 2107392 | tf_op jit(solution)/shard_map/conv_general_dilated | solution.py:45
  43.4 0.5 fusion.36
  44.0 0.5 broadcast_select_fusion
  44.5 0.5 copy-done
  45.0 15.7 %collective-permute-start.2 = (bf16[256,1024]{1,0:T(8,128)(2,1)S(1)}, bf16[256,1024]{1,0:T(8,128)(2,1)S(1)}, u32[]{:S(2)}, u32[]{:S(2)}) collective-permute-start(bf16[256,1024]{1,0:T(8,128)(2,1)S(1)} %get-tuple-element.11), channel_id=1, source_target_pairs={{0,256},{256,0},{1,257},{257,1},{2,258},{258,2},{3,259},{259,3},{4... | collective-permute-start | bytes 1572872 | tf_op jit(solution)/shard_map/ppermute | solution.py:107
  60.7 0.1 slice_select_fusion.5
  60.8 2.9 %collective-permute-start.3 = (bf16[129,1024]{1,0:T(8,128)(2,1)S(1)}, bf16[129,1024]{1,0:T(8,128)(2,1)S(1)}, u32[]{:S(2)}, u32[]{:S(2)}) collective-permute-start(bf16[129,1024]{1,0:T(8,128)(2,1)S(1)} %slice_select_fusion.5), channel_id=1, source_target_pairs={{0,264},{8,272},{16,280},{24,288},{32,296},{40,304},{48,312},{56,3... | collective-permute-start | bytes 792584 | tf_op jit(solution)/shard_map/ppermute | solution.py:111
  63.7 0.7 collective-permute-start.4
  64.4 23.1 %collective-permute-done.3 = bf16[129,1024]{1,0:T(8,128)(2,1)S(1)} collective-permute-done((bf16[129,1024]{1,0:T(8,128)(2,1)S(1)}, bf16[129,1024]{1,0:T(8,128)(2,1)S(1)}, u32[]{:S(2)}, u32[]{:S(2)}) %collective-permute-start.3) | collective-permute-done | bytes 264224 | tf_op jit(solution)/shard_map/ppermute | solution.py:111
  87.5 0.1 slice.347
  87.6 0.2 maximum_convert_fusion.3
  87.8 2.4 %select_bitcast_fusion = (bf16[1,385,1024]{2,1,0:T(8,128)(2,1)}, bf16[385,1024]{1,0:T(8,128)(2,1)S(1)}, f32[385,1024]{1,0:T(8,128)}, bf16[385,1024]{1,0:T(8,128)(2,1)S(1)}) fusion(pred[]{:T(512)S(6)} %eq.3, f32[385,1024]{1,0:T(8,128)S(1)} %get-tuple-element.21, f32[387,1024]{1,0:T(8,128)S(1)} %maximum_convert_fusion.3, f32[1024]{0:T(1024)S(1)} %bitcast.71, ...), kind=kLoop, calls=%fused_computation.74 | loop fusion | flops 6307840 | bytes 12627969 | tf_op jit(solution)/shard_map/broadcast_in_dim | solution.py:46
  90.2 0.1 fusion.44
  90.2 0.1 fusion.31
  90.3 0.8 copy-done.2
  91.1 0.3 copy-done.8
  91.4 13.9 %fusion.12 = f32[1,128,1024]{2,0,1:T(1,128)S(1)} fusion(bf16[1,383,1024]{2,1,0:T(8,128)(2,1)S(1)} %fusion.31, bf16[256,1,1024]{2,0,1:T(8,128)(2,1)S(1)} %fusion.44), kind=kOutput, calls=%fused_computation.28 | convolution fusion | flops 67108864 | bytes 1832960 | tf_op jit(solution)/shard_map/conv_general_dilated | solution.py:45
  105.2 0.9 copy.46
  106.1 4.7 %rev.7 = f32[128,1024]{1,0:T(8,128)} reverse(f32[128,1024]{1,0:T(8,128)} %bitcast.61), dimensions={0} | reverse | bytes 1048576 | tf_op jit(solution)/shard_map/rev | solution.py:147
  110.9 2.0 reshape.41
  112.9 70.1 %all-to-all-start = ((f32[32,4,1024]{2,1,0:T(4,128)}), f32[32,4,1024]{2,1,0:T(4,128)}, u32[]{:S(2)}, u32[]{:S(2)}) async-start(f32[32,4,1024]{2,1,0:T(4,128)} %reshape.41), calls=%async_computation | async-start | bytes 1048576 | tf_op jit(solution)/shard_map/all_to_all | solution.py:40
  183.1 15.6 %fusion.8 = f32[1,258,1024]{2,0,1:T(1,128)S(1)} fusion(bf16[1,385,1024]{2,1,0:T(8,128)(2,1)} %get-tuple-element.7, bf16[128,1,1024]{2,0,1:T(8,128)(2,1)} %get-tuple-element.32), kind=kOutput, calls=%fused_computation.24 | convolution fusion | flops 67633152 | bytes 2107392 | tf_op jit(solution)/shard_map/conv_general_dilated | solution.py:45
  198.8 1.0 fusion.38
  199.8 1.1 fusion.41
  200.9 1.1 fusion.42
  202.0 1.1 fusion.43
  203.2 0.9 fusion.40
  204.1 8.5 %all-to-all-done = f32[32,4,1024]{2,1,0:T(4,128)} async-done(((f32[32,4,1024]{2,1,0:T(4,128)}), f32[32,4,1024]{2,1,0:T(4,128)}, u32[]{:S(2)}, u32[]{:S(2)}) %all-to-all-start) | async-done | bytes 524320 | tf_op jit(solution)/shard_map/all_to_all | solution.py:40
  212.6 1.7 reduce_sum.9
  (43 shorter events, 0.2 us)
Async XLA Ops:
  0.6 7.5 %slice-start.1 = ((bf16[256,1024]{1,0:T(8,128)(2,1)}), bf16[2,1024]{1,0:T(2,128)(2,1)S(1)}, s32[]{:S(2)}) async-start(bf16[256,1024]{1,0:T(8,128)(2,1)} %param.9), calls=%async_computation.2 | async-start | bytes 8192 | tf_op jit(solution)/shard_map/slice | solution.py:87
  0.6 7.5 %copy-start.13 = (bf16[1,256,1024]{2,1,0:T(8,128)(2,1)S(1)}, bf16[1,256,1024]{2,1,0:T(8,128)(2,1)}, u32[]{:S(2)}) copy-start(bf16[1,256,1024]{2,1,0:T(8,128)(2,1)} %param.8) | copy-start | bytes 1572868
  0.7 7.4 %copy-start.14 = (bf16[1,256,1024]{2,1,0:T(8,128)(2,1)S(1)}, bf16[1,256,1024]{2,1,0:T(8,128)(2,1)}, u32[]{:S(2)}) copy-start(bf16[1,256,1024]{2,1,0:T(8,128)(2,1)} %param.7) | copy-start | bytes 1572868
  0.7 7.5 %slice-start = ((bf16[256,1024]{1,0:T(8,128)(2,1)}), bf16[129,1024]{1,0:T(8,128)(2,1)S(1)}, s32[]{:S(2)}) async-start(bf16[256,1024]{1,0:T(8,128)(2,1)} %param.10), calls=%async_computation.1 | async-start | bytes 557056 | tf_op jit(solution)/shard_map/slice | solution.py:87
  3.6 6.8 %copy-start.16 = (f32[1,3,3,1024]{3,0,2,1:T(1,128)S(1)}, f32[1,3,3,1024]{3,0,2,1:T(1,128)}, u32[]{:S(2)}) copy-start(f32[1,3,3,1024]{3,0,2,1:T(1,128)} %param.11) | copy-start | bytes 110596
  3.6 6.8 %copy-start.15 = (bf16[1,128,1024]{2,1,0:T(8,128)(2,1)S(1)}, bf16[1,128,1024]{2,1,0:T(8,128)(2,1)}, u32[]{:S(2)}) copy-start(bf16[1,128,1024]{2,1,0:T(8,128)(2,1)} %param.12) | copy-start | bytes 786436
  4.6 15.3 %collective-permute-start = (bf16[260,1024]{1,0:T(8,128)(2,1)}, bf16[260,1024]{1,0:T(8,128)(2,1)S(1)}, u32[]{:S(2)}, u32[]{:S(2)}) collective-permute-start(bf16[260,1024]{1,0:T(8,128)(2,1)} %pad_maximum_fusion.1), channel_id=1, source_target_pairs={{0,8},{8,16},{16,24},{24,32},{32,40},{40,48},{48,56},{56,64},{64,7... | collective-permute-start | bytes 1597448 | tf_op jit(solution)/shard_map/ppermute | solution.py:10
  9.1 15.8 %collective-permute-start.1 = (bf16[262,1024]{1,0:T(8,128)(2,1)}, bf16[262,1024]{1,0:T(8,128)(2,1)S(1)}, u32[]{:S(2)}, u32[]{:S(2)}) collective-permute-start(bf16[262,1024]{1,0:T(8,128)(2,1)} %pad_maximum_fusion.2), channel_id=1, source_target_pairs={{8,0},{16,8},{24,16},{32,24},{40,32},{48,40},{56,48},{64,56},{72,6... | collective-permute-start | bytes 1609736 | tf_op jit(solution)/shard_map/ppermute | solution.py:10
  20.0 5.2 %copy-start.12 = (bf16[256,1024]{1,0:T(8,128)(2,1)S(1)}, bf16[256,1024]{1,0:T(8,128)(2,1)}, u32[]{:S(2)}) copy-start(bf16[256,1024]{1,0:T(8,128)(2,1)} %param.9) | copy-start | bytes 1572868
  25.2 1.0 copy-start.10
  29.0 14.5 %copy-start.17 = (f32[1,1024]{1,0:T(1,128)S(1)}, f32[1,1024]{1,0:T(1,128)}, u32[]{:S(2)}) copy-start(f32[1,1024]{1,0:T(1,128)} %param.13) | copy-start | bytes 12292
  44.0 1.0 copy-start
  45.0 42.6 %collective-permute-start.2 = (bf16[256,1024]{1,0:T(8,128)(2,1)S(1)}, bf16[256,1024]{1,0:T(8,128)(2,1)S(1)}, u32[]{:S(2)}, u32[]{:S(2)}) collective-permute-start(bf16[256,1024]{1,0:T(8,128)(2,1)S(1)} %get-tuple-element.11), channel_id=1, source_target_pairs={{0,256},{256,0},{1,257},{257,1},{2,258},{258,2},{3,259},{259,3},{4... | collective-permute-start | bytes 1572872 | tf_op jit(solution)/shard_map/ppermute | solution.py:107
  60.8 26.7 %collective-permute-start.3 = (bf16[129,1024]{1,0:T(8,128)(2,1)S(1)}, bf16[129,1024]{1,0:T(8,128)(2,1)S(1)}, u32[]{:S(2)}, u32[]{:S(2)}) collective-permute-start(bf16[129,1024]{1,0:T(8,128)(2,1)S(1)} %slice_select_fusion.5), channel_id=1, source_target_pairs={{0,264},{8,272},{16,280},{24,288},{32,296},{40,304},{48,312},{56,3... | collective-permute-start | bytes 792584 | tf_op jit(solution)/shard_map/ppermute | solution.py:111
  63.7 23.9 %collective-permute-start.4 = (bf16[2,1024]{1,0:T(2,128)(2,1)S(1)}, bf16[2,1024]{1,0:T(2,128)(2,1)S(1)}, u32[]{:S(2)}, u32[]{:S(2)}) collective-permute-start(bf16[2,1024]{1,0:T(2,128)(2,1)S(1)} %slice.346), channel_id=1, source_target_pairs={{8,256},{16,264},{24,272},{32,280},{40,288},{48,296},{56,304},{64,... | collective-permute-start | bytes 12296 | tf_op jit(solution)/shard_map/ppermute | solution.py:120
  87.6 2.6 %copy-start.4 = (bf16[256,1024]{1,0:T(8,128)(2,1)}, bf16[256,1024]{1,0:T(8,128)(2,1)S(1)}, u32[]{:S(2)}) copy-start(bf16[256,1024]{1,0:T(8,128)(2,1)S(1)} %collective-permute-done.2) | copy-start | bytes 1572868
  90.2 0.9 copy-start.2
  90.2 1.2 copy-start.8
  112.9 99.7 %all-to-all-start = ((f32[32,4,1024]{2,1,0:T(4,128)}), f32[32,4,1024]{2,1,0:T(4,128)}, u32[]{:S(2)}, u32[]{:S(2)}) async-start(f32[32,4,1024]{2,1,0:T(4,128)} %reshape.41), calls=%async_computation | async-start | bytes 1048576 | tf_op jit(solution)/shard_map/all_to_all | solution.py:40
  183.0 15.7 %copy-start.1 = (f32[258,1024]{1,0:T(8,128)S(1)}, f32[258,1024]{1,0:T(8,128)}, u32[]{:S(2)}) copy-start(f32[258,1024]{1,0:T(8,128)} %copy-done) | copy-start | bytes 3170308
  183.0 15.7 %copy-start.3 = (bf16[385,1024]{1,0:T(8,128)(2,1)S(1)}, bf16[385,1024]{1,0:T(8,128)(2,1)}, u32[]{:S(2)}) copy-start(bf16[385,1024]{1,0:T(8,128)(2,1)} %copy-done.2) | copy-start | bytes 2365444
  183.0 15.7 %copy-start.5 = (bf16[256,1024]{1,0:T(8,128)(2,1)S(1)}, bf16[256,1024]{1,0:T(8,128)(2,1)}, u32[]{:S(2)}) copy-start(bf16[256,1024]{1,0:T(8,128)(2,1)} %copy-done.4) | copy-start | bytes 1572868
  183.0 15.7 %copy-start.6 = (f32[385,1024]{1,0:T(8,128)S(1)}, f32[385,1024]{1,0:T(8,128)}, u32[]{:S(2)}) copy-start(f32[385,1024]{1,0:T(8,128)} %get-tuple-element.9) | copy-start | bytes 4730884
  183.1 15.7 %copy-start.7 = (f32[385,1024]{1,0:T(8,128)S(1)}, f32[385,1024]{1,0:T(8,128)}, u32[]{:S(2)}) copy-start(f32[385,1024]{1,0:T(8,128)} %get-tuple-element.20) | copy-start | bytes 4730884
  183.1 15.7 %copy-start.9 = (bf16[385,1024]{1,0:T(8,128)(2,1)S(1)}, bf16[385,1024]{1,0:T(8,128)(2,1)}, u32[]{:S(2)}) copy-start(bf16[385,1024]{1,0:T(8,128)(2,1)} %copy-done.8) | copy-start | bytes 2365444
  183.1 15.7 %copy-start.11 = (bf16[256,1024]{1,0:T(8,128)(2,1)S(1)}, bf16[256,1024]{1,0:T(8,128)(2,1)}, u32[]{:S(2)}) copy-start(bf16[256,1024]{1,0:T(8,128)(2,1)} %param.10) | copy-start | bytes 1572868

commit v8 on v4

--- a/solution.py
+++ b/solution.py
@@ -37,8 +37,8 @@
         return lax.psum_scatter(part, axis, scatter_dimension=0, tiled=True)
     rows = part.shape[0] // peers
     pieces = part.reshape((peers, rows) + part.shape[1:])
-    got = lax.all_to_all(pieces, axis, 0, 0)
-    return jnp.sum(got, axis=0)
+    got = lax.all_to_all(pieces.astype(jnp.bfloat16), axis, 0, 0)
+    return jnp.sum(got.astype(jnp.float32), axis=0)
 
 
 def depthwise(source, kernel):

time: 189 us -> 182 us (0.963)
  waiting for transfers between devices: 39.5 us -> 32.4 us
    all_to_all x1, waiting for transfers between devices: 7.14 us -> 0.01 us  [exchange_scatter(): got = lax.all_to_all(pieces.astype(jnp.bfloat16), axis, 0, 0)]
    reshape x1 -> x0, local copies, waits for them, and re-layouts: 2.02 us -> none  [exchange_scatter(): pieces = part.reshape((peers, rows) + part.shape[1:])]
  transfers between devices with their start and end apart: 6 -> 6, of which waited for: 6 -> 5; matrix products, arithmetic and copies ran while one was open for 12% -> 13% of each run, Pallas kernels for 0% -> 0%
where the time goes in v8:
time: 182 us; the launch traced here: 181 us
  starting transfers between devices  73.9 us (41%)
  matrix products  44 us (24%)
  waiting for transfers between devices  32.4 us (18%)
  other arithmetic  16.6 us (9%)
  local copies, waits for them, and re-layouts  12.8 us (7%)
    all_to_all x1, starting transfers between devices, exchange_scatter(): got = lax.all_to_all(pieces.astype(jnp.bfloat16), axis, 0, 0)  47.6 us
    conv_general_dilated x3, matrix products, depthwise(): lax.conv_general_dilated(source[None], kernel[:, None, :], (1,), 'VALID',...  44 us
    ppermute x4, waiting for transfers between devices, shifted(): return lax.ppermute(value, axis, pairs)  17.2 us
    ppermute x1, starting transfers between devices, body(): lax.ppermute(jnp.where(first, out_first, gin_last), 'section', [(0, 1), (...  15.7 us
    ppermute x1, waiting for transfers between devices, body(): lax.ppermute(jnp.where(first, out_first, gin_last), 'section', [(0, 1), (...  15.1 us
    ppermute x4, starting transfers between devices, shifted(): return lax.ppermute(value, axis, pairs)  10.6 us
    broadcast_in_dim x3, other arithmetic, depthwise(): source[None]  5.08 us
    rev x1, local copies, waits for them, and re-layouts, body(): taps_part = depthwise(u[:rows + extent - 1], gz[:rows])[::-1]  4.37 us
  transfers between devices with their start and end apart: 6, of which 5 were waited for; matrix products, arithmetic and copies ran while one was open for 13% of the time, Pallas kernels for 0%

profile of v8, /device:TPU:6, one launch (start us, length us, event | category | flops | bytes accessed | tf_op | source)
XLA Modules:
  0.0 180.8 jit_solution(4914482178786783000)
XLA Ops:
  0.6 0.0 slice-start.1
  0.7 0.0 slice-start
  0.7 1.1 slice.250
  1.8 1.0 slice_bitcast_fusion.1
  2.8 0.7 slice_bitcast_fusion.3
  3.6 1.0 pad_maximum_fusion.3
  4.6 3.5 %collective-permute-start = (bf16[260,1024]{1,0:T(8,128)(2,1)}, bf16[260,1024]{1,0:T(8,128)(2,1)S(1)}, u32[]{:S(2)}, u32[]{:S(2)}) collective-permute-start(bf16[260,1024]{1,0:T(8,128)(2,1)} %pad_maximum_fusion.3), channel_id=1, source_target_pairs={{0,8},{8,16},{16,24},{24,32},{32,40},{40,48},{48,56},{56,64},{64,7... | collective-permute-start | bytes 1597448 | tf_op jit(solution)/shard_map/ppermute | solution.py:10
  8.1 0.9 pad_maximum_fusion.4
  9.1 1.3 collective-permute-start.1
  10.4 0.3 rev.6
  10.7 0.7 select_bitcast_fusion.2
  11.5 8.4 %collective-permute-done = bf16[260,1024]{1,0:T(8,128)(2,1)S(1)} collective-permute-done((bf16[260,1024]{1,0:T(8,128)(2,1)}, bf16[260,1024]{1,0:T(8,128)(2,1)S(1)}, u32[]{:S(2)}, u32[]{:S(2)}) %collective-permute-start) | collective-permute-done | bytes 532512 | tf_op jit(solution)/shard_map/ppermute | solution.py:10
  19.9 0.1 fusion.54
  20.0 4.9 %collective-permute-done.1 = bf16[262,1024]{1,0:T(8,128)(2,1)S(1)} collective-permute-done((bf16[262,1024]{1,0:T(8,128)(2,1)}, bf16[262,1024]{1,0:T(8,128)(2,1)S(1)}, u32[]{:S(2)}, u32[]{:S(2)}) %collective-permute-start.1) | collective-permute-done | bytes 536608 | tf_op jit(solution)/shard_map/ppermute | solution.py:10
  24.9 0.1 fusion.56
  25.0 0.2 maximum_convert_fusion
  25.2 0.4 maximum_convert_fusion.1
  25.7 0.6 copy-done.10
  26.3 2.7 %select_bitcast_fusion.1 = (bf16[1,385,1024]{2,1,0:T(8,128)(2,1)S(1)}, bf16[385,1024]{1,0:T(8,128)(2,1)S(1)}, f32[385,1024]{1,0:T(8,128)S(1)}, bf16[385,1024]{1,...) fusion(pred[]{:T(512)S(6)} %eq.3, bf16[129,1024]{1,0:T(8,128)(2,1)S(1)} %get-tuple-element.28, ...), kind=kLoop, calls=%fused_computation.77 | loop fusion | flops 9461760 | bytes 22114304 | tf_op jit(solution)/shard_map/broadcast_in_dim | solution.py:46
  29.0 14.5 %fusion.10 = f32[1,258,1024]{2,0,1:T(1,128)S(1)} fusion(bf16[1,385,1024]{2,1,0:T(8,128)(2,1)S(1)} %get-tuple-element.13, bf16[128,1,1024]{2,0,1:T(8,128)(2,1)S(1)} %get-tuple-element.30), kind=kOutput, calls=%fused_computation.26 | convolution fusion | flops 67633152 | bytes 2107392 | tf_op jit(solution)/shard_map/conv_general_dilated | solution.py:45
  43.4 0.6 fusion.37
  44.0 0.4 fusion.41
  44.4 0.6 copy-done
  45.0 15.7 %collective-permute-start.2 = (bf16[256,1024]{1,0:T(8,128)(2,1)S(1)}, bf16[256,1024]{1,0:T(8,128)(2,1)S(1)}, u32[]{:S(2)}, u32[]{:S(2)}) collective-permute-start(bf16[256,1024]{1,0:T(8,128)(2,1)S(1)} %fusion.41), channel_id=1, source_target_pairs={{0,256},{256,0},{1,257},{257,1},{2,258},{258,2},{3,259},{259,3},{4... | collective-permute-start | bytes 1572872 | tf_op jit(solution)/shard_map/ppermute | solution.py:107
  60.7 15.1 %collective-permute-done.2 = bf16[256,1024]{1,0:T(8,128)(2,1)S(1)} collective-permute-done((bf16[256,1024]{1,0:T(8,128)(2,1)S(1)}, bf16[256,1024]{1,0:T(8,128)(2,1)S(1)}, u32[]{:S(2)}, u32[]{:S(2)}) %collective-permute-start.2) | collective-permute-done | bytes 524320 | tf_op jit(solution)/shard_map/ppermute | solution.py:107
  75.9 0.1 fusion.57
  75.9 1.3 collective-permute-start.3
  77.2 4.6 %collective-permute-start.4 = (bf16[129,1024]{1,0:T(8,128)(2,1)S(1)}, bf16[129,1024]{1,0:T(8,128)(2,1)S(1)}, u32[]{:S(2)}, u32[]{:S(2)}) collective-permute-start(bf16[129,1024]{1,0:T(8,128)(2,1)S(1)} %get-tuple-element.31), channel_id=1, source_target_pairs={{0,8},{8,16},{16,24},{24,32},{32,40},{40,48},{48,56},{56,64},{64,7... | collective-permute-start | bytes 792584 | tf_op jit(solution)/shard_map/ppermute | solution.py:10
  81.9 2.5 %collective-permute-done.3 = bf16[129,1024]{1,0:T(8,128)(2,1)S(1)} collective-permute-done((bf16[129,1024]{1,0:T(8,128)(2,1)S(1)}, bf16[129,1024]{1,0:T(8,128)(2,1)S(1)}, u32[]{:S(2)}, u32[]{:S(2)}) %collective-permute-start.3) | collective-permute-done | bytes 264224 | tf_op jit(solution)/shard_map/ppermute | solution.py:10
  84.4 1.4 collective-permute-done.4
  85.8 0.2 fusion.31
  86.0 2.3 %select_bitcast_fusion = (bf16[1,385,1024]{2,1,0:T(8,128)(2,1)}, bf16[385,1024]{1,0:T(8,128)(2,1)S(1)}, f32[385,1024]{1,0:T(8,128)}, bf16[385,1024]{1,0:T(8,128)(2,1)S(1)}) fusion(pred[]{:T(512)S(6)} %eq.3, f32[385,1024]{1,0:T(8,128)S(1)} %get-tuple-element.18, f32[387,1024]{1,0:T(8,128)S(1)} %fusion.31, f32[1024]{0:T(1024)S(1)} %bitcast.71, ...), kind=kLoop, calls=%fused_computation.76 | loop fusion | flops 4336640 | bytes 12627969 | tf_op jit(solution)/shard_map/broadcast_in_dim | solution.py:46
  88.3 0.1 fusion.46
  88.4 0.1 fusion.32
  88.5 0.7 copy-done.2
  89.2 0.3 copy-done.6
  89.5 13.9 %fusion.12 = bf16[1,128,1024]{2,0,1:T(2,128)(2,1)S(1)} fusion(bf16[1,383,1024]{2,1,0:T(8,128)(2,1)S(1)} %fusion.32, bf16[256,1,1024]{2,0,1:T(8,128)(2,1)S(1)} %fusion.46), kind=kOutput, calls=%fused_computation.28 | convolution fusion | flops 67108864 | bytes 1570816 | tf_op jit(solution)/shard_map/conv_general_dilated | solution.py:45
  103.5 0.8 copy.46
  104.3 4.4 %rev.7 = bf16[128,1024]{1,0:T(8,128)(2,1)} reverse(bf16[128,1024]{1,0:T(8,128)(2,1)} %bitcast.63), dimensions={0} | reverse | bytes 524288 | tf_op jit(solution)/shard_map/rev | solution.py:134
  108.6 1.8 convert_element_type.118
  110.4 47.6 %all-to-all-start = ((bf16[32,4,1024]{2,1,0:T(4,128)(2,1)}), bf16[32,4,1024]{2,1,0:T(4,128)(2,1)}, u32[]{:S(2)}, u32[]{:S(2)}) async-start(bf16[32,4,1024]{2,1,0:T(4,128)(2,1)} %convert_element_type.118), calls=%async_computation | async-start | bytes 524288 | tf_op jit(solution)/shard_map/all_to_all | solution.py:40
  158.0 15.6 %fusion.8 = f32[1,258,1024]{2,0,1:T(1,128)S(1)} fusion(bf16[1,385,1024]{2,1,0:T(8,128)(2,1)} %get-tuple-element.7, bf16[128,1,1024]{2,0,1:T(8,128)(2,1)} %get-tuple-element.29), kind=kOutput, calls=%fused_computation.24 | convolution fusion | flops 67633152 | bytes 2107392 | tf_op jit(solution)/shard_map/conv_general_dilated | solution.py:45
  173.7 1.1 fusion.39
  174.8 1.1 fusion.43
  175.9 1.1 fusion.44
  177.0 1.1 fusion.45
  178.1 0.9 fusion.42
  179.1 1.7 convert_reduce_fusion
  (42 shorter events, 0.2 us)
Async XLA Ops:
  0.6 7.5 %slice-start.1 = ((bf16[256,1024]{1,0:T(8,128)(2,1)}), bf16[2,1024]{1,0:T(2,128)(2,1)S(1)}, s32[]{:S(2)}) async-start(bf16[256,1024]{1,0:T(8,128)(2,1)} %param.9), calls=%async_computation.2 | async-start | bytes 8192 | tf_op jit(solution)/shard_map/slice | solution.py:87
  0.6 7.5 %copy-start.13 = (bf16[1,256,1024]{2,1,0:T(8,128)(2,1)S(1)}, bf16[1,256,1024]{2,1,0:T(8,128)(2,1)}, u32[]{:S(2)}) copy-start(bf16[1,256,1024]{2,1,0:T(8,128)(2,1)} %param.8) | copy-start | bytes 1572868
  0.7 7.4 %copy-start.14 = (bf16[1,256,1024]{2,1,0:T(8,128)(2,1)S(1)}, bf16[1,256,1024]{2,1,0:T(8,128)(2,1)}, u32[]{:S(2)}) copy-start(bf16[1,256,1024]{2,1,0:T(8,128)(2,1)} %param.7) | copy-start | bytes 1572868
  0.7 7.5 %slice-start = ((bf16[256,1024]{1,0:T(8,128)(2,1)}), bf16[129,1024]{1,0:T(8,128)(2,1)S(1)}, s32[]{:S(2)}) async-start(bf16[256,1024]{1,0:T(8,128)(2,1)} %param.10), calls=%async_computation.1 | async-start | bytes 557056 | tf_op jit(solution)/shard_map/slice | solution.py:87
  3.6 6.8 %copy-start.16 = (f32[1,3,3,1024]{3,0,2,1:T(1,128)S(1)}, f32[1,3,3,1024]{3,0,2,1:T(1,128)}, u32[]{:S(2)}) copy-start(f32[1,3,3,1024]{3,0,2,1:T(1,128)} %param.11) | copy-start | bytes 110596
  3.6 6.8 %copy-start.15 = (bf16[1,128,1024]{2,1,0:T(8,128)(2,1)S(1)}, bf16[1,128,1024]{2,1,0:T(8,128)(2,1)}, u32[]{:S(2)}) copy-start(bf16[1,128,1024]{2,1,0:T(8,128)(2,1)} %param.12) | copy-start | bytes 786436
  4.6 15.3 %collective-permute-start = (bf16[260,1024]{1,0:T(8,128)(2,1)}, bf16[260,1024]{1,0:T(8,128)(2,1)S(1)}, u32[]{:S(2)}, u32[]{:S(2)}) collective-permute-start(bf16[260,1024]{1,0:T(8,128)(2,1)} %pad_maximum_fusion.3), channel_id=1, source_target_pairs={{0,8},{8,16},{16,24},{24,32},{32,40},{40,48},{48,56},{56,64},{64,7... | collective-permute-start | bytes 1597448 | tf_op jit(solution)/shard_map/ppermute | solution.py:10
  9.1 15.8 %collective-permute-start.1 = (bf16[262,1024]{1,0:T(8,128)(2,1)}, bf16[262,1024]{1,0:T(8,128)(2,1)S(1)}, u32[]{:S(2)}, u32[]{:S(2)}) collective-permute-start(bf16[262,1024]{1,0:T(8,128)(2,1)} %pad_maximum_fusion.4), channel_id=1, source_target_pairs={{8,0},{16,8},{24,16},{32,24},{40,32},{48,40},{56,48},{64,56},{72,6... | collective-permute-start | bytes 1609736 | tf_op jit(solution)/shard_map/ppermute | solution.py:10
  20.0 5.2 %copy-start.12 = (bf16[256,1024]{1,0:T(8,128)(2,1)S(1)}, bf16[256,1024]{1,0:T(8,128)(2,1)}, u32[]{:S(2)}) copy-start(bf16[256,1024]{1,0:T(8,128)(2,1)} %param.9) | copy-start | bytes 1572868
  25.2 1.0 copy-start.10
  29.0 14.5 %copy-start.17 = (f32[1,1024]{1,0:T(1,128)S(1)}, f32[1,1024]{1,0:T(1,128)}, u32[]{:S(2)}) copy-start(f32[1,1024]{1,0:T(1,128)} %param.13) | copy-start | bytes 12292
  44.0 1.0 copy-start
  45.0 30.9 %collective-permute-start.2 = (bf16[256,1024]{1,0:T(8,128)(2,1)S(1)}, bf16[256,1024]{1,0:T(8,128)(2,1)S(1)}, u32[]{:S(2)}, u32[]{:S(2)}) collective-permute-start(bf16[256,1024]{1,0:T(8,128)(2,1)S(1)} %fusion.41), channel_id=1, source_target_pairs={{0,256},{256,0},{1,257},{257,1},{2,258},{258,2},{3,259},{259,3},{4... | collective-permute-start | bytes 1572872 | tf_op jit(solution)/shard_map/ppermute | solution.py:107
  75.9 8.4 %collective-permute-start.3 = (bf16[129,1024]{1,0:T(8,128)(2,1)S(1)}, bf16[129,1024]{1,0:T(8,128)(2,1)S(1)}, u32[]{:S(2)}, u32[]{:S(2)}) collective-permute-start(bf16[129,1024]{1,0:T(8,128)(2,1)S(1)} %get-tuple-element.32), channel_id=1, source_target_pairs={{8,0},{16,8},{24,16},{32,24},{40,32},{48,40},{56,48},{64,56},{72,6... | collective-permute-start | bytes 792584 | tf_op jit(solution)/shard_map/ppermute | solution.py:10
  77.2 8.6 %collective-permute-start.4 = (bf16[129,1024]{1,0:T(8,128)(2,1)S(1)}, bf16[129,1024]{1,0:T(8,128)(2,1)S(1)}, u32[]{:S(2)}, u32[]{:S(2)}) collective-permute-start(bf16[129,1024]{1,0:T(8,128)(2,1)S(1)} %get-tuple-element.31), channel_id=1, source_target_pairs={{0,8},{8,16},{16,24},{24,32},{32,40},{40,48},{48,56},{56,64},{64,7... | collective-permute-start | bytes 792584 | tf_op jit(solution)/shard_map/ppermute | solution.py:10
  84.4 3.9 %copy-start.8 = (bf16[385,1024]{1,0:T(8,128)(2,1)}, bf16[385,1024]{1,0:T(8,128)(2,1)S(1)}, u32[]{:S(2)}) copy-start(bf16[385,1024]{1,0:T(8,128)(2,1)S(1)} %constant_dynamic-update-slice_fusion) | copy-start | bytes 2365444
  88.3 0.9 copy-start.2
  88.3 1.2 copy-start.6
  110.4 68.7 %all-to-all-start = ((bf16[32,4,1024]{2,1,0:T(4,128)(2,1)}), bf16[32,4,1024]{2,1,0:T(4,128)(2,1)}, u32[]{:S(2)}, u32[]{:S(2)}) async-start(bf16[32,4,1024]{2,1,0:T(4,128)(2,1)} %convert_element_type.118), calls=%async_computation | async-start | bytes 524288 | tf_op jit(solution)/shard_map/all_to_all | solution.py:40
  158.0 15.7 %copy-start.1 = (f32[258,1024]{1,0:T(8,128)S(1)}, f32[258,1024]{1,0:T(8,128)}, u32[]{:S(2)}) copy-start(f32[258,1024]{1,0:T(8,128)} %copy-done) | copy-start | bytes 3170308
  158.0 15.7 %copy-start.3 = (bf16[385,1024]{1,0:T(8,128)(2,1)S(1)}, bf16[385,1024]{1,0:T(8,128)(2,1)}, u32[]{:S(2)}) copy-start(bf16[385,1024]{1,0:T(8,128)(2,1)} %copy-done.2) | copy-start | bytes 2365444
  158.0 15.7 %copy-start.4 = (f32[385,1024]{1,0:T(8,128)S(1)}, f32[385,1024]{1,0:T(8,128)}, u32[]{:S(2)}) copy-start(f32[385,1024]{1,0:T(8,128)} %get-tuple-element.9) | copy-start | bytes 4730884
  158.0 15.7 %copy-start.5 = (f32[385,1024]{1,0:T(8,128)S(1)}, f32[385,1024]{1,0:T(8,128)}, u32[]{:S(2)}) copy-start(f32[385,1024]{1,0:T(8,128)} %get-tuple-element.17) | copy-start | bytes 4730884
  158.0 15.7 %copy-start.7 = (bf16[385,1024]{1,0:T(8,128)(2,1)S(1)}, bf16[385,1024]{1,0:T(8,128)(2,1)}, u32[]{:S(2)}) copy-start(bf16[385,1024]{1,0:T(8,128)(2,1)} %copy-done.6) | copy-start | bytes 2365444
  158.0 15.7 %copy-start.9 = (bf16[385,1024]{1,0:T(8,128)(2,1)S(1)}, bf16[385,1024]{1,0:T(8,128)(2,1)}, u32[]{:S(2)}) copy-start(bf16[385,1024]{1,0:T(8,128)(2,1)} %copy-done.8) | copy-start | bytes 2365444
  158.0 15.7 %copy-start.11 = (bf16[256,1024]{1,0:T(8,128)(2,1)S(1)}, bf16[256,1024]{1,0:T(8,128)(2,1)}, u32[]{:S(2)}) copy-start(bf16[256,1024]{1,0:T(8,128)(2,1)} %param.10) | copy-start | bytes 1572868

commit v9 on v6

--- a/solution.py
+++ b/solution.py
@@ -37,8 +37,8 @@
         return lax.psum_scatter(part[::-1], axis, scatter_dimension=0, tiled=True)
     rows = part.shape[0] // peers
     pieces = part.reshape((peers, rows) + part.shape[1:])[::-1]
-    got = lax.all_to_all(pieces, axis, 0, 0)
-    return jnp.sum(got, axis=0)[::-1]
+    got = lax.all_to_all(pieces.astype(jnp.bfloat16), axis, 0, 0)
+    return jnp.sum(got.astype(jnp.float32), axis=0)[::-1]
 
 
 def depthwise(source, kernel):

time: 190 us -> 183 us (0.963)
  waiting for transfers between devices: 39.5 us -> 32.4 us
    all_to_all x1, waiting for transfers between devices: 7.14 us -> 0.01 us  [exchange_scatter(): got = lax.all_to_all(pieces.astype(jnp.bfloat16), axis, 0, 0)]
  transfers between devices with their start and end apart: 6 -> 6, of which waited for: 6 -> 5; matrix products, arithmetic and copies ran while one was open for 12% -> 13% of each run, Pallas kernels for 0% -> 0%
where the time goes in v9:
time: 183 us; the launch traced here: 182 us
  starting transfers between devices  73.9 us (40%)
  matrix products  46.9 us (26%)
  waiting for transfers between devices  32.4 us (18%)
  other arithmetic  15.9 us (9%)
  local copies, waits for them, and re-layouts  11.8 us (6%)
    all_to_all x1, starting transfers between devices, exchange_scatter(): got = lax.all_to_all(pieces.astype(jnp.bfloat16), axis, 0, 0)  47.6 us
    conv_general_dilated x3, matrix products, depthwise(): lax.conv_general_dilated(source[None], kernel[:, None, :], (1,), 'VALID',...  46.9 us
    ppermute x4, waiting for transfers between devices, shifted(): return lax.ppermute(value, axis, pairs)  17.2 us
    ppermute x1, starting transfers between devices, body(): lax.ppermute(jnp.where(first, out_first, gin_last), 'section', [(0, 1), (...  15.7 us
    ppermute x1, waiting for transfers between devices, body(): lax.ppermute(jnp.where(first, out_first, gin_last), 'section', [(0, 1), (...  15.1 us
    ppermute x4, starting transfers between devices, shifted(): return lax.ppermute(value, axis, pairs)  10.6 us
    broadcast_in_dim x3, other arithmetic, depthwise(): source[None]  5.04 us
  transfers between devices with their start and end apart: 6, of which 5 were waited for; matrix products, arithmetic and copies ran while one was open for 13% of the time, Pallas kernels for 0%

profile of v9, /device:TPU:6, one launch (start us, length us, event | category | flops | bytes accessed | tf_op | source)
XLA Modules:
  0.0 182.1 jit_solution(12802683934118811270)
XLA Ops:
  0.6 0.0 slice-start.1
  0.7 0.0 slice-start
  0.7 1.1 slice.250
  1.8 1.0 slice_bitcast_fusion.1
  2.8 0.7 slice_bitcast_fusion.3
  3.6 1.0 pad_maximum_fusion.3
  4.6 3.5 %collective-permute-start = (bf16[260,1024]{1,0:T(8,128)(2,1)}, bf16[260,1024]{1,0:T(8,128)(2,1)S(1)}, u32[]{:S(2)}, u32[]{:S(2)}) collective-permute-start(bf16[260,1024]{1,0:T(8,128)(2,1)} %pad_maximum_fusion.3), channel_id=1, source_target_pairs={{0,8},{8,16},{16,24},{24,32},{32,40},{40,48},{48,56},{56,64},{64,7... | collective-permute-start | bytes 1597448 | tf_op jit(solution)/shard_map/ppermute | solution.py:10
  8.1 0.9 pad_maximum_fusion.4
  9.0 1.3 collective-permute-start.1
  10.4 0.3 rev.9
  10.7 0.7 select_bitcast_fusion.2
  11.5 8.4 %collective-permute-done = bf16[260,1024]{1,0:T(8,128)(2,1)S(1)} collective-permute-done((bf16[260,1024]{1,0:T(8,128)(2,1)}, bf16[260,1024]{1,0:T(8,128)(2,1)S(1)}, u32[]{:S(2)}, u32[]{:S(2)}) %collective-permute-start) | collective-permute-done | bytes 532512 | tf_op jit(solution)/shard_map/ppermute | solution.py:10
  19.9 0.1 fusion.57
  20.0 4.9 %collective-permute-done.1 = bf16[262,1024]{1,0:T(8,128)(2,1)S(1)} collective-permute-done((bf16[262,1024]{1,0:T(8,128)(2,1)}, bf16[262,1024]{1,0:T(8,128)(2,1)S(1)}, u32[]{:S(2)}, u32[]{:S(2)}) %collective-permute-start.1) | collective-permute-done | bytes 536608 | tf_op jit(solution)/shard_map/ppermute | solution.py:10
  24.9 0.1 fusion.59
  24.9 0.2 maximum_convert_fusion
  25.2 0.4 maximum_convert_fusion.1
  25.7 0.6 copy-done.10
  26.2 2.7 %select_bitcast_fusion.1 = (bf16[1,385,1024]{2,1,0:T(8,128)(2,1)S(1)}, bf16[385,1024]{1,0:T(8,128)(2,1)S(1)}, f32[385,1024]{1,0:T(8,128)S(1)}, bf16[385,1024]{1,...) fusion(pred[]{:T(512)S(6)} %eq.3, bf16[129,1024]{1,0:T(8,128)(2,1)S(1)} %get-tuple-element.28, ...), kind=kLoop, calls=%fused_computation.78 | loop fusion | flops 9461760 | bytes 22114304 | tf_op jit(solution)/shard_map/broadcast_in_dim | solution.py:46
  28.9 14.5 %fusion.10 = f32[1,258,1024]{2,0,1:T(1,128)S(1)} fusion(bf16[1,385,1024]{2,1,0:T(8,128)(2,1)S(1)} %get-tuple-element.13, bf16[128,1,1024]{2,0,1:T(8,128)(2,1)S(1)} %get-tuple-element.30), kind=kOutput, calls=%fused_computation.26 | convolution fusion | flops 67633152 | bytes 2107392 | tf_op jit(solution)/shard_map/conv_general_dilated | solution.py:45
  43.4 0.6 fusion.40
  44.0 0.4 fusion.44
  44.4 0.6 copy-done
  45.0 15.7 %collective-permute-start.2 = (bf16[256,1024]{1,0:T(8,128)(2,1)S(1)}, bf16[256,1024]{1,0:T(8,128)(2,1)S(1)}, u32[]{:S(2)}, u32[]{:S(2)}) collective-permute-start(bf16[256,1024]{1,0:T(8,128)(2,1)S(1)} %fusion.44), channel_id=1, source_target_pairs={{0,256},{256,0},{1,257},{257,1},{2,258},{258,2},{3,259},{259,3},{4... | collective-permute-start | bytes 1572872 | tf_op jit(solution)/shard_map/ppermute | solution.py:107
  60.7 15.1 %collective-permute-done.2 = bf16[256,1024]{1,0:T(8,128)(2,1)S(1)} collective-permute-done((bf16[256,1024]{1,0:T(8,128)(2,1)S(1)}, bf16[256,1024]{1,0:T(8,128)(2,1)S(1)}, u32[]{:S(2)}, u32[]{:S(2)}) %collective-permute-start.2) | collective-permute-done | bytes 524320 | tf_op jit(solution)/shard_map/ppermute | solution.py:107
  75.8 0.1 fusion.60
  75.9 1.3 collective-permute-start.3
  77.2 4.6 %collective-permute-start.4 = (bf16[129,1024]{1,0:T(8,128)(2,1)S(1)}, bf16[129,1024]{1,0:T(8,128)(2,1)S(1)}, u32[]{:S(2)}, u32[]{:S(2)}) collective-permute-start(bf16[129,1024]{1,0:T(8,128)(2,1)S(1)} %get-tuple-element.31), channel_id=1, source_target_pairs={{0,8},{8,16},{16,24},{24,32},{32,40},{40,48},{48,56},{56,64},{64,7... | collective-permute-start | bytes 792584 | tf_op jit(solution)/shard_map/ppermute | solution.py:10
  81.8 2.5 %collective-permute-done.3 = bf16[129,1024]{1,0:T(8,128)(2,1)S(1)} collective-permute-done((bf16[129,1024]{1,0:T(8,128)(2,1)S(1)}, bf16[129,1024]{1,0:T(8,128)(2,1)S(1)}, u32[]{:S(2)}, u32[]{:S(2)}) %collective-permute-start.3) | collective-permute-done | bytes 264224 | tf_op jit(solution)/shard_map/ppermute | solution.py:10
  84.4 1.4 collective-permute-done.4
  85.8 0.2 fusion.34
  86.0 2.3 %select_bitcast_fusion = (bf16[1,385,1024]{2,1,0:T(8,128)(2,1)}, bf16[385,1024]{1,0:T(8,128)(2,1)S(1)}, f32[385,1024]{1,0:T(8,128)}, bf16[385,1024]{1,0:T(8,128)(2,1)S(1)}) fusion(pred[]{:T(512)S(6)} %eq.3, f32[385,1024]{1,0:T(8,128)S(1)} %get-tuple-element.18, f32[387,1024]{1,0:T(8,128)S(1)} %fusion.34, f32[1024]{0:T(1024)S(1)} %bitcast.67, ...), kind=kLoop, calls=%fused_computation.77 | loop fusion | flops 4336640 | bytes 12627969 | tf_op jit(solution)/shard_map/broadcast_in_dim | solution.py:46
  88.3 0.1 fusion.49
  88.4 0.1 fusion.35
  88.5 0.7 copy-done.2
  89.2 0.3 copy-done.6
  89.5 16.9 %fusion.14 = bf16[128,1024]{1,0:T(8,128)(2,1)} fusion(bf16[1,383,1024]{2,1,0:T(8,128)(2,1)S(1)} %fusion.35, bf16[256,1,1024]{2,0,1:T(8,128)(2,1)S(1)} %fusion.49), kind=kOutput, calls=%fused_computation.30 | convolution fusion | flops 67108864 | bytes 1570816 | tf_op jit(solution)/shard_map/conv_general_dilated | solution.py:45
  106.4 1.8 reshape_squeeze.3
  108.1 1.8 rev.13
  109.9 47.6 %all-to-all-start = ((bf16[32,4,1024]{2,1,0:T(4,128)(2,1)}), bf16[32,4,1024]{2,1,0:T(4,128)(2,1)}, u32[]{:S(2)}, u32[]{:S(2)}) async-start(bf16[32,4,1024]{2,1,0:T(4,128)(2,1)} %rev.13), calls=%async_computation | async-start | bytes 524288 | tf_op jit(solution)/shard_map/all_to_all | solution.py:40
  157.5 15.6 %fusion.8 = f32[1,258,1024]{2,0,1:T(1,128)S(1)} fusion(bf16[1,385,1024]{2,1,0:T(8,128)(2,1)} %get-tuple-element.7, bf16[128,1,1024]{2,0,1:T(8,128)(2,1)} %get-tuple-element.29), kind=kOutput, calls=%fused_computation.24 | convolution fusion | flops 67633152 | bytes 2107392 | tf_op jit(solution)/shard_map/conv_general_dilated | solution.py:45
  173.2 1.1 fusion.42
  174.3 1.1 fusion.46
  175.4 1.1 fusion.47
  176.5 1.1 fusion.48
  177.6 0.9 fusion.45
  178.6 1.1 convert_reduce_fusion
  179.7 2.4 %rev.11 = f32[4,1024]{1,0:T(4,128)} reverse(f32[4,1024]{1,0:T(4,128)S(1)} %convert_reduce_fusion), dimensions={0} | reverse | bytes 32768 | tf_op jit(solution)/shard_map/rev | solution.py:41
  (42 shorter events, 0.2 us)
Async XLA Ops:
  0.6 7.5 %slice-start.1 = ((bf16[256,1024]{1,0:T(8,128)(2,1)}), bf16[2,1024]{1,0:T(2,128)(2,1)S(1)}, s32[]{:S(2)}) async-start(bf16[256,1024]{1,0:T(8,128)(2,1)} %param.9), calls=%async_computation.2 | async-start | bytes 8192 | tf_op jit(solution)/shard_map/slice | solution.py:87
  0.6 7.5 %copy-start.13 = (bf16[1,256,1024]{2,1,0:T(8,128)(2,1)S(1)}, bf16[1,256,1024]{2,1,0:T(8,128)(2,1)}, u32[]{:S(2)}) copy-start(bf16[1,256,1024]{2,1,0:T(8,128)(2,1)} %param.8) | copy-start | bytes 1572868
  0.7 7.4 %copy-start.14 = (bf16[1,256,1024]{2,1,0:T(8,128)(2,1)S(1)}, bf16[1,256,1024]{2,1,0:T(8,128)(2,1)}, u32[]{:S(2)}) copy-start(bf16[1,256,1024]{2,1,0:T(8,128)(2,1)} %param.7) | copy-start | bytes 1572868
  0.7 7.5 %slice-start = ((bf16[256,1024]{1,0:T(8,128)(2,1)}), bf16[129,1024]{1,0:T(8,128)(2,1)S(1)}, s32[]{:S(2)}) async-start(bf16[256,1024]{1,0:T(8,128)(2,1)} %param.10), calls=%async_computation.1 | async-start | bytes 557056 | tf_op jit(solution)/shard_map/slice | solution.py:87
  3.6 6.8 %copy-start.16 = (f32[1,3,3,1024]{3,0,2,1:T(1,128)S(1)}, f32[1,3,3,1024]{3,0,2,1:T(1,128)}, u32[]{:S(2)}) copy-start(f32[1,3,3,1024]{3,0,2,1:T(1,128)} %param.11) | copy-start | bytes 110596
  3.6 6.8 %copy-start.15 = (bf16[1,128,1024]{2,1,0:T(8,128)(2,1)S(1)}, bf16[1,128,1024]{2,1,0:T(8,128)(2,1)}, u32[]{:S(2)}) copy-start(bf16[1,128,1024]{2,1,0:T(8,128)(2,1)} %param.12) | copy-start | bytes 786436
  4.6 15.3 %collective-permute-start = (bf16[260,1024]{1,0:T(8,128)(2,1)}, bf16[260,1024]{1,0:T(8,128)(2,1)S(1)}, u32[]{:S(2)}, u32[]{:S(2)}) collective-permute-start(bf16[260,1024]{1,0:T(8,128)(2,1)} %pad_maximum_fusion.3), channel_id=1, source_target_pairs={{0,8},{8,16},{16,24},{24,32},{32,40},{40,48},{48,56},{56,64},{64,7... | collective-permute-start | bytes 1597448 | tf_op jit(solution)/shard_map/ppermute | solution.py:10
  9.0 15.8 %collective-permute-start.1 = (bf16[262,1024]{1,0:T(8,128)(2,1)}, bf16[262,1024]{1,0:T(8,128)(2,1)S(1)}, u32[]{:S(2)}, u32[]{:S(2)}) collective-permute-start(bf16[262,1024]{1,0:T(8,128)(2,1)} %pad_maximum_fusion.4), channel_id=1, source_target_pairs={{8,0},{16,8},{24,16},{32,24},{40,32},{48,40},{56,48},{64,56},{72,6... | collective-permute-start | bytes 1609736 | tf_op jit(solution)/shard_map/ppermute | solution.py:10
  20.0 5.2 %copy-start.12 = (bf16[256,1024]{1,0:T(8,128)(2,1)S(1)}, bf16[256,1024]{1,0:T(8,128)(2,1)}, u32[]{:S(2)}) copy-start(bf16[256,1024]{1,0:T(8,128)(2,1)} %param.9) | copy-start | bytes 1572868
  25.2 1.0 copy-start.10
  28.9 14.5 %copy-start.17 = (f32[1,1024]{1,0:T(1,128)S(1)}, f32[1,1024]{1,0:T(1,128)}, u32[]{:S(2)}) copy-start(f32[1,1024]{1,0:T(1,128)} %param.13) | copy-start | bytes 12292
  44.0 1.0 copy-start
  45.0 30.9 %collective-permute-start.2 = (bf16[256,1024]{1,0:T(8,128)(2,1)S(1)}, bf16[256,1024]{1,0:T(8,128)(2,1)S(1)}, u32[]{:S(2)}, u32[]{:S(2)}) collective-permute-start(bf16[256,1024]{1,0:T(8,128)(2,1)S(1)} %fusion.44), channel_id=1, source_target_pairs={{0,256},{256,0},{1,257},{257,1},{2,258},{258,2},{3,259},{259,3},{4... | collective-permute-start | bytes 1572872 | tf_op jit(solution)/shard_map/ppermute | solution.py:107
  75.9 8.4 %collective-permute-start.3 = (bf16[129,1024]{1,0:T(8,128)(2,1)S(1)}, bf16[129,1024]{1,0:T(8,128)(2,1)S(1)}, u32[]{:S(2)}, u32[]{:S(2)}) collective-permute-start(bf16[129,1024]{1,0:T(8,128)(2,1)S(1)} %get-tuple-element.32), channel_id=1, source_target_pairs={{8,0},{16,8},{24,16},{32,24},{40,32},{48,40},{56,48},{64,56},{72,6... | collective-permute-start | bytes 792584 | tf_op jit(solution)/shard_map/ppermute | solution.py:10
  77.2 8.6 %collective-permute-start.4 = (bf16[129,1024]{1,0:T(8,128)(2,1)S(1)}, bf16[129,1024]{1,0:T(8,128)(2,1)S(1)}, u32[]{:S(2)}, u32[]{:S(2)}) collective-permute-start(bf16[129,1024]{1,0:T(8,128)(2,1)S(1)} %get-tuple-element.31), channel_id=1, source_target_pairs={{0,8},{8,16},{16,24},{24,32},{32,40},{40,48},{48,56},{56,64},{64,7... | collective-permute-start | bytes 792584 | tf_op jit(solution)/shard_map/ppermute | solution.py:10
  84.4 3.9 %copy-start.8 = (bf16[385,1024]{1,0:T(8,128)(2,1)}, bf16[385,1024]{1,0:T(8,128)(2,1)S(1)}, u32[]{:S(2)}) copy-start(bf16[385,1024]{1,0:T(8,128)(2,1)S(1)} %constant_dynamic-update-slice_fusion) | copy-start | bytes 2365444
  88.3 0.9 copy-start.2
  88.3 1.2 copy-start.6
  109.9 68.7 %all-to-all-start = ((bf16[32,4,1024]{2,1,0:T(4,128)(2,1)}), bf16[32,4,1024]{2,1,0:T(4,128)(2,1)}, u32[]{:S(2)}, u32[]{:S(2)}) async-start(bf16[32,4,1024]{2,1,0:T(4,128)(2,1)} %rev.13), calls=%async_computation | async-start | bytes 524288 | tf_op jit(solution)/shard_map/all_to_all | solution.py:40
  157.5 15.7 %copy-start.1 = (f32[258,1024]{1,0:T(8,128)S(1)}, f32[258,1024]{1,0:T(8,128)}, u32[]{:S(2)}) copy-start(f32[258,1024]{1,0:T(8,128)} %copy-done) | copy-start | bytes 3170308
  157.5 15.7 %copy-start.3 = (bf16[385,1024]{1,0:T(8,128)(2,1)S(1)}, bf16[385,1024]{1,0:T(8,128)(2,1)}, u32[]{:S(2)}) copy-start(bf16[385,1024]{1,0:T(8,128)(2,1)} %copy-done.2) | copy-start | bytes 2365444
  157.5 15.7 %copy-start.4 = (f32[385,1024]{1,0:T(8,128)S(1)}, f32[385,1024]{1,0:T(8,128)}, u32[]{:S(2)}) copy-start(f32[385,1024]{1,0:T(8,128)} %get-tuple-element.9) | copy-start | bytes 4730884
  157.5 15.7 %copy-start.5 = (f32[385,1024]{1,0:T(8,128)S(1)}, f32[385,1024]{1,0:T(8,128)}, u32[]{:S(2)}) copy-start(f32[385,1024]{1,0:T(8,128)} %get-tuple-element.17) | copy-start | bytes 4730884
  157.5 15.7 %copy-start.7 = (bf16[385,1024]{1,0:T(8,128)(2,1)S(1)}, bf16[385,1024]{1,0:T(8,128)(2,1)}, u32[]{:S(2)}) copy-start(bf16[385,1024]{1,0:T(8,128)(2,1)} %copy-done.6) | copy-start | bytes 2365444
  157.5 15.7 %copy-start.9 = (bf16[385,1024]{1,0:T(8,128)(2,1)S(1)}, bf16[385,1024]{1,0:T(8,128)(2,1)}, u32[]{:S(2)}) copy-start(bf16[385,1024]{1,0:T(8,128)(2,1)} %copy-done.8) | copy-start | bytes 2365444
  157.5 15.7 %copy-start.11 = (bf16[256,1024]{1,0:T(8,128)(2,1)S(1)}, bf16[256,1024]{1,0:T(8,128)(2,1)}, u32[]{:S(2)}) copy-start(bf16[256,1024]{1,0:T(8,128)(2,1)} %param.10) | copy-start | bytes 1572868

commit v10 on v8

--- a/solution.py
+++ b/solution.py
@@ -83,12 +83,44 @@
     rows = q.shape[0]
     reach = extent + 1
 
-    prev_a = from_prev(jnp.concatenate([q[-2:], k[-reach:], values[-reach:]], axis=0))
-    next_a = from_next(jnp.concatenate([q[:reach], k[:2], values[:2], cotangent[:reach]], axis=0))
-    q_ext = jnp.concatenate([prev_a[:2], q, next_a[:reach]], axis=0)
-    k_ext = jnp.concatenate([prev_a[2 : 2 + reach], k, next_a[reach : reach + 2]], axis=0)
-    v_ext = jnp.concatenate([prev_a[2 + reach :], values, next_a[reach + 2 : reach + 4]], axis=0)
-    g_ext = jnp.concatenate([cotangent, next_a[reach + 4 :]], axis=0)
+    peers = lax.axis_size("ctx")
+    both = ("section", "ctx")
+    down = [(i, i + 1) for i in range(peers - 1)]
+    up = [(i + 1, i) for i in range(peers - 1)]
+    late = lambda pairs: [(peers + a, peers + b) for a, b in pairs]
+    pad = jnp.zeros((2,) + q.shape[1:], q.dtype)
+    wide = lax.ppermute(
+        jnp.where(
+            first,
+            jnp.concatenate([q[-2:], k[-reach:], values[-reach:]], axis=0),
+            jnp.concatenate([q[:reach], cotangent[:reach], k[:2]], axis=0),
+        ),
+        both,
+        down + late(up),
+    )
+    narrow = lax.ppermute(
+        jnp.where(
+            first,
+            jnp.concatenate([q[:reach], k[:2], values[:2]], axis=0),
+            jnp.concatenate([q[-2:], k[-reach:], pad], axis=0),
+        ),
+        both,
+        up + late(down),
+    )
+    q_ext = jnp.concatenate(
+        [jnp.where(first, wide[:2], narrow[:2]), q, jnp.where(first, narrow[:reach], wide[:reach])],
+        axis=0,
+    )
+    k_ext = jnp.concatenate(
+        [
+            jnp.where(first, wide[2 : 2 + reach], narrow[2 : 2 + reach]),
+            k,
+            jnp.where(first, narrow[reach : reach + 2], wide[2 * reach :]),
+        ],
+        axis=0,
+    )
+    v_ext = jnp.concatenate([wide[2 + reach :], values, narrow[reach + 2 :]], axis=0)
+    g_ext = jnp.concatenate([cotangent, wide[reach : 2 * reach]], axis=0)
 
     q_short = fwd_short(q_ext, w_q)
     k_short = fwd_short(k_ext, w_k)
@@ -105,9 +137,11 @@
     gin_last = bwd_short(gvs_last, w_v).astype(jnp.bfloat16)
 
     handed = lax.ppermute(jnp.where(first, out_first, gin_last), "section", [(0, 1), (1, 0)])
-    prev_b = from_prev(handed[-reach:])
-    next_b = from_next(handed[:reach])
-    y_ext = jnp.concatenate([prev_b, handed, next_b], axis=0)
+    rim = lax.ppermute(jnp.where(first, handed[:reach], handed[-reach:]), both, up + late(down))
+    ahead = lax.ppermute(handed[:2], both, late(up))
+    y_ext = jnp.concatenate(
+        [rim, handed, jnp.where(first, rim[:2], ahead), rim[2:]], axis=0
+    )
 
     gz_first = (y_ext[reach:].astype(jnp.float32) * q_short).astype(jnp.bfloat16)
     v_last = fwd_short(y_ext[: reach + rows + 2], w_v)

time: 182 us -> 173 us (0.951)
  starting transfers between devices: 73.9 us -> 67.5 us
    ppermute x4, starting transfers between devices: 10.6 us -> 6.76 us  [the longest x1 3.51 us: body(): lax.ppermute(jnp.where(first, jnp.concatenate([q[-2:], k[-reach:], values...]
    all_to_all x1, starting transfers between devices: 47.6 us -> 44.1 us  [exchange_scatter(): got = lax.all_to_all(pieces.astype(jnp.bfloat16), axis, 0, 0)]
    slice x7 -> x2, local copies, waits for them, and re-layouts: 2.04 us -> 0.07 us  [the longest x1 0.06 us: body(): rim[2:]]
    concatenate x2 -> x0, other arithmetic: 1.87 us -> none  [the longest x1 0.97 us: body(): jnp.concatenate([q[-2:], k[-reach:], values[-reach:]], axis=0)]
    unnamed x38 -> x37, local copies, waits for them, and re-layouts: 3.1 us -> 4.11 us
  transfers between devices with their start and end apart: 6 -> 6, of which waited for: 5 -> 4; matrix products, arithmetic and copies ran while one was open for 13% -> 13% of each run, Pallas kernels for 0% -> 0%
where the time goes in v10:
time: 173 us; the launch traced here: 172 us
  starting transfers between devices  67.5 us (39%)
  matrix products  44 us (25%)
  waiting for transfers between devices  30.8 us (18%)
  other arithmetic  15.4 us (9%)
  local copies, waits for them, and re-layouts  13.7 us (8%)
    all_to_all x1, starting transfers between devices, exchange_scatter(): got = lax.all_to_all(pieces.astype(jnp.bfloat16), axis, 0, 0)  44.1 us
    conv_general_dilated x3, matrix products, depthwise(): lax.conv_general_dilated(source[None], kernel[:, None, :], (1,), 'VALID',...  44 us
    ppermute x1, starting transfers between devices, body(): lax.ppermute(jnp.where(first, out_first, gin_last), 'section', [(0, 1), (...  16.6 us
    ppermute x1, waiting for transfers between devices, body(): lax.ppermute(jnp.where(first, out_first, gin_last), 'section', [(0, 1), (...  13.9 us
    ppermute x1, waiting for transfers between devices, body(): lax.ppermute(jnp.where(first, handed[:reach], handed[-reach:]), both, up...  8.1 us
    ppermute x1, waiting for transfers between devices, body(): lax.ppermute(jnp.where(first, jnp.concatenate([q[:reach], k[:2], values[:...  7.59 us
    broadcast_in_dim x3, other arithmetic, depthwise(): source[None]  5.11 us
    rev x1, local copies, waits for them, and re-layouts, body(): taps_part = depthwise(u[:rows + extent - 1], gz[:rows])[::-1]  4.37 us
  transfers between devices with their start and end apart: 6, of which 4 were waited for; matrix products, arithmetic and copies ran while one was open for 13% of the time, Pallas kernels for 0%

profile of v10, /device:TPU:6, one launch (start us, length us, event | category | flops | bytes accessed | tf_op | source)
XLA Modules:
  0.0 172.5 jit_solution(12797981722461344263)
XLA Ops:
  0.6 1.2 slice_bitcast_fusion
  1.8 0.8 slice_bitcast_fusion.2
  2.6 1.0 slice.272
  3.7 0.3 maximum_select_fusion
  3.9 3.5 %collective-permute-start = (bf16[260,1024]{1,0:T(8,128)(2,1)S(1)}, bf16[260,1024]{1,0:T(8,128)(2,1)S(1)}, u32[]{:S(2)}, u32[]{:S(2)}) collective-permute-start(bf16[260,1024]{1,0:T(8,128)(2,1)S(1)} %maximum_select_fusion), channel_id=1, source_target_pairs={{0,8},{8,16},{16,24},{24,32},{32,40},{40,48},{48,56},{56,64},{64,7... | collective-permute-start | bytes 1597448 | tf_op jit(solution)/shard_map/ppermute | solution.py:92
  7.5 0.1 pad.21.clone
  7.5 0.2 maximum_select_fusion.1
  7.7 1.3 collective-permute-start.1
  9.0 0.3 rev.6
  9.4 0.7 select_bitcast_fusion.2
  10.1 7.6 %collective-permute-done.1 = bf16[133,1024]{1,0:T(8,128)(2,1)S(1)} collective-permute-done((bf16[133,1024]{1,0:T(8,128)(2,1)S(1)}, bf16[133,1024]{1,0:T(8,128)(2,1)S(1)}, u32[]{:S(2)}, u32[]{:S(2)}) %collective-permute-start.1) | collective-permute-done | bytes 272416 | tf_op jit(solution)/shard_map/ppermute | solution.py:101
  17.7 1.2 collective-permute-done
  18.9 0.3 slice_select_fusion.6
  19.2 0.2 maximum_convert_fusion.2
  19.4 0.8 copy-done.13
  20.2 0.2 maximum_convert_fusion.1
  20.4 0.1 copy-done.14
  20.5 0.2 maximum_convert_fusion
  20.7 0.7 copy-done.10
  21.5 2.7 %select_bitcast_fusion.1 = (bf16[1,385,1024]{2,1,0:T(8,128)(2,1)S(1)}, bf16[385,1024]{1,0:T(8,128)(2,1)S(1)}, f32[385,1024]{1,0:T(8,128)S(1)}, bf16[385,1024]{1,...) fusion(pred[]{:T(512)S(6)} %eq.3, bf16[129,1024]{1,0:T(8,128)(2,1)S(1)} %get-tuple-element.27, ...), kind=kLoop, calls=%fused_computation.75 | loop fusion | flops 9461760 | bytes 22114304 | tf_op jit(solution)/shard_map/broadcast_in_dim | solution.py:46
  24.2 14.5 %fusion.10 = f32[1,258,1024]{2,0,1:T(1,128)S(1)} fusion(bf16[1,385,1024]{2,1,0:T(8,128)(2,1)S(1)} %get-tuple-element.13, bf16[128,1,1024]{2,0,1:T(8,128)(2,1)S(1)} %get-tuple-element.30), kind=kOutput, calls=%fused_computation.26 | convolution fusion | flops 67633152 | bytes 2107392 | tf_op jit(solution)/shard_map/conv_general_dilated | solution.py:45
  38.7 0.5 fusion.36
  39.2 0.4 fusion.40
  39.6 0.6 copy-done
  40.2 16.6 %collective-permute-start.2 = (bf16[256,1024]{1,0:T(8,128)(2,1)S(1)}, bf16[256,1024]{1,0:T(8,128)(2,1)S(1)}, u32[]{:S(2)}, u32[]{:S(2)}) collective-permute-start(bf16[256,1024]{1,0:T(8,128)(2,1)S(1)} %fusion.40), channel_id=1, source_target_pairs={{0,256},{256,0},{1,257},{257,1},{2,258},{258,2},{3,259},{259,3},{4... | collective-permute-start | bytes 1572872 | tf_op jit(solution)/shard_map/ppermute | solution.py:139
  56.8 13.9 %collective-permute-done.2 = bf16[256,1024]{1,0:T(8,128)(2,1)S(1)} collective-permute-done((bf16[256,1024]{1,0:T(8,128)(2,1)S(1)}, bf16[256,1024]{1,0:T(8,128)(2,1)S(1)}, u32[]{:S(2)}, u32[]{:S(2)}) %collective-permute-start.2) | collective-permute-done | bytes 524320 | tf_op jit(solution)/shard_map/ppermute | solution.py:139
  70.8 0.1 slice_select_fusion.5
  70.8 1.3 collective-permute-start.3
  72.2 0.7 collective-permute-start.4
  72.8 8.1 %collective-permute-done.3 = bf16[129,1024]{1,0:T(8,128)(2,1)S(1)} collective-permute-done((bf16[129,1024]{1,0:T(8,128)(2,1)S(1)}, bf16[129,1024]{1,0:T(8,128)(2,1)S(1)}, u32[]{:S(2)}, u32[]{:S(2)}) %collective-permute-start.3) | collective-permute-done | bytes 264224 | tf_op jit(solution)/shard_map/ppermute | solution.py:140
  80.9 0.1 slice.371
  81.0 0.2 maximum_convert_fusion.3
  81.2 2.3 %select_bitcast_fusion = (bf16[1,385,1024]{2,1,0:T(8,128)(2,1)}, bf16[385,1024]{1,0:T(8,128)(2,1)S(1)}, f32[385,1024]{1,0:T(8,128)}, bf16[385,1024]{1,0:T(8,128)(2,1)S(1)}) fusion(pred[]{:T(512)S(6)} %eq.3, f32[385,1024]{1,0:T(8,128)S(1)} %get-tuple-element.18, f32[387,1024]{1,0:T(8,128)S(1)} %maximum_convert_fusion.3, f32[1024]{0:T(1024)S(1)} %bitcast.71, ...), kind=kLoop, calls=%fused_computation.74 | loop fusion | flops 6307840 | bytes 12627969 | tf_op jit(solution)/shard_map/broadcast_in_dim | solution.py:46
  83.6 0.1 fusion.31
  83.7 0.7 copy-done.4
  84.5 0.3 copy-done.8
  84.7 13.9 %fusion.12 = bf16[1,128,1024]{2,0,1:T(2,128)(2,1)S(1)} fusion(bf16[1,383,1024]{2,1,0:T(8,128)(2,1)S(1)} %fusion.31, bf16[256,1,1024]{2,0,1:T(8,128)(2,1)S(1)} %fusion.45), kind=kOutput, calls=%fused_computation.28 | convolution fusion | flops 67108864 | bytes 1570816 | tf_op jit(solution)/shard_map/conv_general_dilated | solution.py:45
  98.7 0.8 copy.46
  99.5 4.4 %rev.7 = bf16[128,1024]{1,0:T(8,128)(2,1)} reverse(bf16[128,1024]{1,0:T(8,128)(2,1)} %bitcast.63), dimensions={0} | reverse | bytes 524288 | tf_op jit(solution)/shard_map/rev | solution.py:168
  103.8 1.7 %convert_element_type.118 = bf16[32,4,1024]{2,1,0:T(4,128)(2,1)} reshape(bf16[128,1024]{1,0:T(8,128)(2,1)} %rev.7) | data formatting | bytes 524288 | tf_op jit(solution)/shard_map/convert_element_type | solution.py:40
  105.6 44.1 %all-to-all-start = ((bf16[32,4,1024]{2,1,0:T(4,128)(2,1)}), bf16[32,4,1024]{2,1,0:T(4,128)(2,1)}, u32[]{:S(2)}, u32[]{:S(2)}) async-start(bf16[32,4,1024]{2,1,0:T(4,128)(2,1)} %convert_element_type.118), calls=%async_computation | async-start | bytes 524288 | tf_op jit(solution)/shard_map/all_to_all | solution.py:40
  149.8 15.6 %fusion.8 = f32[1,258,1024]{2,0,1:T(1,128)S(1)} fusion(bf16[1,385,1024]{2,1,0:T(8,128)(2,1)} %get-tuple-element.7, bf16[128,1,1024]{2,0,1:T(8,128)(2,1)} %get-tuple-element.29), kind=kOutput, calls=%fused_computation.24 | convolution fusion | flops 67633152 | bytes 2107392 | tf_op jit(solution)/shard_map/conv_general_dilated | solution.py:45
  165.4 1.0 fusion.38
  166.5 1.1 fusion.42
  167.6 1.1 fusion.43
  168.7 1.1 fusion.44
  169.8 0.9 fusion.41
  170.8 1.7 convert_reduce_fusion
  (42 shorter events, 0.2 us)
Async XLA Ops:
  0.6 3.0 %slice-start = ((bf16[256,1024]{1,0:T(8,128)(2,1)}), bf16[129,1024]{1,0:T(8,128)(2,1)S(1)}, s32[]{:S(2)}) async-start(bf16[256,1024]{1,0:T(8,128)(2,1)} %param.10), calls=%async_computation.1 | async-start | bytes 557056 | tf_op jit(solution)/shard_map/slice | solution.py:96
  1.8 5.7 %slice-start.1 = ((bf16[256,1024]{1,0:T(8,128)(2,1)}), bf16[2,1024]{1,0:T(2,128)(2,1)S(1)}, s32[]{:S(2)}) async-start(bf16[256,1024]{1,0:T(8,128)(2,1)} %param.9), calls=%async_computation.2 | async-start | bytes 8192 | tf_op jit(solution)/shard_map/slice | solution.py:104
  3.6 5.4 %copy-start.16 = (f32[1,3,3,1024]{3,0,2,1:T(1,128)S(1)}, f32[1,3,3,1024]{3,0,2,1:T(1,128)}, u32[]{:S(2)}) copy-start(f32[1,3,3,1024]{3,0,2,1:T(1,128)} %param.11) | copy-start | bytes 110596
  3.6 5.4 %copy-start.15 = (bf16[1,128,1024]{2,1,0:T(8,128)(2,1)S(1)}, bf16[1,128,1024]{2,1,0:T(8,128)(2,1)}, u32[]{:S(2)}) copy-start(bf16[1,128,1024]{2,1,0:T(8,128)(2,1)} %param.12) | copy-start | bytes 786436
  3.9 15.0 %collective-permute-start = (bf16[260,1024]{1,0:T(8,128)(2,1)S(1)}, bf16[260,1024]{1,0:T(8,128)(2,1)S(1)}, u32[]{:S(2)}, u32[]{:S(2)}) collective-permute-start(bf16[260,1024]{1,0:T(8,128)(2,1)S(1)} %maximum_select_fusion), channel_id=1, source_target_pairs={{0,8},{8,16},{16,24},{24,32},{32,40},{40,48},{48,56},{56,64},{64,7... | collective-permute-start | bytes 1597448 | tf_op jit(solution)/shard_map/ppermute | solution.py:92
  7.7 10.0 %collective-permute-start.1 = (bf16[133,1024]{1,0:T(8,128)(2,1)S(1)}, bf16[133,1024]{1,0:T(8,128)(2,1)S(1)}, u32[]{:S(2)}, u32[]{:S(2)}) collective-permute-start(bf16[133,1024]{1,0:T(8,128)(2,1)S(1)} %maximum_select_fusion.1), channel_id=1, source_target_pairs={{8,0},{16,8},{24,16},{32,24},{40,32},{48,40},{56,48},{64,56},{72,6... | collective-permute-start | bytes 817160 | tf_op jit(solution)/shard_map/ppermute | solution.py:101
  10.1 9.1 %copy-start.12 = (bf16[256,1024]{1,0:T(8,128)(2,1)S(1)}, bf16[256,1024]{1,0:T(8,128)(2,1)}, u32[]{:S(2)}) copy-start(bf16[256,1024]{1,0:T(8,128)(2,1)} %param.9) | copy-start | bytes 1572868
  19.2 1.0 copy-start.13
  19.4 1.1 copy-start.14
  20.4 1.1 copy-start.10
  24.2 14.5 %copy-start.17 = (f32[1,1024]{1,0:T(1,128)S(1)}, f32[1,1024]{1,0:T(1,128)}, u32[]{:S(2)}) copy-start(f32[1,1024]{1,0:T(1,128)} %param.13) | copy-start | bytes 12292
  39.2 1.0 copy-start
  40.2 30.5 %collective-permute-start.2 = (bf16[256,1024]{1,0:T(8,128)(2,1)S(1)}, bf16[256,1024]{1,0:T(8,128)(2,1)S(1)}, u32[]{:S(2)}, u32[]{:S(2)}) collective-permute-start(bf16[256,1024]{1,0:T(8,128)(2,1)S(1)} %fusion.40), channel_id=1, source_target_pairs={{0,256},{256,0},{1,257},{257,1},{2,258},{258,2},{3,259},{259,3},{4... | collective-permute-start | bytes 1572872 | tf_op jit(solution)/shard_map/ppermute | solution.py:139
  70.8 10.5 %copy-start.2 = (bf16[256,1024]{1,0:T(8,128)(2,1)}, bf16[256,1024]{1,0:T(8,128)(2,1)S(1)}, u32[]{:S(2)}) copy-start(bf16[256,1024]{1,0:T(8,128)(2,1)S(1)} %collective-permute-done.2) | copy-start | bytes 1572868
  70.8 10.1 %collective-permute-start.3 = (bf16[129,1024]{1,0:T(8,128)(2,1)S(1)}, bf16[129,1024]{1,0:T(8,128)(2,1)S(1)}, u32[]{:S(2)}, u32[]{:S(2)}) collective-permute-start(bf16[129,1024]{1,0:T(8,128)(2,1)S(1)} %slice_select_fusion.5), channel_id=1, source_target_pairs={{8,0},{16,8},{24,16},{32,24},{40,32},{48,40},{56,48},{64,56},{72,6... | collective-permute-start | bytes 792584 | tf_op jit(solution)/shard_map/ppermute | solution.py:140
  72.2 8.8 %collective-permute-start.4 = (bf16[2,1024]{1,0:T(2,128)(2,1)S(1)}, bf16[2,1024]{1,0:T(2,128)(2,1)S(1)}, u32[]{:S(2)}, u32[]{:S(2)}) collective-permute-start(bf16[2,1024]{1,0:T(2,128)(2,1)S(1)} %slice.370), channel_id=1, source_target_pairs={{264,256},{272,264},{280,272},{288,280},{296,288},{304,296},{312,3... | collective-permute-start | bytes 12296 | tf_op jit(solution)/shard_map/ppermute | solution.py:141
  83.6 0.9 copy-start.4
  83.6 1.2 copy-start.8
  105.6 65.2 %all-to-all-start = ((bf16[32,4,1024]{2,1,0:T(4,128)(2,1)}), bf16[32,4,1024]{2,1,0:T(4,128)(2,1)}, u32[]{:S(2)}, u32[]{:S(2)}) async-start(bf16[32,4,1024]{2,1,0:T(4,128)(2,1)} %convert_element_type.118), calls=%async_computation | async-start | bytes 524288 | tf_op jit(solution)/shard_map/all_to_all | solution.py:40
  149.7 15.7 %copy-start.1 = (f32[258,1024]{1,0:T(8,128)S(1)}, f32[258,1024]{1,0:T(8,128)}, u32[]{:S(2)}) copy-start(f32[258,1024]{1,0:T(8,128)} %copy-done) | copy-start | bytes 3170308
  149.7 15.7 %copy-start.3 = (bf16[256,1024]{1,0:T(8,128)(2,1)S(1)}, bf16[256,1024]{1,0:T(8,128)(2,1)}, u32[]{:S(2)}) copy-start(bf16[256,1024]{1,0:T(8,128)(2,1)} %copy-done.2) | copy-start | bytes 1572868
  149.7 15.7 %copy-start.5 = (bf16[385,1024]{1,0:T(8,128)(2,1)S(1)}, bf16[385,1024]{1,0:T(8,128)(2,1)}, u32[]{:S(2)}) copy-start(bf16[385,1024]{1,0:T(8,128)(2,1)} %copy-done.4) | copy-start | bytes 2365444
  149.7 15.7 %copy-start.6 = (f32[385,1024]{1,0:T(8,128)S(1)}, f32[385,1024]{1,0:T(8,128)}, u32[]{:S(2)}) copy-start(f32[385,1024]{1,0:T(8,128)} %get-tuple-element.9) | copy-start | bytes 4730884
  149.7 15.7 %copy-start.7 = (f32[385,1024]{1,0:T(8,128)S(1)}, f32[385,1024]{1,0:T(8,128)}, u32[]{:S(2)}) copy-start(f32[385,1024]{1,0:T(8,128)} %get-tuple-element.17) | copy-start | bytes 4730884
  149.8 15.7 %copy-start.9 = (bf16[385,1024]{1,0:T(8,128)(2,1)S(1)}, bf16[385,1024]{1,0:T(8,128)(2,1)}, u32[]{:S(2)}) copy-start(bf16[385,1024]{1,0:T(8,128)(2,1)} %copy-done.8) | copy-start | bytes 2365444
  149.8 15.7 %copy-start.11 = (bf16[256,1024]{1,0:T(8,128)(2,1)S(1)}, bf16[256,1024]{1,0:T(8,128)(2,1)}, u32[]{:S(2)}) copy-start(bf16[256,1024]{1,0:T(8,128)(2,1)} %param.10) | copy-start | bytes 1572868

commit v11 on v10

--- a/solution.py
+++ b/solution.py
@@ -14,7 +14,7 @@
     peers = lax.axis_size(axis)
     steps = peers.bit_length() - 1
     if peers != 1 << steps or part.shape[0] % peers:
-        return lax.psum_scatter(part, axis, scatter_dimension=0, tiled=True)
+        return lax.psum_scatter(part[::-1], axis, scatter_dimension=0, tiled=True)
     me = lax.axis_index(axis)
     rows = part.shape[0] // peers
     held = part.reshape((2,) * steps + (rows,) + part.shape[1:])
@@ -34,11 +34,11 @@
 def exchange_scatter(part, axis):
     peers = lax.axis_size(axis)
     if part.shape[0] % peers:
-        return lax.psum_scatter(part, axis, scatter_dimension=0, tiled=True)
+        return lax.psum_scatter(part[::-1], axis, scatter_dimension=0, tiled=True)
     rows = part.shape[0] // peers
-    pieces = part.reshape((peers, rows) + part.shape[1:])
+    pieces = part.reshape((peers, rows) + part.shape[1:])[::-1]
     got = lax.all_to_all(pieces.astype(jnp.bfloat16), axis, 0, 0)
-    return jnp.sum(got.astype(jnp.float32), axis=0)
+    return jnp.sum(got.astype(jnp.float32), axis=0)[::-1]
 
 
 def depthwise(source, kernel):
@@ -165,7 +165,7 @@
     grad_q = bwd_short(gqs, w_q).astype(jnp.bfloat16)
     grad_k = bwd_short(gks, w_k).astype(jnp.bfloat16)
     grad_input = bwd_short(gvs, w_v).astype(jnp.bfloat16)
-    taps_part = depthwise(u[: rows + extent - 1], gz[:rows])[::-1]
+    taps_part = depthwise(u[: rows + extent - 1], gz[:rows])
     tap_sum = exchange_scatter(taps_part, "ctx")
     return (output[None], grad_q[None], grad_k[None], grad_input[None], tap_sum[None])
 

time: 173 us -> 174 us (level)
  matrix products: 44 us -> 46.9 us
    conv_general_dilated x3, matrix products: 44 us -> 46.9 us  [depthwise(): lax.conv_general_dilated(source[None], kernel[:, None, :], (1,), 'VALID',...]
    another operation x0 -> x1, local copies, waits for them, and re-layouts: none -> 1.76 us  [exchange_scatter(): pieces = part.reshape((peers, rows) + part.shape[1:])[::-1]]
    convert_element_type x1 -> x0, local copies, waits for them, and re-layouts: 1.74 us -> none  [exchange_scatter(): got = lax.all_to_all(pieces.astype(jnp.bfloat16), axis, 0, 0)]
    unnamed x37 -> x36, local copies, waits for them, and re-layouts: 4.11 us -> 3.33 us
    rev x1 -> x2, local copies, waits for them, and re-layouts: 4.37 us -> 4.16 us  [the longest x1 2.43 us: exchange_scatter(): return jnp.sum(got.astype(jnp.float32), axis=0)[::-1]]
where the time goes in v11:
time: 174 us
  starting transfers between devices  67.5 us (39%)
  matrix products  46.9 us (27%)
  waiting for transfers between devices  30.8 us (18%)
  other arithmetic  14.8 us (9%)
  local copies, waits for them, and re-layouts  12.7 us (7%)
    conv_general_dilated x3, matrix products, depthwise(): lax.conv_general_dilated(source[None], kernel[:, None, :], (1,), 'VALID',...  46.9 us
    all_to_all x1, starting transfers between devices, exchange_scatter(): got = lax.all_to_all(pieces.astype(jnp.bfloat16), axis, 0, 0)  44.1 us
    ppermute x1, starting transfers between devices, body(): lax.ppermute(jnp.where(first, out_first, gin_last), 'section', [(0, 1), (...  16.6 us
    ppermute x1, waiting for transfers between devices, body(): lax.ppermute(jnp.where(first, out_first, gin_last), 'section', [(0, 1), (...  13.9 us
    ppermute x1, waiting for transfers between devices, body(): lax.ppermute(jnp.where(first, handed[:reach], handed[-reach:]), both, up...  8.1 us
    ppermute x1, waiting for transfers between devices, body(): lax.ppermute(jnp.where(first, jnp.concatenate([q[:reach], k[:2], values[:...  7.59 us
    broadcast_in_dim x3, other arithmetic, depthwise(): source[None]  5.13 us
    ppermute x1, starting transfers between devices, body(): lax.ppermute(jnp.where(first, jnp.concatenate([q[-2:], k[-reach:], values...  3.51 us
  transfers between devices with their start and end apart: 6, of which 4 were waited for; matrix products, arithmetic and copies ran while one was open for 13% of the time, Pallas kernels for 0%

profile of v11, /device:TPU:6, one launch (start us, length us, event | category | flops | bytes accessed | tf_op | source)
XLA Modules:
  0.0 173.9 jit_solution(9085575502607232216)
XLA Ops:
  0.6 1.2 slice_bitcast_fusion
  1.8 0.8 slice_bitcast_fusion.2
  2.6 1.0 slice.272
  3.7 0.3 maximum_select_fusion
  3.9 3.5 %collective-permute-start = (bf16[260,1024]{1,0:T(8,128)(2,1)S(1)}, bf16[260,1024]{1,0:T(8,128)(2,1)S(1)}, u32[]{:S(2)}, u32[]{:S(2)}) collective-permute-start(bf16[260,1024]{1,0:T(8,128)(2,1)S(1)} %maximum_select_fusion), channel_id=1, source_target_pairs={{0,8},{8,16},{16,24},{24,32},{32,40},{40,48},{48,56},{56,64},{64,7... | collective-permute-start | bytes 1597448 | tf_op jit(solution)/shard_map/ppermute | solution.py:92
  7.5 0.1 pad.21.clone
  7.5 0.2 maximum_select_fusion.1
  7.7 1.3 collective-permute-start.1
  9.0 0.3 rev.9
  9.4 0.7 select_bitcast_fusion.2
  10.1 7.6 %collective-permute-done.1 = bf16[133,1024]{1,0:T(8,128)(2,1)S(1)} collective-permute-done((bf16[133,1024]{1,0:T(8,128)(2,1)S(1)}, bf16[133,1024]{1,0:T(8,128)(2,1)S(1)}, u32[]{:S(2)}, u32[]{:S(2)}) %collective-permute-start.1) | collective-permute-done | bytes 272416 | tf_op jit(solution)/shard_map/ppermute | solution.py:101
  17.7 1.2 collective-permute-done
  18.9 0.3 slice_select_fusion.6
  19.2 0.2 maximum_convert_fusion.2
  19.4 0.8 copy-done.13
  20.2 0.2 maximum_convert_fusion.1
  20.4 0.1 copy-done.14
  20.5 0.2 maximum_convert_fusion
  20.7 0.7 copy-done.10
  21.5 2.7 %select_bitcast_fusion.1 = (bf16[1,385,1024]{2,1,0:T(8,128)(2,1)S(1)}, bf16[385,1024]{1,0:T(8,128)(2,1)S(1)}, f32[385,1024]{1,0:T(8,128)S(1)}, bf16[385,1024]{1,...) fusion(pred[]{:T(512)S(6)} %eq.3, bf16[129,1024]{1,0:T(8,128)(2,1)S(1)} %get-tuple-element.27, ...), kind=kLoop, calls=%fused_computation.76 | loop fusion | flops 9461760 | bytes 22114304 | tf_op jit(solution)/shard_map/broadcast_in_dim | solution.py:46
  24.2 14.5 %fusion.10 = f32[1,258,1024]{2,0,1:T(1,128)S(1)} fusion(bf16[1,385,1024]{2,1,0:T(8,128)(2,1)S(1)} %get-tuple-element.13, bf16[128,1,1024]{2,0,1:T(8,128)(2,1)S(1)} %get-tuple-element.30), kind=kOutput, calls=%fused_computation.26 | convolution fusion | flops 67633152 | bytes 2107392 | tf_op jit(solution)/shard_map/conv_general_dilated | solution.py:45
  38.7 0.5 fusion.39
  39.2 0.4 fusion.43
  39.6 0.6 copy-done
  40.2 16.6 %collective-permute-start.2 = (bf16[256,1024]{1,0:T(8,128)(2,1)S(1)}, bf16[256,1024]{1,0:T(8,128)(2,1)S(1)}, u32[]{:S(2)}, u32[]{:S(2)}) collective-permute-start(bf16[256,1024]{1,0:T(8,128)(2,1)S(1)} %fusion.43), channel_id=1, source_target_pairs={{0,256},{256,0},{1,257},{257,1},{2,258},{258,2},{3,259},{259,3},{4... | collective-permute-start | bytes 1572872 | tf_op jit(solution)/shard_map/ppermute | solution.py:139
  56.8 13.9 %collective-permute-done.2 = bf16[256,1024]{1,0:T(8,128)(2,1)S(1)} collective-permute-done((bf16[256,1024]{1,0:T(8,128)(2,1)S(1)}, bf16[256,1024]{1,0:T(8,128)(2,1)S(1)}, u32[]{:S(2)}, u32[]{:S(2)}) %collective-permute-start.2) | collective-permute-done | bytes 524320 | tf_op jit(solution)/shard_map/ppermute | solution.py:139
  70.8 0.1 slice_select_fusion.5
  70.8 1.3 collective-permute-start.3
  72.2 0.7 collective-permute-start.4
  72.8 8.1 %collective-permute-done.3 = bf16[129,1024]{1,0:T(8,128)(2,1)S(1)} collective-permute-done((bf16[129,1024]{1,0:T(8,128)(2,1)S(1)}, bf16[129,1024]{1,0:T(8,128)(2,1)S(1)}, u32[]{:S(2)}, u32[]{:S(2)}) %collective-permute-start.3) | collective-permute-done | bytes 264224 | tf_op jit(solution)/shard_map/ppermute | solution.py:140
  80.9 0.1 slice.371
  81.0 0.2 maximum_convert_fusion.3
  81.2 2.3 %select_bitcast_fusion = (bf16[1,385,1024]{2,1,0:T(8,128)(2,1)}, bf16[385,1024]{1,0:T(8,128)(2,1)S(1)}, f32[385,1024]{1,0:T(8,128)}, bf16[385,1024]{1,0:T(8,128)(2,1)S(1)}) fusion(pred[]{:T(512)S(6)} %eq.3, f32[385,1024]{1,0:T(8,128)S(1)} %get-tuple-element.18, f32[387,1024]{1,0:T(8,128)S(1)} %maximum_convert_fusion.3, f32[1024]{0:T(1024)S(1)} %bitcast.67, ...), kind=kLoop, calls=%fused_computation.75 | loop fusion | flops 6307840 | bytes 12627969 | tf_op jit(solution)/shard_map/broadcast_in_dim | solution.py:46
  83.6 0.1 fusion.34
  83.7 0.8 copy-done.4
  84.5 0.3 copy-done.8
  84.8 16.9 %fusion.14 = bf16[128,1024]{1,0:T(8,128)(2,1)} fusion(bf16[1,383,1024]{2,1,0:T(8,128)(2,1)S(1)} %fusion.34, bf16[256,1,1024]{2,0,1:T(8,128)(2,1)S(1)} %fusion.48), kind=kOutput, calls=%fused_computation.30 | convolution fusion | flops 67108864 | bytes 1570816 | tf_op jit(solution)/shard_map/conv_general_dilated | solution.py:45
  101.7 1.8 %reshape_squeeze.3 = bf16[32,4,1024]{2,1,0:T(4,128)(2,1)} reshape(bf16[128,1024]{1,0:T(8,128)(2,1)} %fusion.14) | data formatting | bytes 524288 | tf_op jit(solution)/shard_map/reshape;squeeze | solution.py:39
  103.4 1.7 rev.13
  105.1 44.1 %all-to-all-start = ((bf16[32,4,1024]{2,1,0:T(4,128)(2,1)}), bf16[32,4,1024]{2,1,0:T(4,128)(2,1)}, u32[]{:S(2)}, u32[]{:S(2)}) async-start(bf16[32,4,1024]{2,1,0:T(4,128)(2,1)} %rev.13), calls=%async_computation | async-start | bytes 524288 | tf_op jit(solution)/shard_map/all_to_all | solution.py:40
  149.3 15.6 %fusion.8 = f32[1,258,1024]{2,0,1:T(1,128)S(1)} fusion(bf16[1,385,1024]{2,1,0:T(8,128)(2,1)} %get-tuple-element.7, bf16[128,1,1024]{2,0,1:T(8,128)(2,1)} %get-tuple-element.29), kind=kOutput, calls=%fused_computation.24 | convolution fusion | flops 67633152 | bytes 2107392 | tf_op jit(solution)/shard_map/conv_general_dilated | solution.py:45
  165.0 1.0 fusion.41
  166.1 1.1 fusion.45
  167.2 1.1 fusion.46
  168.3 1.1 fusion.47
  169.4 0.9 fusion.44
  170.4 1.1 convert_reduce_fusion
  171.4 2.4 %rev.11 = f32[4,1024]{1,0:T(4,128)} reverse(f32[4,1024]{1,0:T(4,128)S(1)} %convert_reduce_fusion), dimensions={0} | reverse | bytes 32768 | tf_op jit(solution)/shard_map/rev | solution.py:41
  (42 shorter events, 0.2 us)
Async XLA Ops:
  0.6 3.0 %slice-start = ((bf16[256,1024]{1,0:T(8,128)(2,1)}), bf16[129,1024]{1,0:T(8,128)(2,1)S(1)}, s32[]{:S(2)}) async-start(bf16[256,1024]{1,0:T(8,128)(2,1)} %param.10), calls=%async_computation.1 | async-start | bytes 557056 | tf_op jit(solution)/shard_map/slice | solution.py:96
  1.8 5.7 %slice-start.1 = ((bf16[256,1024]{1,0:T(8,128)(2,1)}), bf16[2,1024]{1,0:T(2,128)(2,1)S(1)}, s32[]{:S(2)}) async-start(bf16[256,1024]{1,0:T(8,128)(2,1)} %param.9), calls=%async_computation.2 | async-start | bytes 8192 | tf_op jit(solution)/shard_map/slice | solution.py:104
  3.6 5.4 %copy-start.16 = (f32[1,3,3,1024]{3,0,2,1:T(1,128)S(1)}, f32[1,3,3,1024]{3,0,2,1:T(1,128)}, u32[]{:S(2)}) copy-start(f32[1,3,3,1024]{3,0,2,1:T(1,128)} %param.11) | copy-start | bytes 110596
  3.6 5.4 %copy-start.15 = (bf16[1,128,1024]{2,1,0:T(8,128)(2,1)S(1)}, bf16[1,128,1024]{2,1,0:T(8,128)(2,1)}, u32[]{:S(2)}) copy-start(bf16[1,128,1024]{2,1,0:T(8,128)(2,1)} %param.12) | copy-start | bytes 786436
  3.9 15.0 %collective-permute-start = (bf16[260,1024]{1,0:T(8,128)(2,1)S(1)}, bf16[260,1024]{1,0:T(8,128)(2,1)S(1)}, u32[]{:S(2)}, u32[]{:S(2)}) collective-permute-start(bf16[260,1024]{1,0:T(8,128)(2,1)S(1)} %maximum_select_fusion), channel_id=1, source_target_pairs={{0,8},{8,16},{16,24},{24,32},{32,40},{40,48},{48,56},{56,64},{64,7... | collective-permute-start | bytes 1597448 | tf_op jit(solution)/shard_map/ppermute | solution.py:92
  7.7 10.0 %collective-permute-start.1 = (bf16[133,1024]{1,0:T(8,128)(2,1)S(1)}, bf16[133,1024]{1,0:T(8,128)(2,1)S(1)}, u32[]{:S(2)}, u32[]{:S(2)}) collective-permute-start(bf16[133,1024]{1,0:T(8,128)(2,1)S(1)} %maximum_select_fusion.1), channel_id=1, source_target_pairs={{8,0},{16,8},{24,16},{32,24},{40,32},{48,40},{56,48},{64,56},{72,6... | collective-permute-start | bytes 817160 | tf_op jit(solution)/shard_map/ppermute | solution.py:101
  10.1 9.1 %copy-start.12 = (bf16[256,1024]{1,0:T(8,128)(2,1)S(1)}, bf16[256,1024]{1,0:T(8,128)(2,1)}, u32[]{:S(2)}) copy-start(bf16[256,1024]{1,0:T(8,128)(2,1)} %param.9) | copy-start | bytes 1572868
  19.2 1.0 copy-start.13
  19.4 1.1 copy-start.14
  20.4 1.1 copy-start.10
  24.2 14.5 %copy-start.17 = (f32[1,1024]{1,0:T(1,128)S(1)}, f32[1,1024]{1,0:T(1,128)}, u32[]{:S(2)}) copy-start(f32[1,1024]{1,0:T(1,128)} %param.13) | copy-start | bytes 12292
  39.2 1.0 copy-start
  40.2 30.5 %collective-permute-start.2 = (bf16[256,1024]{1,0:T(8,128)(2,1)S(1)}, bf16[256,1024]{1,0:T(8,128)(2,1)S(1)}, u32[]{:S(2)}, u32[]{:S(2)}) collective-permute-start(bf16[256,1024]{1,0:T(8,128)(2,1)S(1)} %fusion.43), channel_id=1, source_target_pairs={{0,256},{256,0},{1,257},{257,1},{2,258},{258,2},{3,259},{259,3},{4... | collective-permute-start | bytes 1572872 | tf_op jit(solution)/shard_map/ppermute | solution.py:139
  70.8 10.5 %copy-start.2 = (bf16[256,1024]{1,0:T(8,128)(2,1)}, bf16[256,1024]{1,0:T(8,128)(2,1)S(1)}, u32[]{:S(2)}) copy-start(bf16[256,1024]{1,0:T(8,128)(2,1)S(1)} %collective-permute-done.2) | copy-start | bytes 1572868
  70.8 10.1 %collective-permute-start.3 = (bf16[129,1024]{1,0:T(8,128)(2,1)S(1)}, bf16[129,1024]{1,0:T(8,128)(2,1)S(1)}, u32[]{:S(2)}, u32[]{:S(2)}) collective-permute-start(bf16[129,1024]{1,0:T(8,128)(2,1)S(1)} %slice_select_fusion.5), channel_id=1, source_target_pairs={{8,0},{16,8},{24,16},{32,24},{40,32},{48,40},{56,48},{64,56},{72,6... | collective-permute-start | bytes 792584 | tf_op jit(solution)/shard_map/ppermute | solution.py:140
  72.2 8.8 %collective-permute-start.4 = (bf16[2,1024]{1,0:T(2,128)(2,1)S(1)}, bf16[2,1024]{1,0:T(2,128)(2,1)S(1)}, u32[]{:S(2)}, u32[]{:S(2)}) collective-permute-start(bf16[2,1024]{1,0:T(2,128)(2,1)S(1)} %slice.370), channel_id=1, source_target_pairs={{264,256},{272,264},{280,272},{288,280},{296,288},{304,296},{312,3... | collective-permute-start | bytes 12296 | tf_op jit(solution)/shard_map/ppermute | solution.py:141
  83.6 0.9 copy-start.4
  83.6 1.2 copy-start.8
  105.1 65.2 %all-to-all-start = ((bf16[32,4,1024]{2,1,0:T(4,128)(2,1)}), bf16[32,4,1024]{2,1,0:T(4,128)(2,1)}, u32[]{:S(2)}, u32[]{:S(2)}) async-start(bf16[32,4,1024]{2,1,0:T(4,128)(2,1)} %rev.13), calls=%async_computation | async-start | bytes 524288 | tf_op jit(solution)/shard_map/all_to_all | solution.py:40
  149.3 15.7 %copy-start.1 = (f32[258,1024]{1,0:T(8,128)S(1)}, f32[258,1024]{1,0:T(8,128)}, u32[]{:S(2)}) copy-start(f32[258,1024]{1,0:T(8,128)} %copy-done) | copy-start | bytes 3170308
  149.3 15.7 %copy-start.3 = (bf16[256,1024]{1,0:T(8,128)(2,1)S(1)}, bf16[256,1024]{1,0:T(8,128)(2,1)}, u32[]{:S(2)}) copy-start(bf16[256,1024]{1,0:T(8,128)(2,1)} %copy-done.2) | copy-start | bytes 1572868
  149.3 15.7 %copy-start.5 = (bf16[385,1024]{1,0:T(8,128)(2,1)S(1)}, bf16[385,1024]{1,0:T(8,128)(2,1)}, u32[]{:S(2)}) copy-start(bf16[385,1024]{1,0:T(8,128)(2,1)} %copy-done.4) | copy-start | bytes 2365444
  149.3 15.7 %copy-start.6 = (f32[385,1024]{1,0:T(8,128)S(1)}, f32[385,1024]{1,0:T(8,128)}, u32[]{:S(2)}) copy-start(f32[385,1024]{1,0:T(8,128)} %get-tuple-element.9) | copy-start | bytes 4730884
  149.3 15.7 %copy-start.7 = (f32[385,1024]{1,0:T(8,128)S(1)}, f32[385,1024]{1,0:T(8,128)}, u32[]{:S(2)}) copy-start(f32[385,1024]{1,0:T(8,128)} %get-tuple-element.17) | copy-start | bytes 4730884
  149.3 15.7 %copy-start.9 = (bf16[385,1024]{1,0:T(8,128)(2,1)S(1)}, bf16[385,1024]{1,0:T(8,128)(2,1)}, u32[]{:S(2)}) copy-start(bf16[385,1024]{1,0:T(8,128)(2,1)} %copy-done.8) | copy-start | bytes 2365444
  149.3 15.7 %copy-start.11 = (bf16[256,1024]{1,0:T(8,128)(2,1)S(1)}, bf16[256,1024]{1,0:T(8,128)(2,1)}, u32[]{:S(2)}) copy-start(bf16[256,1024]{1,0:T(8,128)(2,1)} %param.10) | copy-start | bytes 1572868
